TPU v7x, 256 devices: a whole 4x4x8 slice. The times are simulated.
256 devices in a mesh: seq: 32 (over y, z), grp: 8 (over x, core).
Axes of the slice: x: 4, y: 4, z: 8, core: 2. Of those that a mesh axis runs over, the one named last changes fastest.
Arguments:
- mixer_input: bfloat16 [5120, 32768], P('grp', 'seq'), may hold values from -5 to 5
- step_sizes: float32 [80, 32768], P('grp', 'seq'), may hold values from 0 to 1, as said below
- decay_rates: float32 [80], P('grp'), may hold values from 1 to 2
- skip_gain: float32 [80], P('grp'), may hold values from 0.5 to 1.5
- input_basis: bfloat16 [32768, 128], P('seq'), may hold values from -5 to 5
- output_basis: bfloat16 [32768, 128], P('seq'), may hold values from -0.5 to 0.5
- out_weight: bfloat16 [5120, 2560], P(None, 'grp'), may hold values from -0.078125 to 0.078125
Outputs:
- layer_output: bfloat16 [32768, 2560], P('seq', 'grp')
Inputs may be any that keep to these rules, and one draw needn't show every extreme that they name: `step_sizes`: positive step sizes.
All inputs are finite; a program needn't handle non-finite values.
Results may differ from a plain program's by a relative error of at most 0.0065.
Values may be sent and summed in bfloat16 or wider, within the bound.
A program may use at most 128 MiB of HBM per device.

v0:
```python
import jax
import jax.numpy as jnp
from jax import lax
from jax.sharding import PartitionSpec as P

HP = 64
N = 128
GROUP = 256


def entering_2(value, axis, combine, identity):
    peers, here = (lax.axis_size(axis), lax.axis_index(axis))
    everything = jax.tree.map(
        lambda part, kind: lax.all_gather(part.astype(kind), axis),
        value,
        (jnp.bfloat16, jnp.bfloat16),
    )
    start = jax.tree.map(
        lambda part, zero: jnp.broadcast_to(jnp.asarray(zero, part.dtype), part.shape),
        value,
        identity,
    )

    def lap(k, before):
        reached = k < here
        new = combine(
            before, jax.tree.map(lambda part, own: part[k].astype(own.dtype), everything, value)
        )
        return jax.tree.map(lambda a, b: jnp.where(reached, a, b), new, before)

    return lax.fori_loop(0, peers, lap, start)


def carry_in(total_log, final_state):
    total_decay = jnp.exp(total_log)

    def combine(earlier, later):
        return (earlier[0] * later[0], later[0][:, None, None] * earlier[1] + later[1])

    identity = (jnp.ones_like(total_decay), jnp.zeros_like(final_state))
    _, carried = entering_2((total_decay, final_state), "seq", combine, identity)
    return carried


def on_device(
    mixer_input, step_sizes, decay_rates, skip_gain, input_basis, output_basis, out_weight
):
    heads_here = step_sizes.shape[0]
    tokens_here = step_sizes.shape[1]
    count = tokens_here // GROUP
    channels = mixer_input.reshape(heads_here, HP, count, GROUP)
    log_decay = -(decay_rates[:, None] * step_sizes).reshape(heads_here, count, GROUP)
    steps_blocked = step_sizes.reshape(heads_here, count, GROUP)
    running = jnp.cumsum(log_decay, axis=2)
    basis_in_blocked = input_basis.reshape(count, GROUP, N)
    basis_out_blocked = output_basis.reshape(count, GROUP, N)
    gram = jnp.einsum(
        "cin,cjn->cij", basis_out_blocked, basis_in_blocked, preferred_element_type=jnp.float32
    )
    rows_index = lax.broadcasted_iota(jnp.int32, (GROUP, GROUP), 0)
    cols_index = lax.broadcasted_iota(jnp.int32, (GROUP, GROUP), 1)
    causal = rows_index >= cols_index
    gaps = running[:, :, :, None] - running[:, :, None, :]
    mixing = jnp.where(
        causal,
        gram[None] * jnp.exp(jnp.where(causal, gaps, 0.0)) * steps_blocked[:, :, None, :],
        0.0,
    ).astype(jnp.bfloat16)
    inner = jnp.einsum("hcij,hpcj->hpci", mixing, channels, preferred_element_type=jnp.float32)
    tail = jnp.exp(running[:, :, -1:] - running) * steps_blocked
    weighted_terms = (basis_in_blocked.astype(jnp.float32)[None] * tail[:, :, :, None]).astype(
        jnp.bfloat16
    )
    summaries = jnp.einsum(
        "hcjn,hpcj->chnp", weighted_terms, channels, preferred_element_type=jnp.float32
    )
    block_decay = jnp.exp(running[:, :, -1])

    def advance(state, pair):
        decay, digest_record = pair
        return (decay[:, None, None] * state + digest_record, state)

    zero_state = jnp.zeros((heads_here, N, HP), jnp.float32)
    final_state, entering = lax.scan(advance, zero_state, (block_decay.T, summaries))
    block_sums = jnp.sum(log_decay, axis=2)
    prefix = jnp.exp(jnp.cumsum(block_sums, axis=1) - block_sums)
    total_log = jnp.sum(block_sums, axis=1)
    basis_out_wide = basis_out_blocked.astype(jnp.float32)
    within = jnp.exp(running)[:, None]
    direct = skip_gain[:, None, None, None] * channels.astype(jnp.float32)
    carried = carry_in(total_log, final_state)
    states = entering + prefix.T[:, :, None, None] * carried[None]
    from_state = jnp.einsum(
        "cin,chnp->hpci", basis_out_wide, states, precision=lax.Precision.HIGHEST
    )
    mixed = inner + from_state * within + direct
    mixed_columns = mixed.astype(jnp.bfloat16).reshape(heads_here * HP, tokens_here)
    result = jnp.einsum(
        "kt,kd->td",
        lax.all_gather(mixed_columns, "grp", axis=0, tiled=True),
        out_weight,
        preferred_element_type=jnp.float32,
    )
    return result.astype(jnp.bfloat16)


def solution(mesh):
    placed = (
        P("grp", "seq"),
        P("grp", "seq"),
        P("grp"),
        P("grp"),
        P("seq", None),
        P("seq", None),
        P(None, "grp"),
    )
    return jax.shard_map(
        on_device, mesh=mesh, in_specs=placed, out_specs=P("seq", "grp"), check_vma=False
    )
```

profile of v0, /device:TPU:1, one launch (start us, length us, event | category | flops | bytes accessed | tf_op | source)
XLA Modules:
  0.0 377.4 jit_solution(3592990008132862632)
XLA Ops:
  14.0 5.1 %reduce-window.6 = f32[10,4,2,128]{3,0,1,2:T(8,128)} reduce-window(f32[10,4,2,128]{3,0,1,2:T(8,128)} %copy.30, f32[]{:T(128)} %constant.47.clone.1), window={size=1x1x1x128 pad=0_0x0_0x0_0x127_0}, to_apply=%region_0.0 | reduce-window | flops 1300480 | bytes 81924 | tf_op jit(solution)/shard_map/reduce-window
  27.5 3.8 %reshape.116 = bf16[10,64,4,256]{3,2,1,0:T(4,128)(2,1)} reshape(bf16[640,1024]{1,0:T(8,128)(2,1)} %param.11) | data formatting | bytes 2621440 | tf_op jit(solution)/shard_map/reshape | solution.py:51
  32.1 5.6 %fusion.9 = f32[4,10,128,64]{3,2,1,0:T(8,128)} fusion(f32[10,4,256]{2,0,1:T(8,128)} %copy.35, f32[4,256,128]{2,1,0:T(8,128)} %convert_element_type.64, bf16[10,64,4,256]{3,2,1,0:T(4,128)(2,1)} %reshape.116), kind=kOutput, calls=%fused_computation.17 | convolution fusion | flops 170393600 | bytes 3186688 | tf_op jit(solution)/shard_map/hcjn,hpcj->chnp/dot_general | solution.py:74
  37.8 15.7 %while.27 = (s32[]{:T(128)}, f32[10,128,64]{2,1,0:T(8,128)}, f32[4,10,128,64]{3,2,1,0:T(8,128)}, f32[4,10]{1,0:T(4,128)S(1)}, f32[4,10,128,64]{3,2,1,0:T(8,128)}, /*index=5*/s32[]{:T(128)}, s32[]{:T(128)}) while((s32[]{:T(128)}, f32[10,128,64]{2,1,0:T(8,128)}, f32[4,10,128,64]{3,2,1,0:T(8,128)}, f32[4,10]{1,0:T(4,128)S(1)}, ...), condition=%wide.region_3.4_spmd.clone, body=%wide.region_2.3_spmd.clone.sunk | while | flops 327683 | bytes 2294488 | solution.py:84
  42.7 2.3 bitcast_add_fusion.2
  47.0 2.3 bitcast_add_fusion.2
  51.2 2.3 bitcast_add_fusion.2
  58.5 64.9 %all-reduce = bf16[320]{0:T(512)(128)(2,1)S(1)} all-reduce(bf16[320]{0:T(512)(128)(2,1)S(1)} %dynamic-update-slice), channel_id=2, replica_groups=mesh['seq'=32,'grp'=8] {'seq'}, use_global_device_ids=true, to_apply=%add | all-reduce | flops 320 | bytes 1280
  127.2 2.2 fusion.23
  129.4 12.8 %all-gather.7.cloned.1.call-done = bf16[320,128,64]{1,2,0:T(8,128)(2,1)} async-done(((bf16[10,128,64]{1,2,0:T(8,128)(2,1)}), bf16[320,128,64]{1,2,0:T(8,128)(2,1)}) %all-gather.7.cloned.1.call-update) | async-done | bytes 5242896 | tf_op jit(solution)/shard_map/all_gather | solution.py:14
  142.2 149.2 %while.28 = (s32[]{:T(128)}, f32[10,128,64]{2,1,0:T(8,128)}, s32[]{:T(128)}, bf16[32,10]{1,0:T(8,128)(2,1)}, bf16[32,10,128,64]{2,3,1,0:T(8,128)(2,1)}, /*index=5*/s32[]{:T(128)}, s32[]{:T(128)}) while((s32[]{:T(128)}, f32[10,128,64]{2,1,0:T(8,128)}, s32[]{:T(128)}, bf16[32,10]{1,0:T(8,128)(2,1)}, ...), condition=%wide.region_8.9_spmd.clone, body=%wide.region_7.8_spmd.clone.sunk | while | flops 409614 | bytes 1474765 | solution.py:31
  149.2 2.2 fusion.33
  153.8 2.2 fusion.33
  158.5 2.2 fusion.33
  163.1 2.2 fusion.33
  167.8 2.2 fusion.33
  172.5 2.2 fusion.33
  177.1 2.2 fusion.33
  181.8 2.2 fusion.33
  186.5 2.2 fusion.33
  191.2 2.2 fusion.33
  195.9 2.2 fusion.33
  200.6 2.2 fusion.33
  219.3 2.2 fusion.33
  233.2 2.2 fusion.33
  247.1 2.2 fusion.33
  261.1 2.2 fusion.33
  279.8 2.2 fusion.33
  291.4 4.4 %fusion.13 = f32[4,10,64,256]{3,2,0,1:T(8,128)S(1)} fusion(bf16[4,256,128,1]{2,1,0,3:T(8,128)(2,1)} %bitcast.58, f32[4,10,128,64]{3,2,1,0:T(8,128)} %get-tuple-element.127, f32[10,128,64]{2,1,0:T(8,128)} %get-tuple-element.129, f32[4,10]{1,0:T(4,128)S(1)} %copy.38), kind=kOutput, calls=%fused_computation.22 | convolution fusion | flops 1007288320 | bytes 4522144 | tf_op jit(solution)/shard_map/cin,chnp->hpci/dot_general | solution.py:93
  295.9 4.0 %fusion.12 = bf16[10,64,4,256]{3,1,2,0:T(8,128)(2,1)S(1)} fusion(f32[4,10,64,256]{3,2,0,1:T(8,128)S(1)} %fusion.13, f32[10,4,256]{2,1,0:T(4,128)S(1)} %copy-done.6, f32[10,4,256]{2,1,0:T(4,128)S(1)} %copy-done.5, f32[4,256,256]{2,1,0:T(8,128)S(1)} %copy-done.2, pred[256,256]{1,0:T(8,128)(4,1)S(1)} %copy-done.7, bf16[10,64,4,256]{3,2,1,0:T(4,128)(2,1)S(1)} %copy-done.1, ...), kind=kOutput, calls=%fused_computation.21 | convolution fusion | flops 355205120 | bytes 6479912 | tf_op jit(solution)/shard_map/hcij,hpcj->hpci/dot_general | solution.py:69
  302.3 61.1 %all-gather.5.cloned.1.call-done = bf16[5120,1024]{1,0:T(8,128)(2,1)} async-done(((bf16[640,1024]{1,0:T(8,128)(2,1)}), bf16[5120,1024]{1,0:T(8,128)(2,1)}) %all-gather.5.cloned.1.call-update) | async-done | bytes 10485776 | tf_op jit(solution)/shard_map/all_gather | solution.py:100
  363.4 7.2 %convolution_convert_fusion = bf16[1024,320]{0,1:T(8,128)(2,1)} fusion(bf16[5120,320]{0,1:T(8,128)(2,1)S(1)} %copy-done, bf16[5120,1024]{1,0:T(8,128)(2,1)} %all-gather.5.cloned.1.call-done), kind=kOutput, calls=%fused_computation.27 | convolution fusion | flops 3355770880 | bytes 14417920 | tf_op jit(solution)/shard_map/kt,kd->td/dot_general | solution.py:98
  (184 shorter events, 148.4 us)
Async XLA Ops:
  6.5 356.9 %copy-start = (bf16[5120,320]{0,1:T(8,128)(2,1)S(1)}, bf16[5120,320]{0,1:T(8,128)(2,1)}, u32[]{:S(2)}) copy-start(bf16[5120,320]{0,1:T(8,128)(2,1)} %param.17) | copy-start | bytes 9830404
  6.5 24.7 %copy-start.3 = (bf16[1024,128]{1,0:T(8,128)(2,1)S(1)}, bf16[1024,128]{1,0:T(8,128)(2,1)}, u32[]{:S(2)}) copy-start(bf16[1024,128]{1,0:T(8,128)(2,1)} %param.15) | copy-start | bytes 786436
  6.5 135.6 %all-gather.7.cloned.1.call-start = ((), (), s32[]{:S(2)}) async-start(), calls=%async_computation.1 | async-start | bytes 5406720 | tf_op jit(solution)/shard_map/all_gather | solution.py:14
  9.8 0.6 copy-start.4
  37.8 19.2 %copy-start.11 = (u32[256]{0:T(256)S(1)}, u32[256]{0:T(256)}, u32[]{:S(2)}) copy-start(u32[256]{0:T(256)} %constant.56) | copy-start | bytes 3076
  37.8 20.5 %copy-start.9 = (f32[10]{0:T(128)S(1)}, f32[10]{0:T(128)}, u32[]{:S(2)}) copy-start(f32[10]{0:T(128)} %get-tuple-element.206) | copy-start | bytes 124
  55.4 308.0 %all-gather.5.cloned.1.call-start = ((), (), s32[]{:S(2)}) async-start(), calls=%async_computation | async-start | bytes 11796480 | tf_op jit(solution)/shard_map/all_gather | solution.py:100
  291.3 4.5 %copy-start.1 = (bf16[10,64,4,256]{3,2,1,0:T(4,128)(2,1)S(1)}, bf16[10,64,4,256]{3,2,1,0:T(4,128)(2,1)}, u32[]{:S(2)}) copy-start(bf16[10,64,4,256]{3,2,1,0:T(4,128)(2,1)} %reshape.116) | copy-start | bytes 3932164
  291.4 4.5 %copy-start.2 = (f32[4,256,256]{2,1,0:T(8,128)S(1)}, f32[4,256,256]{2,1,0:T(8,128)}, u32[]{:S(2)}) copy-start(f32[4,256,256]{2,1,0:T(8,128)} %fusion.23) | copy-start | bytes 3145732
  291.4 4.5 %copy-start.5 = (f32[10,4,256]{2,1,0:T(4,128)S(1)}, f32[10,4,256]{2,1,0:T(4,128)}, u32[]{:S(2)}) copy-start(f32[10,4,256]{2,1,0:T(4,128)} %reduce_window_sum.42) | copy-start | bytes 122884
  291.4 4.5 %copy-start.6 = (f32[10,4,256]{2,1,0:T(4,128)S(1)}, f32[10,4,256]{2,1,0:T(4,128)}, u32[]{:S(2)}) copy-start(f32[10,4,256]{2,1,0:T(4,128)} %mul.111) | copy-start | bytes 122884
  291.4 4.5 %copy-start.7 = (pred[256,256]{1,0:T(8,128)(4,1)S(1)}, pred[256,256]{1,0:T(8,128)(4,1)}, u32[]{:S(2)}) copy-start(pred[256,256]{1,0:T(8,128)(4,1)} %iota_compare_fusion) | copy-start | bytes 196612
  291.4 4.5 %copy-start.8 = (f32[10,4,256]{2,1,0:T(4,128)S(1)}, f32[10,4,256]{2,1,0:T(4,128)}, u32[]{:S(2)}) copy-start(f32[10,4,256]{2,1,0:T(4,128)} %get-tuple-element.208) | copy-start | bytes 122884
  291.4 4.5 %copy-start.10 = (f32[10]{0:T(128)S(1)}, f32[10]{0:T(128)}, u32[]{:S(2)}) copy-start(f32[10]{0:T(128)} %param.14) | copy-start | bytes 124
Sparse Core Ops, SparseCore 0:
  55.5 86.6 all-gather.6
  302.5 60.9 all-gather.4
where the time goes:
time: 381 us; the launch traced here: 377 us
  other arithmetic  120 us (31%)
  local copies, waits for them, and re-layouts  81.2 us (21%)
  waiting for transfers between devices  73.9 us (19%)
  blocking collectives  64.9 us (17%)
  matrix products  23.5 us (6%)
  between operations  14.2 us (4%)
    select_n x32, other arithmetic, lap(): return jax.tree.map(lambda a, b: jnp.where(reached, a, b), new, before)  68.9 us
    unnamed x1, blocking collectives  64.9 us
    all_gather x1, waiting for transfers between devices, on_device(): lax.all_gather(mixed_columns, 'grp', axis=0, tiled=True)  61.1 us
    dynamic_slice x64, local copies, waits for them, and re-layouts, lap(): part[k].astype(own.dtype)  58.7 us
    convert_element_type x32, other arithmetic, lap(): part[k].astype(own.dtype)  21.4 us
    all_gather x1, waiting for transfers between devices, entering_2(): lax.all_gather(part.astype(kind), axis)  12.8 us
    add x4, other arithmetic, advance(): return (decay[:, None, None] * state + digest_record, state)  8.81 us
  transfers between devices with their start and end apart: 2, of which 2 were waited for; matrix products, arithmetic and copies ran while one was open for 2% of the time, Pallas kernels for 0%

commit v1 on v0

--- a/solution.py
+++ b/solution.py
@@ -8,38 +8,23 @@
 GROUP = 256
 
 
-def entering_2(value, axis, combine, identity):
-    peers, here = (lax.axis_size(axis), lax.axis_index(axis))
-    everything = jax.tree.map(
-        lambda part, kind: lax.all_gather(part.astype(kind), axis),
-        value,
-        (jnp.bfloat16, jnp.bfloat16),
-    )
-    start = jax.tree.map(
-        lambda part, zero: jnp.broadcast_to(jnp.asarray(zero, part.dtype), part.shape),
-        value,
-        identity,
-    )
+def carry_in(total_log, final_state):
+    peers, here = lax.axis_size("seq"), lax.axis_index("seq")
 
-    def lap(k, before):
-        reached = k < here
-        new = combine(
-            before, jax.tree.map(lambda part, own: part[k].astype(own.dtype), everything, value)
-        )
-        return jax.tree.map(lambda a, b: jnp.where(reached, a, b), new, before)
+    def shifted(value, d):
+        return lax.ppermute(value, "seq", [(i, i + d) for i in range(peers - d)])
 
-    return lax.fori_loop(0, peers, lap, start)
-
-
-def carry_in(total_log, final_state):
-    total_decay = jnp.exp(total_log)
-
-    def combine(earlier, later):
-        return (earlier[0] * later[0], later[0][:, None, None] * earlier[1] + later[1])
-
-    identity = (jnp.ones_like(total_decay), jnp.zeros_like(final_state))
-    _, carried = entering_2((total_decay, final_state), "seq", combine, identity)
-    return carried
+    decay = shifted(jnp.exp(total_log), 1)
+    decay = jnp.where(here >= 1, decay, jnp.ones_like(decay))
+    state = shifted(final_state, 1)
+    d = 1
+    while d < peers:
+        decay_r, state_r = shifted(decay, d), shifted(state, d)
+        reached = here >= d
+        state = jnp.where(reached, decay[:, None, None] * state_r + state, state)
+        decay = jnp.where(reached, decay * decay_r, decay)
+        d *= 2
+    return state
 
 
 def on_device(

time: 381 us -> 232 us (0.61)
  other arithmetic: 120 us -> 33.6 us
  local copies, waits for them, and re-layouts: 81.2 us -> 14.2 us
  starting transfers between devices: 0.04 us -> 65.2 us
  blocking collectives: 64.9 us -> 0 us
  waiting for transfers between devices: 73.9 us -> 81 us
    ppermute x0 -> x11, starting transfers between devices: none -> 65.2 us  [shifted(): return lax.ppermute(value, 'seq', [(i, i + d) for i in range(peers - d)])]
    unnamed x1 -> x0, blocking collectives: 64.9 us -> none
    select_n x32 -> x10, other arithmetic: 68.9 us -> 9.11 us  [the longest x5 7.74 us: carry_in(): state = jnp.where(reached, decay[:, None, None] * state_r + state, state)]
    dynamic_slice x64 -> x0, local copies, waits for them, and re-layouts: 58.7 us -> none  [lap(): part[k].astype(own.dtype)]
    convert_element_type x33 -> x0, other arithmetic: 21.4 us -> none  [the longest x32 21.4 us: lap(): part[k].astype(own.dtype)]
    ppermute x0 -> x11, waiting for transfers between devices: none -> 20.2 us  [shifted(): return lax.ppermute(value, 'seq', [(i, i + d) for i in range(peers - d)])]
    all_gather x1 -> x0, waiting for transfers between devices: 12.8 us -> none  [entering_2(): lax.all_gather(part.astype(kind), axis)]
  transfers between devices with their start and end apart: 2 -> 12, of which waited for: 2 -> 7; matrix products, arithmetic and copies ran while one was open for 2% -> 4% of each run, Pallas kernels for 0% -> 0%
where the time goes in v1:
time: 232 us; the launch traced here: 231 us
  waiting for transfers between devices  81 us (35%)
  starting transfers between devices  65.2 us (28%)
  other arithmetic  33.6 us (14%)
  matrix products  23.4 us (10%)
  local copies, waits for them, and re-layouts  14.2 us (6%)
  between operations  13.7 us (6%)
    ppermute x11, starting transfers between devices, shifted(): return lax.ppermute(value, 'seq', [(i, i + d) for i in range(peers - d)])  65.2 us
    all_gather x1, waiting for transfers between devices, on_device(): lax.all_gather(mixed_columns, 'grp', axis=0, tiled=True)  60.8 us
    ppermute x11, waiting for transfers between devices, shifted(): return lax.ppermute(value, 'seq', [(i, i + d) for i in range(peers - d)])  20.2 us
    add x4, other arithmetic, advance(): return (decay[:, None, None] * state + digest_record, state)  8.81 us
    select_n x5, other arithmetic, carry_in(): state = jnp.where(reached, decay[:, None, None] * state_r + state, state)  7.74 us
    dot_general x1, matrix products, on_device(): jnp.einsum('kt,kd->td', lax.all_gather(mixed_columns, 'grp', axis=0, tile...  7.17 us
    dynamic_update_slice x4, other arithmetic, on_device(): lax.scan(advance, zero_state, (block_decay.T, summaries))  6.89 us
    dot_general x1, matrix products, on_device(): jnp.einsum('hcjn,hpcj->chnp', weighted_terms, channels, preferred_element...  5.63 us
  transfers between devices with their start and end apart: 12, of which 7 were waited for; matrix products, arithmetic and copies ran while one was open for 4% of the time, Pallas kernels for 0%

profile of v1, /device:TPU:1, one launch (start us, length us, event | category | flops | bytes accessed | tf_op | source)
XLA Modules:
  0.0 231.2 jit_solution(14767401530149646596)
XLA Ops:
  9.3 2.3 reduce-window.6
  14.7 3.8 %reshape.94 = bf16[10,64,4,256]{3,2,1,0:T(4,128)(2,1)} reshape(bf16[640,1024]{1,0:T(8,128)(2,1)} %param.9) | data formatting | bytes 2621440 | tf_op jit(solution)/shard_map/reshape | solution.py:36
  18.5 5.6 %fusion.8 = f32[4,10,128,64]{3,2,1,0:T(8,128)} fusion(f32[10,4,256]{2,0,1:T(8,128)S(1)} %copy.35, f32[4,256,128]{2,1,0:T(8,128)} %convert_element_type.24, bf16[10,64,4,256]{3,2,1,0:T(4,128)(2,1)} %reshape.94), kind=kOutput, calls=%fused_computation.13 | convolution fusion | flops 170393600 | bytes 3186688 | tf_op jit(solution)/shard_map/hcjn,hpcj->chnp/dot_general | solution.py:59
  24.1 15.7 %while.13 = (s32[]{:T(128)}, f32[10,128,64]{2,1,0:T(8,128)}, f32[4,10,128,64]{3,2,1,0:T(8,128)}, f32[4,10]{1,0:T(4,128)S(1)}, f32[4,10,128,64]{3,2,1,0:T(8,128)}, /*index=5*/s32[]{:T(128)}, s32[]{:T(128)}) while((s32[]{:T(128)}, f32[10,128,64]{2,1,0:T(8,128)}, f32[4,10,128,64]{3,2,1,0:T(8,128)}, f32[4,10]{1,0:T(4,128)S(1)}, ...), condition=%wide.region_3.4_spmd.clone, body=%wide.region_2.3_spmd.clone.sunk | while | flops 327683 | bytes 2293988 | solution.py:69
  25.1 2.1 bitcast_add_fusion.2
  27.1 2.0 bitcast_dynamic-update-slice_fusion.2
  29.1 2.3 bitcast_add_fusion.2
  31.4 2.0 bitcast_dynamic-update-slice_fusion.2
  33.4 2.3 bitcast_add_fusion.2
  35.6 2.0 bitcast_dynamic-update-slice_fusion.2
  37.6 2.3 bitcast_add_fusion.2
  39.9 2.1 copy.39
  41.9 5.1 %collective-permute-start.5 = (f32[10,128,64]{1,2,0:T(8,128)}, f32[10,128,64]{1,2,0:T(8,128)}, u32[]{:S(2)}, u32[]{:S(2)}) collective-permute-start(f32[10,128,64]{1,2,0:T(8,128)} %copy.39), channel_id=1, source_target_pairs={{0,8},{8,16},{16,24},{24,32},{32,40},{40,48},{48,56},{56,64},{64,7... | collective-permute-start | bytes 983048 | tf_op jit(solution)/shard_map/ppermute | solution.py:15
  47.0 6.0 %collective-permute-done.5 = f32[10,128,64]{1,2,0:T(8,128)} collective-permute-done((f32[10,128,64]{1,2,0:T(8,128)}, f32[10,128,64]{1,2,0:T(8,128)}, u32[]{:S(2)}, u32[]{:S(2)}) %collective-permute-start.5) | collective-permute-done | bytes 327712 | tf_op jit(solution)/shard_map/ppermute | solution.py:15
  53.0 4.8 %collective-permute-start.6 = (f32[10,128,64]{1,2,0:T(8,128)}, f32[10,128,64]{1,2,0:T(8,128)}, u32[]{:S(2)}, u32[]{:S(2)}) collective-permute-start(f32[10,128,64]{1,2,0:T(8,128)} %collective-permute-done.5), channel_id=1, source_target_pairs={{0,8},{8,16},{16,24},{24,32},{32,40},{40,48},{48,56},{56,64},{64,7... | collective-permute-start | bytes 983048 | tf_op jit(solution)/shard_map/ppermute | solution.py:15
  57.8 2.8 %collective-permute-start = (f32[10]{0:T(128)S(1)}, f32[10]{0:T(128)S(1)}, u32[]{:S(2)}, u32[]{:S(2)}) collective-permute-start(f32[10]{0:T(128)S(1)} %negate_exponential_fusion), channel_id=1, source_target_pairs={{0,8},{8,16},{16,24},{24,32},{32,40},{40,48},{48,56},{56,64},{64,7... | collective-permute-start | bytes 128 | tf_op jit(solution)/shard_map/ppermute | solution.py:15
  60.7 2.2 collective-permute-done
  64.8 6.6 %collective-permute-start.7 = (f32[10,128,64]{1,2,0:T(8,128)}, f32[10,128,64]{1,2,0:T(8,128)}, u32[]{:S(2)}, u32[]{:S(2)}) collective-permute-start(f32[10,128,64]{1,2,0:T(8,128)} %add_select_fusion.4), channel_id=1, source_target_pairs={{0,16},{8,24},{16,32},{24,40},{32,48},{40,56},{48,64},{56,72},{64,... | collective-permute-start | bytes 983048 | tf_op jit(solution)/shard_map/ppermute | solution.py:15
  71.3 5.0 %collective-permute-start.1 = (f32[10]{0:T(128)S(1)}, f32[10]{0:T(128)S(1)}, u32[]{:S(2)}, u32[]{:S(2)}) collective-permute-start(f32[10]{0:T(128)S(1)} %broadcast_select_fusion.1), channel_id=1, source_target_pairs={{0,8},{8,16},{16,24},{24,32},{32,40},{40,48},{48,56},{56,64},{64,7... | collective-permute-start | bytes 128 | tf_op jit(solution)/shard_map/ppermute | solution.py:15
  77.0 1.9 add_select_fusion.3
  79.0 20.3 %collective-permute-start.8 = (f32[10,128,64]{1,2,0:T(8,128)}, f32[10,128,64]{1,2,0:T(8,128)}, u32[]{:S(2)}, u32[]{:S(2)}) collective-permute-start(f32[10,128,64]{1,2,0:T(8,128)} %add_select_fusion.3), channel_id=1, source_target_pairs={{0,32},{8,40},{16,48},{24,56},{32,64},{40,72},{48,80},{56,88},{64,... | collective-permute-start | bytes 983048 | tf_op jit(solution)/shard_map/ppermute | solution.py:15
  99.3 2.2 fusion.22
  106.0 7.2 %collective-permute-done.2 = f32[10]{0:T(128)S(1)} collective-permute-done((f32[10]{0:T(128)}, f32[10]{0:T(128)S(1)}, u32[]{:S(2)}, u32[]{:S(2)}) %collective-permute-start.2) | collective-permute-done | bytes 72 | tf_op jit(solution)/shard_map/ppermute | solution.py:15
  115.7 5.6 %collective-permute-start.9 = (f32[10,128,64]{1,2,0:T(8,128)}, f32[10,128,64]{1,2,0:T(8,128)}, u32[]{:S(2)}, u32[]{:S(2)}) collective-permute-start(f32[10,128,64]{1,2,0:T(8,128)} %add_select_fusion.2), channel_id=1, source_target_pairs={{0,64},{8,72},{16,80},{24,88},{32,96},{40,104},{48,112},{56,120},{... | collective-permute-start | bytes 983048 | tf_op jit(solution)/shard_map/ppermute | solution.py:15
  122.1 3.8 %collective-permute-start.3 = (f32[10]{0:T(128)}, f32[10]{0:T(128)S(1)}, u32[]{:S(2)}, u32[]{:S(2)}) collective-permute-start(f32[10]{0:T(128)} %copy-done.13), channel_id=1, source_target_pairs={{0,32},{8,40},{16,48},{24,56},{32,64},{40,72},{48,80},{56,88},{64,... | collective-permute-start | bytes 128 | tf_op jit(solution)/shard_map/ppermute | solution.py:15
  128.7 8.7 %collective-permute-start.10 = (f32[10,128,64]{1,2,0:T(8,128)S(1)}, f32[10,128,64]{1,2,0:T(8,128)S(1)}, u32[]{:S(2)}, u32[]{:S(2)}) collective-permute-start(f32[10,128,64]{1,2,0:T(8,128)S(1)} %add_select_fusion.1), channel_id=1, source_target_pairs={{0,128},{8,136},{16,144},{24,152},{32,160},{40,168},{48,176},{56,1... | collective-permute-start | bytes 983048 | tf_op jit(solution)/shard_map/ppermute | solution.py:15
  139.3 3.3 %collective-permute-done.4 = f32[10]{0:T(128)S(1)} collective-permute-done((f32[10]{0:T(128)S(1)}, f32[10]{0:T(128)S(1)}, u32[]{:S(2)}, u32[]{:S(2)}) %collective-permute-start.4) | collective-permute-done | bytes 72 | tf_op jit(solution)/shard_map/ppermute | solution.py:15
  143.5 2.0 copy.40
  145.6 4.4 %fusion.12 = f32[4,10,64,256]{3,2,0,1:T(8,128)S(1)} fusion(bf16[4,256,128,1]{2,1,0,3:T(8,128)(2,1)S(1)} %bitcast.46, f32[4,10,128,64]{3,2,1,0:T(8,128)} %get-tuple-element.33, f32[10,128,64]{2,1,0:T(8,128)} %copy.40, f32[4,10]{1,0:T(4,128)S(1)} %copy.38), kind=kOutput, calls=%fused_computation.18 | convolution fusion | flops 1007288320 | bytes 4522144 | tf_op jit(solution)/shard_map/cin,chnp->hpci/dot_general | solution.py:78
  150.0 4.0 %fusion.11 = bf16[10,64,4,256]{3,1,2,0:T(8,128)(2,1)S(1)} fusion(f32[4,10,64,256]{3,2,0,1:T(8,128)S(1)} %fusion.12, f32[10,4,256]{2,1,0:T(4,128)S(1)} %copy-done.9, f32[10,4,256]{2,1,0:T(4,128)S(1)} %copy-done.7, f32[4,256,256]{2,1,0:T(8,128)S(1)} %copy-done.2, pred[256,256]{1,0:T(8,128)(4,1)S(1)} %copy-done.10, bf16[10,64,4,256]{3,2,1,0:T(4,128)(2,1)S(1)} %copy-done.1, ...), kind=kOutput, calls=%fused_computation.17 | convolution fusion | flops 355205120 | bytes 6479912 | tf_op jit(solution)/shard_map/hcij,hpcj->hpci/dot_general | solution.py:54
  156.4 60.8 %all-gather.2.cloned.1.call-done = bf16[5120,1024]{1,0:T(8,128)(2,1)} async-done(((bf16[640,1024]{1,0:T(8,128)(2,1)}), bf16[5120,1024]{1,0:T(8,128)(2,1)}) %all-gather.2.cloned.1.call-update) | async-done | bytes 10485776 | tf_op jit(solution)/shard_map/all_gather | solution.py:85
  217.2 7.2 %convolution_convert_fusion = bf16[1024,320]{0,1:T(8,128)(2,1)} fusion(bf16[5120,320]{0,1:T(8,128)(2,1)S(1)} %copy-done, bf16[5120,1024]{1,0:T(8,128)(2,1)} %all-gather.2.cloned.1.call-done), kind=kOutput, calls=%fused_computation.23 | convolution fusion | flops 3355770880 | bytes 14417920 | tf_op jit(solution)/shard_map/kt,kd->td/dot_general | solution.py:83
  (85 shorter events, 25.2 us)
Async XLA Ops:
  6.5 210.6 %copy-start = (bf16[5120,320]{0,1:T(8,128)(2,1)S(1)}, bf16[5120,320]{0,1:T(8,128)(2,1)}, u32[]{:S(2)}) copy-start(bf16[5120,320]{0,1:T(8,128)(2,1)} %param.15) | copy-start | bytes 9830404
  6.5 210.6 %all-gather.2.cloned.1.call-start = ((), (), s32[]{:S(2)}) async-start(), calls=%async_computation | async-start | bytes 11796480 | tf_op jit(solution)/shard_map/all_gather | solution.py:85
  7.6 16.6 %copy-start.8 = (f32[10,4,256]{2,1,0:T(4,128)}, f32[10,4,256]{2,1,0:T(4,128)S(1)}, u32[]{:S(2)}) copy-start(f32[10,4,256]{2,1,0:T(4,128)S(1)} %mul.141) | copy-start | bytes 122884
  8.6 0.6 copy-start.5
  12.0 12.1 %copy-start.6 = (f32[10,4,256]{2,1,0:T(4,128)}, f32[10,4,256]{2,1,0:T(4,128)S(1)}, u32[]{:S(2)}) copy-start(f32[10,4,256]{2,1,0:T(4,128)S(1)} %reduce_window_sum.42) | copy-start | bytes 122884
  39.9 59.4 %copy-start.3 = (bf16[1024,128]{1,0:T(8,128)(2,1)S(1)}, bf16[1024,128]{1,0:T(8,128)(2,1)}, u32[]{:S(2)}) copy-start(bf16[1024,128]{1,0:T(8,128)(2,1)} %param.13) | copy-start | bytes 786436
  41.9 11.0 %collective-permute-start.5 = (f32[10,128,64]{1,2,0:T(8,128)}, f32[10,128,64]{1,2,0:T(8,128)}, u32[]{:S(2)}, u32[]{:S(2)}) collective-permute-start(f32[10,128,64]{1,2,0:T(8,128)} %copy.39), channel_id=1, source_target_pairs={{0,8},{8,16},{16,24},{24,32},{32,40},{40,48},{48,56},{56,64},{64,7... | collective-permute-start | bytes 983048 | tf_op jit(solution)/shard_map/ppermute | solution.py:15
  53.0 9.9 %collective-permute-start.6 = (f32[10,128,64]{1,2,0:T(8,128)}, f32[10,128,64]{1,2,0:T(8,128)}, u32[]{:S(2)}, u32[]{:S(2)}) collective-permute-start(f32[10,128,64]{1,2,0:T(8,128)} %collective-permute-done.5), channel_id=1, source_target_pairs={{0,8},{8,16},{16,24},{24,32},{32,40},{40,48},{48,56},{56,64},{64,7... | collective-permute-start | bytes 983048 | tf_op jit(solution)/shard_map/ppermute | solution.py:15
  57.8 5.0 %collective-permute-start = (f32[10]{0:T(128)S(1)}, f32[10]{0:T(128)S(1)}, u32[]{:S(2)}, u32[]{:S(2)}) collective-permute-start(f32[10]{0:T(128)S(1)} %negate_exponential_fusion), channel_id=1, source_target_pairs={{0,8},{8,16},{16,24},{24,32},{32,40},{40,48},{48,56},{56,64},{64,7... | collective-permute-start | bytes 128 | tf_op jit(solution)/shard_map/ppermute | solution.py:15
  64.8 12.3 %collective-permute-start.7 = (f32[10,128,64]{1,2,0:T(8,128)}, f32[10,128,64]{1,2,0:T(8,128)}, u32[]{:S(2)}, u32[]{:S(2)}) collective-permute-start(f32[10,128,64]{1,2,0:T(8,128)} %add_select_fusion.4), channel_id=1, source_target_pairs={{0,16},{8,24},{16,32},{24,40},{32,48},{40,56},{48,64},{56,72},{64,... | collective-permute-start | bytes 983048 | tf_op jit(solution)/shard_map/ppermute | solution.py:15
  71.3 5.7 %collective-permute-start.1 = (f32[10]{0:T(128)S(1)}, f32[10]{0:T(128)S(1)}, u32[]{:S(2)}, u32[]{:S(2)}) collective-permute-start(f32[10]{0:T(128)S(1)} %broadcast_select_fusion.1), channel_id=1, source_target_pairs={{0,8},{8,16},{16,24},{24,32},{32,40},{40,48},{48,56},{56,64},{64,7... | collective-permute-start | bytes 128 | tf_op jit(solution)/shard_map/ppermute | solution.py:15
  77.0 22.3 %copy-start.12 = (f32[10]{0:T(128)}, f32[10]{0:T(128)S(1)}, u32[]{:S(2)}) copy-start(f32[10]{0:T(128)S(1)} %broadcast_select_fusion) | copy-start | bytes 124
  79.0 34.9 %collective-permute-start.8 = (f32[10,128,64]{1,2,0:T(8,128)}, f32[10,128,64]{1,2,0:T(8,128)}, u32[]{:S(2)}, u32[]{:S(2)}) collective-permute-start(f32[10,128,64]{1,2,0:T(8,128)} %add_select_fusion.3), channel_id=1, source_target_pairs={{0,32},{8,40},{16,48},{24,56},{32,64},{40,72},{48,80},{56,88},{64,... | collective-permute-start | bytes 983048 | tf_op jit(solution)/shard_map/ppermute | solution.py:15
  101.5 44.0 %copy-start.4 = (bf16[1024,128]{1,0:T(8,128)(2,1)S(1)}, bf16[1024,128]{1,0:T(8,128)(2,1)}, u32[]{:S(2)}) copy-start(bf16[1024,128]{1,0:T(8,128)(2,1)} %param.14) | copy-start | bytes 786436
  104.7 8.5 %collective-permute-start.2 = (f32[10]{0:T(128)}, f32[10]{0:T(128)S(1)}, u32[]{:S(2)}, u32[]{:S(2)}) collective-permute-start(f32[10]{0:T(128)} %copy-done.12), channel_id=1, source_target_pairs={{0,16},{8,24},{16,32},{24,40},{32,48},{40,56},{48,64},{56,72},{64,... | collective-permute-start | bytes 128 | tf_op jit(solution)/shard_map/ppermute | solution.py:15
  113.8 1.9 copy-start.13
  115.7 11.8 %collective-permute-start.9 = (f32[10,128,64]{1,2,0:T(8,128)}, f32[10,128,64]{1,2,0:T(8,128)}, u32[]{:S(2)}, u32[]{:S(2)}) collective-permute-start(f32[10,128,64]{1,2,0:T(8,128)} %add_select_fusion.2), channel_id=1, source_target_pairs={{0,64},{8,72},{16,80},{24,88},{32,96},{40,104},{48,112},{56,120},{... | collective-permute-start | bytes 983048 | tf_op jit(solution)/shard_map/ppermute | solution.py:15
  122.1 4.7 %collective-permute-start.3 = (f32[10]{0:T(128)}, f32[10]{0:T(128)S(1)}, u32[]{:S(2)}, u32[]{:S(2)}) collective-permute-start(f32[10]{0:T(128)} %copy-done.13), channel_id=1, source_target_pairs={{0,32},{8,40},{16,48},{24,56},{32,64},{40,72},{48,80},{56,88},{64,... | collective-permute-start | bytes 128 | tf_op jit(solution)/shard_map/ppermute | solution.py:15
  128.7 13.9 %collective-permute-start.10 = (f32[10,128,64]{1,2,0:T(8,128)S(1)}, f32[10,128,64]{1,2,0:T(8,128)S(1)}, u32[]{:S(2)}, u32[]{:S(2)}) collective-permute-start(f32[10,128,64]{1,2,0:T(8,128)S(1)} %add_select_fusion.1), channel_id=1, source_target_pairs={{0,128},{8,136},{16,144},{24,152},{32,160},{40,168},{48,176},{56,1... | collective-permute-start | bytes 983048 | tf_op jit(solution)/shard_map/ppermute | solution.py:15
  138.0 4.6 %collective-permute-start.4 = (f32[10]{0:T(128)S(1)}, f32[10]{0:T(128)S(1)}, u32[]{:S(2)}, u32[]{:S(2)}) collective-permute-start(f32[10]{0:T(128)S(1)} %broadcast_select_fusion.3), channel_id=1, source_target_pairs={{0,64},{8,72},{16,80},{24,88},{32,96},{40,104},{48,112},{56,120},{... | collective-permute-start | bytes 128 | tf_op jit(solution)/shard_map/ppermute | solution.py:15
  145.5 4.4 %copy-start.1 = (bf16[10,64,4,256]{3,2,1,0:T(4,128)(2,1)S(1)}, bf16[10,64,4,256]{3,2,1,0:T(4,128)(2,1)}, u32[]{:S(2)}) copy-start(bf16[10,64,4,256]{3,2,1,0:T(4,128)(2,1)} %reshape.94) | copy-start | bytes 3932164
  145.5 4.4 %copy-start.2 = (f32[4,256,256]{2,1,0:T(8,128)S(1)}, f32[4,256,256]{2,1,0:T(8,128)}, u32[]{:S(2)}) copy-start(f32[4,256,256]{2,1,0:T(8,128)} %fusion.22) | copy-start | bytes 3145732
  145.5 4.5 %copy-start.7 = (f32[10,4,256]{2,1,0:T(4,128)S(1)}, f32[10,4,256]{2,1,0:T(4,128)}, u32[]{:S(2)}) copy-start(f32[10,4,256]{2,1,0:T(4,128)} %copy-done.6) | copy-start | bytes 122884
  145.5 4.5 %copy-start.9 = (f32[10,4,256]{2,1,0:T(4,128)S(1)}, f32[10,4,256]{2,1,0:T(4,128)}, u32[]{:S(2)}) copy-start(f32[10,4,256]{2,1,0:T(4,128)} %copy-done.8) | copy-start | bytes 122884
  145.5 4.5 %copy-start.10 = (pred[256,256]{1,0:T(8,128)(4,1)S(1)}, pred[256,256]{1,0:T(8,128)(4,1)}, u32[]{:S(2)}) copy-start(pred[256,256]{1,0:T(8,128)(4,1)} %iota_compare_fusion) | copy-start | bytes 196612
  145.5 4.5 %copy-start.11 = (f32[10,4,256]{2,1,0:T(4,128)S(1)}, f32[10,4,256]{2,1,0:T(4,128)}, u32[]{:S(2)}) copy-start(f32[10,4,256]{2,1,0:T(4,128)} %get-tuple-element.80) | copy-start | bytes 122884
  145.5 4.5 %copy-start.14 = (f32[10]{0:T(128)S(1)}, f32[10]{0:T(128)}, u32[]{:S(2)}) copy-start(f32[10]{0:T(128)} %param.12) | copy-start | bytes 124
Sparse Core Ops, SparseCore 0:
  156.5 60.5 all-gather.1

commit v2 on v1

--- a/solution.py
+++ b/solution.py
@@ -1,6 +1,10 @@
+import functools
+
 import jax
 import jax.numpy as jnp
 from jax import lax
+from jax.experimental import pallas as pl
+from jax.experimental.pallas import tpu as pltpu
 from jax.sharding import PartitionSpec as P
 
 HP = 64
@@ -8,26 +12,80 @@
 GROUP = 256
 
 
-def carry_in(total_log, final_state):
-    peers, here = lax.axis_size("seq"), lax.axis_index("seq")
+def scan_kernel(peers, names, msg_ref, out_ref, inc_ref, recv_ref, send_sem, recv_sem):
+    here = lax.axis_index("seq")
+    grp_here = lax.axis_index("grp")
+    rows = msg_ref.shape[1] - 8
 
-    def shifted(value, d):
-        return lax.ppermute(value, "seq", [(i, i + d) for i in range(peers - d)])
+    def device(target):
+        return tuple(target if name == "seq" else grp_here for name in names)
 
-    decay = shifted(jnp.exp(total_log), 1)
-    decay = jnp.where(here >= 1, decay, jnp.ones_like(decay))
-    state = shifted(final_state, 1)
-    d = 1
+    offsets = sorted({d % peers for d in _hops(peers)} | {(-d) % peers for d in _hops(peers)})
+    barrier = pltpu.get_barrier_semaphore()
+    for offset in offsets:
+        pl.semaphore_signal(
+            barrier, inc=1, device_id=device(lax.rem(here + offset, peers)),
+            device_id_type=pl.DeviceIdType.MESH,
+        )
+    pl.semaphore_wait(barrier, len(offsets))
+
+    inc_ref[...] = msg_ref[...]
+    out_ref[:, :rows] = jnp.zeros((out_ref.shape[0], rows, out_ref.shape[2]), jnp.float32)
+    out_ref[:, rows:] = jnp.ones((out_ref.shape[0], 8, out_ref.shape[2]), jnp.float32)
+    for r, d in enumerate(_hops(peers)):
+        copy = pltpu.make_async_remote_copy(
+            src_ref=inc_ref,
+            dst_ref=recv_ref.at[r],
+            send_sem=send_sem.at[r],
+            recv_sem=recv_sem.at[r],
+            device_id=device(lax.rem(here + d, peers)),
+            device_id_type=pl.DeviceIdType.MESH,
+        )
+        copy.start()
+        copy.wait()
+        reached = here >= d
+        got_state = recv_ref[r, :, :rows, :]
+        got_decay = recv_ref[r, :, rows:, :]
+        for ref in ((out_ref, inc_ref) if 2 * d < peers else (out_ref,)):
+            decay = ref[:, rows:rows + 1, :]
+            ref[:, :rows] = jnp.where(reached, decay * got_state + ref[:, :rows], ref[:, :rows])
+            ref[:, rows:] = jnp.where(reached, decay * got_decay, ref[:, rows:])
+
+
+def _hops(peers):
+    d, hops = 1, []
     while d < peers:
-        decay_r, state_r = shifted(decay, d), shifted(state, d)
-        reached = here >= d
-        state = jnp.where(reached, decay[:, None, None] * state_r + state, state)
-        decay = jnp.where(reached, decay * decay_r, decay)
+        hops.append(d)
         d *= 2
-    return state
+    return hops
+
+
+def carry_in(total_log, final_state, names):
+    peers = lax.axis_size("seq")
+    heads = final_state.shape[0]
+    rows = N * HP // 128
+    state = final_state.reshape(heads, rows, 128)
+    decay = jnp.broadcast_to(jnp.exp(total_log)[:, None, None], (heads, 8, 128))
+    msg = jnp.concatenate([state, decay], axis=1)
+    shape = msg.shape
+    out = pl.pallas_call(
+        functools.partial(scan_kernel, peers, names),
+        out_shape=jax.ShapeDtypeStruct(shape, jnp.float32),
+        in_specs=[pl.BlockSpec(memory_space=pltpu.VMEM)],
+        out_specs=pl.BlockSpec(memory_space=pltpu.VMEM),
+        scratch_shapes=[
+            pltpu.VMEM(shape, jnp.float32),
+            pltpu.VMEM((len(_hops(peers)),) + shape, jnp.float32),
+            pltpu.SemaphoreType.DMA((len(_hops(peers)),)),
+            pltpu.SemaphoreType.DMA((len(_hops(peers)),)),
+        ],
+        compiler_params=pltpu.CompilerParams(collective_id=0, has_side_effects=True),
+    )(msg)
+    return out[:, :rows].reshape(heads, N, HP)
 
 
 def on_device(
+    names,
     mixer_input, step_sizes, decay_rates, skip_gain, input_basis, output_basis, out_weight
 ):
     heads_here = step_sizes.shape[0]
@@ -73,7 +131,7 @@
     basis_out_wide = basis_out_blocked.astype(jnp.float32)
     within = jnp.exp(running)[:, None]
     direct = skip_gain[:, None, None, None] * channels.astype(jnp.float32)
-    carried = carry_in(total_log, final_state)
+    carried = carry_in(total_log, final_state, names)
     states = entering + prefix.T[:, :, None, None] * carried[None]
     from_state = jnp.einsum(
         "cin,chnp->hpci", basis_out_wide, states, precision=lax.Precision.HIGHEST
@@ -100,5 +158,5 @@
         P(None, "grp"),
     )
     return jax.shard_map(
-        on_device, mesh=mesh, in_specs=placed, out_specs=P("seq", "grp"), check_vma=False
+        functools.partial(on_device, mesh.axis_names), mesh=mesh, in_specs=placed, out_specs=P("seq", "grp"), check_vma=False
     )

time: 232 us -> 237 us (1.022)
  Pallas kernels: 0 us -> 73.5 us
  starting transfers between devices: 65.2 us -> 0.01 us
  waiting for transfers between devices: 81 us -> 67.3 us
  local copies, waits for them, and re-layouts: 14.2 us -> 24.7 us
    pallas_call x0 -> x1, Pallas kernels: none -> 73.5 us  [carry_in(): pl.pallas_call(functools.partial(scan_kernel, peers, names), out_shape=ja...]
    ppermute x11 -> x0, starting transfers between devices: 65.2 us -> none  [shifted(): return lax.ppermute(value, 'seq', [(i, i + d) for i in range(peers - d)])]
    ppermute x11 -> x0, waiting for transfers between devices: 20.2 us -> none  [shifted(): return lax.ppermute(value, 'seq', [(i, i + d) for i in range(peers - d)])]
    select_n x10 -> x0, other arithmetic: 9.11 us -> none  [the longest x5 7.74 us: carry_in(): state = jnp.where(reached, decay[:, None, None] * state_r + state, state)]
    all_gather x1, waiting for transfers between devices: 60.8 us -> 67.3 us  [on_device(): lax.all_gather(mixed_columns, 'grp', axis=0, tiled=True)]
    another operation x3, other arithmetic: 2.37 us -> 6.04 us
    neg x2, local copies, waits for them, and re-layouts: 0.05 us -> 2.9 us  [on_device(): -(decay_rates[:, None] * step_sizes).reshape(heads_here, count, GROUP)]
    slice x1 -> x2, local copies, waits for them, and re-layouts: 0.18 us -> 2.75 us  [the longest x1 1.74 us: carry_in(): return out[:, :rows].reshape(heads, N, HP)]
  transfers between devices with their start and end apart: 12 -> 1, of which waited for: 7 -> 1; matrix products, arithmetic and copies ran while one was open for 4% -> 0% of each run, Pallas kernels for 0% -> 0%
where the time goes in v2:
time: 237 us; the launch traced here: 236 us
  Pallas kernels  73.5 us (31%)
  waiting for transfers between devices  67.3 us (28%)
  other arithmetic  33.3 us (14%)
  local copies, waits for them, and re-layouts  24.7 us (10%)
  matrix products  23.4 us (10%)
  between operations  13.6 us (6%)
    pallas_call x1, Pallas kernels, carry_in(): pl.pallas_call(functools.partial(scan_kernel, peers, names), out_shape=ja...  73.5 us
    all_gather x1, waiting for transfers between devices, on_device(): lax.all_gather(mixed_columns, 'grp', axis=0, tiled=True)  67.3 us
    add x4, other arithmetic, advance(): return (decay[:, None, None] * state + digest_record, state)  8.81 us
    dot_general x1, matrix products, on_device(): jnp.einsum('kt,kd->td', lax.all_gather(mixed_columns, 'grp', axis=0, tile...  7.17 us
    dynamic_update_slice x4, other arithmetic, on_device(): lax.scan(advance, zero_state, (block_decay.T, summaries))  6.88 us
    another operation x3, other arithmetic  6.04 us
    dot_general x1, matrix products, on_device(): jnp.einsum('hcjn,hpcj->chnp', weighted_terms, channels, preferred_element...  5.66 us
  transfers between devices with their start and end apart: 1, of which 1 were waited for; matrix products, arithmetic and copies ran while one was open for 0% of the time, Pallas kernels for 0%

profile of v2, /device:TPU:1, one launch (start us, length us, event | category | flops | bytes accessed | tf_op | source)
XLA Modules:
  0.0 235.9 jit_solution(17278178556010201519)
XLA Ops:
  7.2 1.6 mul.91
  8.7 1.7 fusion.19
  10.4 1.5 reshape.97
  11.9 1.5 neg.11
  13.9 1.5 neg.12
  18.4 1.4 copy.30
  19.8 5.1 %reduce-window.6 = f32[10,4,2,128]{3,0,1,2:T(8,128)} reduce-window(f32[10,4,2,128]{3,0,1,2:T(8,128)} %copy.30, f32[]{:T(128)} %constant.16.clone.1), window={size=1x1x1x128 pad=0_0x0_0x0_0x127_0}, to_apply=%region_0.0 | reduce-window | flops 1300480 | bytes 81924 | tf_op jit(solution)/shard_map/reduce-window
  27.5 1.4 reduce_window_sum.42
  28.9 1.4 slice.19
  31.3 1.4 fusion.20
  33.4 1.8 convert_element_type.24
  35.1 2.2 fusion.22
  37.4 3.8 %reshape.96 = bf16[10,64,4,256]{3,2,1,0:T(4,128)(2,1)} reshape(bf16[640,1024]{1,0:T(8,128)(2,1)} %param.9) | data formatting | bytes 2621440 | tf_op jit(solution)/shard_map/reshape | solution.py:94
  41.2 5.7 %fusion.8 = f32[4,10,128,64]{3,2,1,0:T(8,128)} fusion(f32[10,4,256]{2,0,1:T(8,128)} %copy.35, f32[4,256,128]{2,1,0:T(8,128)} %convert_element_type.24, bf16[10,64,4,256]{3,2,1,0:T(4,128)(2,1)} %reshape.96), kind=kOutput, calls=%fused_computation.13 | convolution fusion | flops 170393600 | bytes 3186688 | tf_op jit(solution)/shard_map/hcjn,hpcj->chnp/dot_general | solution.py:117
  46.8 15.7 %while.13 = (s32[]{:T(128)}, f32[10,128,64]{2,1,0:T(8,128)}, f32[4,10,128,64]{3,2,1,0:T(8,128)}, f32[4,10]{1,0:T(4,128)S(1)}, f32[4,10,128,64]{3,2,1,0:T(8,128)}, /*index=5*/s32[]{:T(128)}, s32[]{:T(128)}) while((s32[]{:T(128)}, f32[10,128,64]{2,1,0:T(8,128)}, f32[4,10,128,64]{3,2,1,0:T(8,128)}, f32[4,10]{1,0:T(4,128)S(1)}, ...), condition=%wide.region_3.4_spmd.clone, body=%wide.region_2.3_spmd.clone.sunk | while | flops 327683 | bytes 2293988 | solution.py:127
  47.8 2.1 bitcast_add_fusion.2
  49.8 2.0 bitcast_dynamic-update-slice_fusion.2
  51.8 2.3 bitcast_add_fusion.2
  54.1 2.0 bitcast_dynamic-update-slice_fusion.2
  56.1 2.3 bitcast_add_fusion.2
  58.3 2.0 bitcast_dynamic-update-slice_fusion.2
  60.3 2.3 bitcast_add_fusion.2
  62.6 2.0 reshape.98
  64.6 1.7 pad_maximum_fusion.msg_ref
  66.4 73.5 %shard_map.73 = f32[10,72,128]{2,1,0:T(8,128)} custom-call(f32[10,72,128]{2,1,0:T(8,128)} %pad_maximum_fusion.msg_ref), custom_call_target="tpu_custom_call" | custom-call | tf_op jit(solution)/shard_map/pallas_call | solution.py:71
  139.9 1.7 slice.16
  141.6 2.0 mul.99
  143.7 4.4 %fusion.12 = f32[4,10,64,256]{3,2,0,1:T(8,128)S(1)} fusion(bf16[4,256,128,1]{2,1,0,3:T(8,128)(2,1)S(1)} %bitcast.46, f32[4,10,128,64]{3,2,1,0:T(8,128)} %get-tuple-element.33, f32[10,128,64]{2,1,0:T(8,128)} %mul.99, f32[4,10]{1,0:T(4,128)S(1)} %copy-done.9), kind=kOutput, calls=%fused_computation.18 | convolution fusion | flops 1007288320 | bytes 4522144 | tf_op jit(solution)/shard_map/cin,chnp->hpci/dot_general | solution.py:136
  148.1 4.0 %fusion.11 = bf16[10,64,4,256]{3,1,2,0:T(8,128)(2,1)S(1)} fusion(f32[4,10,64,256]{3,2,0,1:T(8,128)S(1)} %fusion.12, f32[10,4,256]{2,1,0:T(4,128)S(1)} %copy-done.6, f32[10,4,256]{2,1,0:T(4,128)S(1)} %copy-done.5, f32[4,256,256]{2,1,0:T(8,128)S(1)} %copy-done.2, pred[256,256]{1,0:T(8,128)(4,1)S(1)} %copy-done.7, bf16[10,64,4,256]{3,2,1,0:T(4,128)(2,1)S(1)} %copy-done.1, ...), kind=kOutput, calls=%fused_computation.17 | convolution fusion | flops 355205120 | bytes 6479912 | tf_op jit(solution)/shard_map/hcij,hpcj->hpci/dot_general | solution.py:112
  153.2 1.4 copy.45
  154.5 67.3 %all-gather.2.cloned.1.call-done = bf16[5120,1024]{1,0:T(8,128)(2,1)} async-done(((bf16[640,1024]{1,0:T(8,128)(2,1)}), bf16[5120,1024]{1,0:T(8,128)(2,1)}) %all-gather.2.cloned.1.call-update) | async-done | bytes 10485776 | tf_op jit(solution)/shard_map/all_gather | solution.py:143
  221.8 7.2 %convolution_convert_fusion = bf16[1024,320]{0,1:T(8,128)(2,1)} fusion(bf16[5120,320]{0,1:T(8,128)(2,1)S(1)} %copy-done, bf16[5120,1024]{1,0:T(8,128)(2,1)} %all-gather.2.cloned.1.call-done), kind=kOutput, calls=%fused_computation.23 | convolution fusion | flops 3355770880 | bytes 14417920 | tf_op jit(solution)/shard_map/kt,kd->td/dot_general | solution.py:141
  (51 shorter events, 10.4 us)
Async XLA Ops:
  6.5 215.3 %copy-start = (bf16[5120,320]{0,1:T(8,128)(2,1)S(1)}, bf16[5120,320]{0,1:T(8,128)(2,1)}, u32[]{:S(2)}) copy-start(bf16[5120,320]{0,1:T(8,128)(2,1)} %param.15) | copy-start | bytes 9830404
  6.5 28.6 %copy-start.3 = (bf16[1024,128]{1,0:T(8,128)(2,1)S(1)}, bf16[1024,128]{1,0:T(8,128)(2,1)}, u32[]{:S(2)}) copy-start(bf16[1024,128]{1,0:T(8,128)(2,1)} %param.13) | copy-start | bytes 786436
  6.5 215.3 %all-gather.2.cloned.1.call-start = ((), (), s32[]{:S(2)}) async-start(), calls=%async_computation | async-start | bytes 11796480 | tf_op jit(solution)/shard_map/all_gather | solution.py:143
  46.8 17.7 %copy-start.10 = (f32[10]{0:T(128)S(1)}, f32[10]{0:T(128)}, u32[]{:S(2)}) copy-start(f32[10]{0:T(128)} %negate_exponential_fusion) | copy-start | bytes 124
  62.6 81.1 %copy-start.4 = (bf16[1024,128]{1,0:T(8,128)(2,1)S(1)}, bf16[1024,128]{1,0:T(8,128)(2,1)}, u32[]{:S(2)}) copy-start(bf16[1024,128]{1,0:T(8,128)(2,1)} %param.14) | copy-start | bytes 786436
  62.6 81.1 %copy-start.9 = (f32[4,10]{1,0:T(4,128)S(1)}, f32[4,10]{1,0:T(4,128)}, u32[]{:S(2)}) copy-start(f32[4,10]{1,0:T(4,128)} %copy.38) | copy-start | bytes 484
  143.6 4.4 %copy-start.1 = (bf16[10,64,4,256]{3,2,1,0:T(4,128)(2,1)S(1)}, bf16[10,64,4,256]{3,2,1,0:T(4,128)(2,1)}, u32[]{:S(2)}) copy-start(bf16[10,64,4,256]{3,2,1,0:T(4,128)(2,1)} %reshape.96) | copy-start | bytes 3932164
  143.6 4.5 %copy-start.2 = (f32[4,256,256]{2,1,0:T(8,128)S(1)}, f32[4,256,256]{2,1,0:T(8,128)}, u32[]{:S(2)}) copy-start(f32[4,256,256]{2,1,0:T(8,128)} %fusion.22) | copy-start | bytes 3145732
  143.6 4.5 %copy-start.5 = (f32[10,4,256]{2,1,0:T(4,128)S(1)}, f32[10,4,256]{2,1,0:T(4,128)}, u32[]{:S(2)}) copy-start(f32[10,4,256]{2,1,0:T(4,128)} %reduce_window_sum.42) | copy-start | bytes 122884
  143.6 4.5 %copy-start.6 = (f32[10,4,256]{2,1,0:T(4,128)S(1)}, f32[10,4,256]{2,1,0:T(4,128)}, u32[]{:S(2)}) copy-start(f32[10,4,256]{2,1,0:T(4,128)} %mul.91) | copy-start | bytes 122884
  143.6 4.5 %copy-start.7 = (pred[256,256]{1,0:T(8,128)(4,1)S(1)}, pred[256,256]{1,0:T(8,128)(4,1)}, u32[]{:S(2)}) copy-start(pred[256,256]{1,0:T(8,128)(4,1)} %iota_compare_fusion) | copy-start | bytes 196612
  143.7 4.5 %copy-start.8 = (f32[10,4,256]{2,1,0:T(4,128)S(1)}, f32[10,4,256]{2,1,0:T(4,128)}, u32[]{:S(2)}) copy-start(f32[10,4,256]{2,1,0:T(4,128)} %get-tuple-element.80) | copy-start | bytes 122884
  143.7 4.5 %copy-start.11 = (f32[10]{0:T(128)S(1)}, f32[10]{0:T(128)}, u32[]{:S(2)}) copy-start(f32[10]{0:T(128)} %param.12) | copy-start | bytes 124
Sparse Core Ops, SparseCore 0:
  154.7 67.1 all-gather.1

commit v3 on v2

--- a/solution.py
+++ b/solution.py
@@ -12,7 +12,7 @@
 GROUP = 256
 
 
-def scan_kernel(peers, names, msg_ref, out_ref, inc_ref, recv_ref, send_sem, recv_sem):
+def scan_kernel(peers, names, msg_ref, after_ref, out_ref, inc_ref, recv_ref, send_sem, recv_sem):
     here = lax.axis_index("seq")
     grp_here = lax.axis_index("grp")
     rows = msg_ref.shape[1] - 8
@@ -60,7 +60,7 @@
     return hops
 
 
-def carry_in(total_log, final_state, names):
+def carry_in(total_log, final_state, names, after):
     peers = lax.axis_size("seq")
     heads = final_state.shape[0]
     rows = N * HP // 128
@@ -71,7 +71,7 @@
     out = pl.pallas_call(
         functools.partial(scan_kernel, peers, names),
         out_shape=jax.ShapeDtypeStruct(shape, jnp.float32),
-        in_specs=[pl.BlockSpec(memory_space=pltpu.VMEM)],
+        in_specs=[pl.BlockSpec(memory_space=pltpu.VMEM), pl.BlockSpec(memory_space=pl.ANY)],
         out_specs=pl.BlockSpec(memory_space=pltpu.VMEM),
         scratch_shapes=[
             pltpu.VMEM(shape, jnp.float32),
@@ -80,7 +80,8 @@
             pltpu.SemaphoreType.DMA((len(_hops(peers)),)),
         ],
         compiler_params=pltpu.CompilerParams(collective_id=0, has_side_effects=True),
-    )(msg)
+        cost_estimate=pl.CostEstimate(flops=0, transcendentals=0, bytes_accessed=512 * msg.size * 4),
+    )(msg, after)
     return out[:, :rows].reshape(heads, N, HP)
 
 
@@ -126,24 +127,34 @@
     zero_state = jnp.zeros((heads_here, N, HP), jnp.float32)
     final_state, entering = lax.scan(advance, zero_state, (block_decay.T, summaries))
     block_sums = jnp.sum(log_decay, axis=2)
-    prefix = jnp.exp(jnp.cumsum(block_sums, axis=1) - block_sums)
+    log_prefix = jnp.cumsum(block_sums, axis=1) - block_sums
     total_log = jnp.sum(block_sums, axis=1)
     basis_out_wide = basis_out_blocked.astype(jnp.float32)
     within = jnp.exp(running)[:, None]
     direct = skip_gain[:, None, None, None] * channels.astype(jnp.float32)
-    carried = carry_in(total_log, final_state, names)
-    states = entering + prefix.T[:, :, None, None] * carried[None]
-    from_state = jnp.einsum(
-        "cin,chnp->hpci", basis_out_wide, states, precision=lax.Precision.HIGHEST
+    from_local = jnp.einsum(
+        "cin,chnp->hpci", basis_out_wide, entering, precision=lax.Precision.HIGHEST
     )
-    mixed = inner + from_state * within + direct
-    mixed_columns = mixed.astype(jnp.bfloat16).reshape(heads_here * HP, tokens_here)
-    result = jnp.einsum(
-        "kt,kd->td",
-        lax.all_gather(mixed_columns, "grp", axis=0, tiled=True),
-        out_weight,
-        preferred_element_type=jnp.float32,
+    local = (inner + from_local * within + direct).astype(jnp.bfloat16)
+    local_all = lax.all_gather(local.reshape(heads_here * HP, tokens_here), "grp", axis=0, tiled=True)
+    carried = carry_in(total_log, final_state, names, local)
+    scale = jnp.exp(running + log_prefix[:, :, None]).reshape(heads_here, tokens_here)
+    scale_hi = scale.astype(jnp.bfloat16)
+    scale_lo = (scale - scale_hi.astype(jnp.float32)).astype(jnp.bfloat16)
+    message = jnp.concatenate(
+        [carried.reshape(heads_here, N * HP).astype(jnp.bfloat16), scale_hi, scale_lo], axis=1
     )
+    message, local_all = lax.optimization_barrier((message, local_all))
+    message_all = lax.all_gather(message, "grp", axis=0, tiled=True)
+    carried_all = message_all[:, : N * HP].reshape(-1, N, HP)
+    scale_all = message_all[:, N * HP : N * HP + tokens_here].astype(jnp.float32) + message_all[
+        :, N * HP + tokens_here :
+    ].astype(jnp.float32)
+    carry = jnp.einsum(
+        "tn,hnp->hpt", output_basis, carried_all, preferred_element_type=jnp.float32
+    ) * scale_all[:, None, :]
+    mixed = (local_all.astype(jnp.float32) + carry.reshape(local_all.shape)).astype(jnp.bfloat16)
+    result = jnp.einsum("kt,kd->td", mixed, out_weight, preferred_element_type=jnp.float32)
     return result.astype(jnp.bfloat16)
 
 

time: 237 us -> 224 us (0.945)
  waiting for transfers between devices: 67.3 us -> 36.8 us
  other arithmetic: 33.3 us -> 46.8 us
  matrix products: 23.4 us -> 26.9 us
    all_gather x1 -> x2, waiting for transfers between devices: 67.3 us -> 36.8 us  [the longest x1 36.8 us: on_device(): message_all = lax.all_gather(message, 'grp', axis=0, tiled=True)]
    convert_element_type x0 -> x3, other arithmetic: none -> 16.8 us  [the longest x1 11.4 us: on_device(): (local_all.astype(jnp.float32) + carry.reshape(local_all.shape)).astype(j...]
    reshape x0 -> x2, local copies, waits for them, and re-layouts: none -> 6.03 us  [the longest x1 4.84 us: on_device(): carried_all = message_all[:, :N * HP].reshape(-1, N, HP)]
    unnamed x25 -> x28, local copies, waits for them, and re-layouts: 1.41 us -> 6.92 us
    another operation x4, other arithmetic: 6.8 us -> 3.22 us
    mul x2 -> x0, local copies, waits for them, and re-layouts: 3.54 us -> none  [the longest x1 1.98 us: on_device(): states = entering + prefix.T[:, :, None, None] * carried[None]]
    neg x2, local copies, waits for them, and re-layouts: 2.9 us -> 0.05 us  [on_device(): -(decay_rates[:, None] * step_sizes).reshape(heads_here, count, GROUP)]
    dot_general x2 -> x3, matrix products: 11.6 us -> 14.2 us  [the longest x1 7.17 us: on_device(): jnp.einsum('kt,kd->td', mixed, out_weight, preferred_element_type=jnp.flo...]
  transfers between devices with their start and end apart: 1 -> 2, of which waited for: 1 -> 1; matrix products, arithmetic and copies ran while one was open for 0% -> 6% of each run, Pallas kernels for 0% -> 32%
where the time goes in v3:
time: 224 us; the launch traced here: 223 us
  Pallas kernels  72.4 us (32%)
  other arithmetic  46.8 us (21%)
  waiting for transfers between devices  36.8 us (16%)
  matrix products  26.9 us (12%)
  local copies, waits for them, and re-layouts  25.9 us (12%)
  between operations  13.6 us (6%)
    pallas_call x1, Pallas kernels, carry_in(): pl.pallas_call(functools.partial(scan_kernel, peers, names), out_shape=ja...  72.4 us
    all_gather x1, waiting for transfers between devices, on_device(): message_all = lax.all_gather(message, 'grp', axis=0, tiled=True)  36.8 us
    convert_element_type x1, other arithmetic, on_device(): (local_all.astype(jnp.float32) + carry.reshape(local_all.shape)).astype(j...  11.4 us
    add x4, other arithmetic, advance(): return (decay[:, None, None] * state + digest_record, state)  8.81 us
    dot_general x1, matrix products, on_device(): jnp.einsum('kt,kd->td', mixed, out_weight, preferred_element_type=jnp.flo...  7.17 us
    unnamed x28, local copies, waits for them, and re-layouts  6.92 us
    dynamic_update_slice x4, other arithmetic, on_device(): lax.scan(advance, zero_state, (block_decay.T, summaries))  6.84 us
    dot_general x1, matrix products, on_device(): jnp.einsum('hcjn,hpcj->chnp', weighted_terms, channels, preferred_element...  5.6 us
  transfers between devices with their start and end apart: 2, of which 1 were waited for; matrix products, arithmetic and copies ran while one was open for 6% of the time, Pallas kernels for 32%

profile of v3, /device:TPU:1, one launch (start us, length us, event | category | flops | bytes accessed | tf_op | source)
XLA Modules:
  0.0 222.7 jit_solution(9285696263099699699)
XLA Ops:
  7.2 1.2 reshape.120
  8.4 1.6 fusion.20
  10.7 2.3 %reduce-window.6 = f32[10,4,2,128]{3,0,1,2:T(8,128)S(1)} reduce-window(f32[10,4,2,128]{3,0,1,2:T(8,128)S(1)} %copy.33, f32[]{:T(128)} %constant.22.clone.1), window={size=1x1x1x128 pad=0_0x0_0x0_0x127_0}, to_apply=%region_0.0 | reduce-window | flops 1300480 | bytes 81924 | tf_op jit(solution)/shard_map/reduce-window
  14.3 1.8 convert_element_type.48
  16.1 2.3 %fusion.23 = f32[4,256,256]{2,1,0:T(8,128)} fusion(bf16[4,256,128]{2,1,0:T(8,128)(2,1)} %bitcast.59, bf16[4,256,128]{2,1,0:T(8,128)(2,1)} %bitcast.63), kind=kOutput, calls=%fused_computation.46 | convolution fusion | flops 67108864 | bytes 1572864 | tf_op jit(solution)/shard_map/cin,cjn->cij/dot_general | solution.py:101
  18.4 3.8 %reshape.121 = bf16[10,64,4,256]{3,2,1,0:T(4,128)(2,1)} reshape(bf16[640,1024]{1,0:T(8,128)(2,1)} %param.9) | data formatting | bytes 2621440 | tf_op jit(solution)/shard_map/reshape | solution.py:95
  22.2 5.6 %fusion.9 = f32[4,10,128,64]{3,2,1,0:T(8,128)} fusion(f32[10,4,256]{2,0,1:T(8,128)S(1)} %copy.37, f32[4,256,128]{2,1,0:T(8,128)} %convert_element_type.48, bf16[10,64,4,256]{3,2,1,0:T(4,128)(2,1)} %reshape.121), kind=kOutput, calls=%fused_computation.16 | convolution fusion | flops 170393600 | bytes 3186688 | tf_op jit(solution)/shard_map/hcjn,hpcj->chnp/dot_general | solution.py:118
  27.8 15.7 %while.13 = (s32[]{:T(128)}, f32[10,128,64]{2,1,0:T(8,128)}, f32[4,10,128,64]{3,2,1,0:T(8,128)}, f32[4,10]{1,0:T(4,128)S(1)}, f32[4,10,128,64]{3,2,1,0:T(8,128)}, /*index=5*/s32[]{:T(128)}, s32[]{:T(128)}) while((s32[]{:T(128)}, f32[10,128,64]{2,1,0:T(8,128)}, f32[4,10,128,64]{3,2,1,0:T(8,128)}, f32[4,10]{1,0:T(4,128)S(1)}, ...), condition=%wide.region_3.4_spmd.clone, body=%wide.region_2.3_spmd.clone.sunk | while | flops 327683 | bytes 2293988 | solution.py:128
  28.7 2.1 bitcast_add_fusion.3
  30.8 2.0 bitcast_dynamic-update-slice_fusion.2
  32.8 2.3 %bitcast_add_fusion.3 = f32[10,128,64]{2,1,0:T(8,128)} fusion(f32[4,10,128,64]{3,2,1,0:T(8,128)} %get-tuple-element.137, s32[]{:T(128)S(6)} %copy.63, f32[10,128,64]{2,1,0:T(8,128)} %get-tuple-element.127, f32[10]{0:T(128)S(1)} %fusion.34, pred[]{:T(512)S(6)} %compare.3), kind=kLoop, calls=%fused_computation.1.clone.1 | loop fusion | flops 245760 | bytes 983085 | tf_op jit(solution)/shard_map/while/body/eval_jaxpr/add | solution.py:125
  35.0 2.0 bitcast_dynamic-update-slice_fusion.2
  37.0 2.3 %bitcast_add_fusion.3 = f32[10,128,64]{2,1,0:T(8,128)} fusion(f32[4,10,128,64]{3,2,1,0:T(8,128)} %get-tuple-element.137, s32[]{:T(128)S(6)} %copy.63, f32[10,128,64]{2,1,0:T(8,128)} %get-tuple-element.127, f32[10]{0:T(128)S(1)} %fusion.34, pred[]{:T(512)S(6)} %compare.3), kind=kLoop, calls=%fused_computation.1.clone.1 | loop fusion | flops 245760 | bytes 983085 | tf_op jit(solution)/shard_map/while/body/eval_jaxpr/add | solution.py:125
  39.3 2.0 bitcast_dynamic-update-slice_fusion.2
  41.2 2.3 %bitcast_add_fusion.3 = f32[10,128,64]{2,1,0:T(8,128)} fusion(f32[4,10,128,64]{3,2,1,0:T(8,128)} %get-tuple-element.137, s32[]{:T(128)S(6)} %copy.63, f32[10,128,64]{2,1,0:T(8,128)} %get-tuple-element.127, f32[10]{0:T(128)S(1)} %fusion.34, pred[]{:T(512)S(6)} %compare.3), kind=kLoop, calls=%fused_computation.1.clone.1 | loop fusion | flops 245760 | bytes 983085 | tf_op jit(solution)/shard_map/while/body/eval_jaxpr/add | solution.py:125
  43.5 4.9 %fusion.2 = f32[10,4,256,64]{2,3,1,0:T(8,128)S(1)} fusion(f32[10,4,256]{2,1,0:T(4,128)} %copy-done.9, f32[10,4,256]{2,1,0:T(4,128)} %copy-done.7, f32[4,256,256]{2,1,0:T(8,128)} %fusion.23, pred[256,256]{1,0:T(8,128)(4,1)} %iota_compare_fusion, bf16[10,64,4,256]{3,2,1,0:T(4,128)(2,1)} %reshape.121), kind=kOutput, calls=%fused_computation.8 | convolution fusion | flops 351272960 | bytes 5128192 | tf_op jit(solution)/shard_map/hcij,hpcj->hpci/dot_general | solution.py:113
  48.4 2.3 %fusion.24 = f32[4,10,64,256]{3,2,1,0:T(8,128)S(1)} fusion(f32[4,10,128,64]{3,2,1,0:T(8,128)S(1)} %copy-done.3, bf16[4,256,128,1]{2,1,3,0:T(8,128)(2,1)S(1)} %bitcast.60), kind=kOutput, calls=%fused_computation.47 | convolution fusion | flops 1006632960 | bytes 4194304 | tf_op jit(solution)/shard_map/cin,chnp->hpci/dot_general | solution.py:135
  50.8 4.5 %fusion.12.after_ref = bf16[10,64,4,256]{3,2,1,0:T(4,128)(2,1)S(1)} fusion(f32[4,10,64,256]{3,2,1,0:T(8,128)S(1)} %fusion.24, f32[10,4,256,64]{2,3,1,0:T(8,128)S(1)} %fusion.2, bf16[10,64,4,256]{3,2,1,0:T(4,128)(2,1)S(1)} %copy-done.2, f32[10]{0:T(128)S(1)} %copy-done.10, f32[10,4,256]{2,1,0:T(4,128)S(1)} %copy-done.8), kind=kLoop, calls=%fused_computation.20 | loop fusion | flops 3932160 | bytes 7905320 | tf_op jit(solution)/shard_map/convert_element_type | solution.py:138
  56.4 1.4 copy.52
  58.0 1.5 reshape.124
  59.5 1.4 reduce_window_sum.47
  64.0 2.0 reshape.122
  66.8 1.7 pad_maximum_fusion.msg_ref
  68.5 72.4 %shard_map.73 = f32[10,72,128]{2,1,0:T(8,128)} custom-call(f32[10,72,128]{2,1,0:T(8,128)} %pad_maximum_fusion.msg_ref, bf16[10,64,4,256]{3,2,1,0:T(4,128)(2,1)} %copy-done.1), custom_call_target="tpu_custom_call" | custom-call | bytes 188743680 | tf_op jit(solution)/shard_map/pallas_call | solution.py:71
  143.8 36.8 %all-gather.6.cloned.1.call-done = bf16[8,10,10240]{2,1,0:T(8,128)(2,1)} async-done(((bf16[1,10,10240]{2,1,0:T(8,128)(2,1)}), bf16[8,10,10240]{2,1,0:T(8,128)(2,1)}) %all-gather.6.cloned.1.call-update) | async-done | bytes 1638416 | tf_op jit(solution)/shard_map/all_gather | solution.py:148
  180.6 2.9 %reshape.129 = bf16[80,10240]{1,0:T(8,128)(2,1)} reshape(bf16[8,10,10240]{2,1,0:T(8,128)(2,1)} %all-gather.6.cloned.1.call-done) | data formatting | bytes 3276800
  183.5 1.8 convert_add_fusion
  185.3 2.5 %slice.34 = bf16[80,8192]{1,0:T(8,128)(2,1)} slice(bf16[80,10240]{1,0:T(8,128)(2,1)} %reshape.129), slice={[0:80], [0:8192]} | slice | bytes 2621440 | tf_op jit(solution)/shard_map/slice | solution.py:149
  187.8 4.8 %reshape.126 = bf16[80,128,64]{2,1,0:T(8,128)(2,1)} reshape(bf16[80,8192]{1,0:T(8,128)(2,1)} %slice.34) | data formatting | bytes 2621440 | tf_op jit(solution)/shard_map/reshape | solution.py:149
  192.6 4.7 %broadcast_multiply_fusion = f32[80,64,1024]{2,1,0:T(8,128)S(1)} fusion(f32[80,1024]{1,0:T(8,128)} %convert_add_fusion, bf16[80,128,64]{2,1,0:T(8,128)(2,1)} %reshape.126, bf16[1024,128]{1,0:T(8,128)(2,1)S(1)} %copy-done.4), kind=kOutput, calls=%fused_computation.6 | convolution fusion | flops 1347420160 | bytes 22872064 | tf_op jit(solution)/shard_map/tn,hnp->hpt/dot_general | solution.py:153
  197.3 11.4 %fusion.1 = bf16[5120,1024]{1,0:T(8,128)(2,1)} fusion(f32[80,64,1024]{2,1,0:T(8,128)S(1)} %broadcast_multiply_fusion, bf16[5120,1024]{1,0:T(8,128)(2,1)} %all-gather.4.cloned.1.call-done), kind=kLoop, calls=%fused_computation.5 | loop fusion | flops 15728640 | bytes 41943040 | tf_op jit(solution)/shard_map/convert_element_type | solution.py:156
  208.7 7.2 %convolution_convert_fusion = bf16[1024,320]{0,1:T(8,128)(2,1)} fusion(bf16[5120,320]{0,1:T(8,128)(2,1)S(1)} %copy-done, bf16[5120,1024]{1,0:T(8,128)(2,1)} %fusion.1), kind=kOutput, calls=%fused_computation.23 | convolution fusion | flops 3355770880 | bytes 14417920 | tf_op jit(solution)/shard_map/kt,kd->td/dot_general | solution.py:157
  (64 shorter events, 11.6 us)
Async XLA Ops:
  6.5 202.2 %copy-start = (bf16[5120,320]{0,1:T(8,128)(2,1)S(1)}, bf16[5120,320]{0,1:T(8,128)(2,1)}, u32[]{:S(2)}) copy-start(bf16[5120,320]{0,1:T(8,128)(2,1)} %param.15) | copy-start | bytes 9830404
  6.5 137.2 %all-gather.4.cloned.1.call-start = ((), (), s32[]{:S(2)}) async-start(), calls=%async_computation | async-start | bytes 11796480 | tf_op jit(solution)/shard_map/all_gather | solution.py:139
  8.4 13.8 %copy-start.9 = (f32[10,4,256]{2,1,0:T(4,128)}, f32[10,4,256]{2,1,0:T(4,128)S(1)}, u32[]{:S(2)}) copy-start(f32[10,4,256]{2,1,0:T(4,128)S(1)} %reshape.120) | copy-start | bytes 122884
  10.0 0.6 copy-start.5
  13.3 8.9 %copy-start.6 = (f32[10,4,2,128]{3,2,1,0:T(2,128)}, f32[10,4,2,128]{3,2,1,0:T(2,128)S(1)}, u32[]{:S(2)}) copy-start(f32[10,4,2,128]{3,2,1,0:T(2,128)S(1)} %copy.34) | copy-start | bytes 122884
  13.4 8.8 %copy-start.7 = (f32[10,4,256]{2,1,0:T(4,128)}, f32[10,4,256]{2,1,0:T(4,128)S(1)}, u32[]{:S(2)}) copy-start(f32[10,4,256]{2,1,0:T(4,128)S(1)} %reduce_window_sum.46) | copy-start | bytes 122884
  43.5 4.9 %copy-start.3 = (f32[4,10,128,64]{3,2,1,0:T(8,128)S(1)}, f32[4,10,128,64]{3,2,1,0:T(8,128)}, u32[]{:S(2)}) copy-start(f32[4,10,128,64]{3,2,1,0:T(8,128)} %get-tuple-element.36) | copy-start | bytes 3932164
  43.5 4.9 %copy-start.4 = (bf16[1024,128]{1,0:T(8,128)(2,1)S(1)}, bf16[1024,128]{1,0:T(8,128)(2,1)}, u32[]{:S(2)}) copy-start(bf16[1024,128]{1,0:T(8,128)(2,1)} %param.14) | copy-start | bytes 786436
  48.4 2.3 %copy-start.2 = (bf16[10,64,4,256]{3,2,1,0:T(4,128)(2,1)S(1)}, bf16[10,64,4,256]{3,2,1,0:T(4,128)(2,1)}, u32[]{:S(2)}) copy-start(bf16[10,64,4,256]{3,2,1,0:T(4,128)(2,1)} %reshape.121) | copy-start | bytes 3932164
  48.4 2.3 %copy-start.8 = (f32[10,4,256]{2,1,0:T(4,128)S(1)}, f32[10,4,256]{2,1,0:T(4,128)}, u32[]{:S(2)}) copy-start(f32[10,4,256]{2,1,0:T(4,128)} %get-tuple-element.86) | copy-start | bytes 122884
  48.4 2.3 %copy-start.10 = (f32[10]{0:T(128)S(1)}, f32[10]{0:T(128)}, u32[]{:S(2)}) copy-start(f32[10]{0:T(128)} %param.12) | copy-start | bytes 124
  55.3 1.1 copy-start.1
  57.8 122.8 %all-gather.6.cloned.1.call-start = ((), (), s32[]{:S(2)}) async-start(), calls=%async_computation.1 | async-start | bytes 2949120 | tf_op jit(solution)/shard_map/all_gather | solution.py:148
Sparse Core Ops, SparseCore 0:
  57.9 65.2 all-gather.3
  143.9 36.6 all-gather.5

commit v4 on v3

--- a/solution.py
+++ b/solution.py
@@ -111,24 +111,27 @@
         0.0,
     ).astype(jnp.bfloat16)
     inner = jnp.einsum("hcij,hpcj->hpci", mixing, channels, preferred_element_type=jnp.float32)
-    tail = jnp.exp(running[:, :, -1:] - running) * steps_blocked
-    weighted_terms = (basis_in_blocked.astype(jnp.float32)[None] * tail[:, :, :, None]).astype(
+    tail_decay = jnp.exp(running[:, :, -1:] - running) * steps_blocked
+    weighted_terms = (basis_in_blocked.astype(jnp.float32)[None] * tail_decay[:, :, :, None]).astype(
         jnp.bfloat16
     )
     summaries = jnp.einsum(
         "hcjn,hpcj->chnp", weighted_terms, channels, preferred_element_type=jnp.float32
     )
-    block_decay = jnp.exp(running[:, :, -1])
-
-    def advance(state, pair):
-        decay, digest_record = pair
-        return (decay[:, None, None] * state + digest_record, state)
-
-    zero_state = jnp.zeros((heads_here, N, HP), jnp.float32)
-    final_state, entering = lax.scan(advance, zero_state, (block_decay.T, summaries))
     block_sums = jnp.sum(log_decay, axis=2)
-    log_prefix = jnp.cumsum(block_sums, axis=1) - block_sums
-    total_log = jnp.sum(block_sums, axis=1)
+    block_cum = jnp.cumsum(block_sums, axis=1)
+    log_prefix = block_cum - block_sums
+    total_log = block_cum[:, -1]
+    entering = [jnp.zeros_like(summaries[0])]
+    for c in range(1, count + 1):
+        reach = log_prefix[:, c] if c < count else total_log
+        term = jnp.zeros_like(summaries[0])
+        for earlier in range(c):
+            weight = jnp.exp(reach - block_cum[:, earlier])
+            term = term + weight[:, None, None] * summaries[earlier]
+        entering.append(term)
+    final_state = entering[count]
+    entering = jnp.stack(entering[:count])
     basis_out_wide = basis_out_blocked.astype(jnp.float32)
     within = jnp.exp(running)[:, None]
     direct = skip_gain[:, None, None, None] * channels.astype(jnp.float32)
@@ -150,12 +153,62 @@
     scale_all = message_all[:, N * HP : N * HP + tokens_here].astype(jnp.float32) + message_all[
         :, N * HP + tokens_here :
     ].astype(jnp.float32)
-    carry = jnp.einsum(
-        "tn,hnp->hpt", output_basis, carried_all, preferred_element_type=jnp.float32
-    ) * scale_all[:, None, :]
-    mixed = (local_all.astype(jnp.float32) + carry.reshape(local_all.shape)).astype(jnp.bfloat16)
-    result = jnp.einsum("kt,kd->td", mixed, out_weight, preferred_element_type=jnp.float32)
-    return result.astype(jnp.bfloat16)
+    carried_t = jnp.swapaxes(carried_all, 1, 2)
+    result_t = tail(local_all, output_basis, carried_t, scale_all, out_weight.T)
+    return result_t.T
+
+
+def tail_kernel(local_ref, basis_ref, carried_ref, scale_ref, weight_ref, out_ref, acc_ref, mixed_ref):
+    g = pl.program_id(0)
+
+    @pl.when(g == 0)
+    def _():
+        acc_ref[...] = jnp.zeros_like(acc_ref)
+
+    basis = basis_ref[...]
+    for h in range(carried_ref.shape[0]):
+        rows = pl.ds(h * HP, HP)
+        carry = lax.dot_general(
+            carried_ref[h], basis, (((1,), (1,)), ((), ())), preferred_element_type=jnp.float32
+        )
+        mixed_ref[rows, :] = (
+            local_ref[rows, :].astype(jnp.float32) + carry * scale_ref[pl.ds(h, 1), :]
+        ).astype(jnp.bfloat16)
+    acc_ref[...] += jnp.dot(weight_ref[...], mixed_ref[...], preferred_element_type=jnp.float32)
+
+    @pl.when(g == pl.num_programs(0) - 1)
+    def _():
+        out_ref[...] = acc_ref[...].astype(out_ref.dtype)
+
+
+def tail(local_all, basis, carried_t, scale_all, weight_t):
+    channels, tokens = local_all.shape
+    features = weight_t.shape[0]
+    heads = carried_t.shape[0]
+    groups = lax.axis_size("grp")
+    per = heads // groups
+    return pl.pallas_call(
+        tail_kernel,
+        out_shape=jax.ShapeDtypeStruct((features, tokens), jnp.bfloat16),
+        grid=(groups,),
+        in_specs=[
+            pl.BlockSpec((per * HP, tokens), lambda g: (g, 0)),
+            pl.BlockSpec(basis.shape, lambda g: (0, 0)),
+            pl.BlockSpec((per, HP, N), lambda g: (g, 0, 0)),
+            pl.BlockSpec((None, per, tokens), lambda g: (g, 0, 0)),
+            pl.BlockSpec((features, per * HP), lambda g: (0, g)),
+        ],
+        out_specs=pl.BlockSpec((features, tokens), lambda g: (0, 0)),
+        scratch_shapes=[
+            pltpu.VMEM((features, tokens), jnp.float32),
+            pltpu.VMEM((per * HP, tokens), jnp.bfloat16),
+        ],
+        cost_estimate=pl.CostEstimate(
+            flops=2 * tokens * channels * (N + features),
+            transcendentals=0,
+            bytes_accessed=2 * (local_all.size + weight_t.size) + 2 * features * tokens,
+        ),
+    )(local_all, basis, carried_t, scale_all.reshape(groups, per, tokens), weight_t)
 
 
 def solution(mesh):

time: 224 us -> 183 us (0.82)
  other arithmetic: 46.8 us -> 14.7 us
  matrix products: 26.9 us -> 9.14 us
  Pallas kernels: 72.4 us -> 86 us
  local copies, waits for them, and re-layouts: 25.9 us -> 19.7 us
    pallas_call x0 -> x1, Pallas kernels: none -> 15.9 us  [tail(): pl.pallas_call(tail_kernel, out_shape=jax.ShapeDtypeStruct((features, tok...]
    dot_general x2 -> x0, matrix products: 11.9 us -> none  [the longest x1 7.17 us: on_device(): jnp.einsum('kt,kd->td', mixed, out_weight, preferred_element_type=jnp.flo...]
    convert_element_type x2 -> x1, other arithmetic: 13.2 us -> 1.78 us  [on_device(): basis_in_blocked.astype(jnp.float32)[None] * tail_decay[:, :, :, None]]
    add x4 -> x1, other arithmetic: 8.81 us -> 0.16 us  [on_device(): term = term + weight[:, None, None] * summaries[earlier]]
    dynamic_update_slice x4 -> x0, other arithmetic: 6.84 us -> none  [on_device(): lax.scan(advance, zero_state, (block_decay.T, summaries))]
    reshape x1, local copies, waits for them, and re-layouts: 3.77 us -> 1.01 us  [on_device(): channels = mixer_input.reshape(heads_here, HP, count, GROUP)]
    unnamed x28 -> x62, local copies, waits for them, and re-layouts: 6.92 us -> 4.38 us
    pallas_call x1, Pallas kernels: 72.4 us -> 70.1 us  [carry_in(): pl.pallas_call(functools.partial(scan_kernel, peers, names), out_shape=ja...]
  transfers between devices with their start and end apart: 2 -> 2, of which waited for: 1 -> 1; matrix products, arithmetic and copies ran while one was open for 6% -> 3% of each run, Pallas kernels for 32% -> 38%
where the time goes in v4:
time: 183 us
  Pallas kernels  86 us (47%)
  waiting for transfers between devices  39 us (21%)
  local copies, waits for them, and re-layouts  19.7 us (11%)
  other arithmetic  14.7 us (8%)
  between operations  14 us (8%)
  matrix products  9.14 us (5%)
    pallas_call x1, Pallas kernels, carry_in(): pl.pallas_call(functools.partial(scan_kernel, peers, names), out_shape=ja...  70.1 us
    all_gather x1, waiting for transfers between devices, on_device(): message_all = lax.all_gather(message, 'grp', axis=0, tiled=True)  38.9 us
    pallas_call x1, Pallas kernels, tail(): pl.pallas_call(tail_kernel, out_shape=jax.ShapeDtypeStruct((features, tok...  15.9 us
    reshape x2, local copies, waits for them, and re-layouts, on_device(): carried_all = message_all[:, :N * HP].reshape(-1, N, HP)  6.83 us
    convert_element_type x1, other arithmetic, on_device(): local = (inner + from_local * within + direct).astype(jnp.bfloat16)  4.53 us
    unnamed x62, local copies, waits for them, and re-layouts  4.38 us
    dot_general x1, matrix products, on_device(): jnp.einsum('hcjn,hpcj->chnp', weighted_terms, channels, preferred_element...  3.66 us
  transfers between devices with their start and end apart: 2, of which 1 were waited for; matrix products, arithmetic and copies ran while one was open for 3% of the time, Pallas kernels for 38%

profile of v4, /device:TPU:1, one launch (start us, length us, event | category | flops | bytes accessed | tf_op | source)
XLA Modules:
  0.0 182.8 jit_solution(10687173755664293496)
XLA Ops:
  6.5 0.6 iota_compare_fusion
  7.2 0.9 reshape.232
  8.1 0.9 fusion.28
  9.1 2.3 %reduce-window.6 = f32[10,4,2,128]{3,0,1,2:T(8,128)S(1)} reduce-window(f32[10,4,2,128]{3,0,1,2:T(8,128)S(1)} %copy.54, f32[]{:T(128)} %constant.8.clone.1), window={size=1x1x1x128 pad=0_0x0_0x0_0x127_0}, to_apply=%region_2.3 | reduce-window | flops 1300480 | bytes 81924 | tf_op jit(solution)/shard_map/reduce-window
  12.3 0.9 fusion.25
  13.2 0.6 fusion.29
  13.8 0.6 copy.58
  14.5 1.8 convert_element_type.39
  16.2 1.3 fusion.31
  17.5 1.0 reshape.233
  18.7 3.7 %fusion.7 = f32[4,10,128,64]{2,3,1,0:T(8,128)S(1)} fusion(f32[10,4,256]{2,0,1:T(8,128)S(1)} %copy-done.17, f32[4,256,128]{2,1,0:T(8,128)} %convert_element_type.39, bf16[10,64,4,256]{3,2,1,0:T(4,128)(2,1)S(1)} %reshape.233), kind=kOutput, calls=%fused_computation.9 | convolution fusion | flops 170393600 | bytes 3186688 | tf_op jit(solution)/shard_map/hcjn,hpcj->chnp/dot_general | solution.py:118
  22.4 2.9 %fusion = f32[10,4,256,64]{2,3,1,0:T(8,128)S(1)} fusion(f32[10,4,256]{2,1,0:T(4,128)S(1)} %copy-done.15, f32[10,4,256]{2,1,0:T(4,128)S(1)} %copy-done.12, f32[4,256,256]{2,1,0:T(8,128)S(1)} %copy-done.4, pred[256,256]{1,0:T(8,128)(4,1)S(1)} %copy-done.16, bf16[10,64,4,256]{3,2,1,0:T(4,128)(2,1)S(1)} %reshape.233), kind=kOutput, calls=%fused_computation.1 | convolution fusion | flops 351272960 | bytes 5128192 | tf_op jit(solution)/shard_map/hcij,hpcj->hpci/dot_general | solution.py:113
  25.4 1.0 broadcast_multiply_fusion
  26.4 1.3 fusion.13
  27.7 4.5 %fusion.10.after_ref = bf16[10,64,4,256]{3,2,1,0:T(4,128)(2,1)S(1)} fusion(f32[4,10,64,256]{3,2,1,0:T(8,128)S(1)} %fusion.13, f32[10,4,256,64]{2,3,1,0:T(8,128)S(1)} %fusion, bf16[10,64,4,256]{3,2,1,0:T(4,128)(2,1)S(1)} %reshape.233, f32[10]{0:T(128)S(1)} %copy-done.27, f32[10,4,256]{2,1,0:T(4,128)S(1)} %copy-done.13), kind=kLoop, calls=%fused_computation.13 | loop fusion | flops 3932160 | bytes 7905320 | tf_op jit(solution)/shard_map/convert_element_type | solution.py:141
  32.3 1.4 copy.72
  33.9 0.7 reduce_window_sum.48
  34.6 0.7 copy.71
  35.7 0.2 copy.62
  36.1 0.2 copy.61
  36.5 0.2 copy.60
  37.2 0.8 pad_maximum_fusion.msg_ref
  38.0 70.1 %shard_map.73 = f32[10,72,128]{2,1,0:T(8,128)} custom-call(f32[10,72,128]{2,1,0:T(8,128)} %pad_maximum_fusion.msg_ref, bf16[10,64,4,256]{3,2,1,0:T(4,128)(2,1)} %copy-done), custom_call_target="tpu_custom_call" | custom-call | bytes 188743680 | tf_op jit(solution)/shard_map/pallas_call | solution.py:71
  108.1 1.0 slice.138
  109.3 0.8 pad_maximum_fusion.1
  110.1 38.9 %all-gather.6.cloned.1.call-done = bf16[8,10,10240]{2,1,0:T(8,128)(2,1)} async-done(((bf16[1,10,10240]{2,1,0:T(8,128)(2,1)}), bf16[8,10,10240]{2,1,0:T(8,128)(2,1)}) %all-gather.6.cloned.1.call-update) | async-done | bytes 1638416 | tf_op jit(solution)/shard_map/all_gather | solution.py:151
  149.1 2.0 %reshape.239 = bf16[80,10240]{1,0:T(8,128)(2,1)S(1)} reshape(bf16[8,10,10240]{2,1,0:T(8,128)(2,1)} %all-gather.6.cloned.1.call-done) | data formatting | bytes 3276800
  151.2 1.2 slice.101
  152.3 0.8 reshape.237.scale_ref
  153.2 3.8 %reshape.236 = bf16[80,128,64]{2,1,0:T(8,128)(2,1)S(1)} reshape(bf16[80,8192]{1,0:T(8,128)(2,1)} %slice.101) | data formatting | bytes 2621440 | tf_op jit(solution)/shard_map/reshape | solution.py:152
  157.0 3.0 %copy.68 = bf16[80,128,64]{1,2,0:T(8,128)(2,1)} copy(bf16[80,128,64]{2,1,0:T(8,128)(2,1)S(1)} %reshape.236) | data formatting | bytes 2621440 | tf_op jit(solution)/shard_map/reshape | solution.py:152
  160.0 15.9 %shard_map.74 = bf16[320,1024]{1,0:T(8,128)(2,1)} custom-call(bf16[5120,1024]{1,0:T(8,128)(2,1)} %all-gather.4.cloned.1.call-done.local_ref, bf16[1024,128]{1,0:T(8,128)(2,1)} %basis_ref.1, bf16[80,64,128]{2,1,0:T(8,128)(2,1)} %bitcast.46, f32[8,10,1024]{2,1,0:T(8,128)} %reshape.237.scale_ref, bf16[320,5120]{1,0:T(8,128)(2,1)} %bitcast.56), custom_call_target="tpu_custom_call" | custom-call | flops 4697620480 | bytes 14417920 | tf_op jit(solution)/shard_map/pallas_call | solution.py:190
  (91 shorter events, 2.7 us)
Async XLA Ops:
  6.5 9.7 %copy-start.5 = (bf16[1024,128]{1,0:T(8,128)(2,1)S(1)}, bf16[1024,128]{1,0:T(8,128)(2,1)}, u32[]{:S(2)}) copy-start(bf16[1024,128]{1,0:T(8,128)(2,1)} %param.11) | copy-start | bytes 786436
  6.5 9.7 %copy-start.6 = (bf16[1024,128]{1,0:T(8,128)(2,1)S(1)}, bf16[1024,128]{1,0:T(8,128)(2,1)}, u32[]{:S(2)}) copy-start(bf16[1024,128]{1,0:T(8,128)(2,1)} %basis_ref.1) | copy-start | bytes 786436
  6.5 11.0 %copy-start.1 = (bf16[640,1024]{1,0:T(8,128)(2,1)S(1)}, bf16[640,1024]{1,0:T(8,128)(2,1)}, u32[]{:S(2)}) copy-start(bf16[640,1024]{1,0:T(8,128)(2,1)} %param.7) | copy-start | bytes 3932164
  6.5 103.5 %all-gather.4.cloned.1.call-start = ((), (), s32[]{:S(2)}) async-start(), calls=%async_computation | async-start | bytes 11796480 | tf_op jit(solution)/shard_map/all_gather | solution.py:142
  8.0 10.5 %copy-start.14 = (f32[10,4,256]{2,1,0:T(4,128)}, f32[10,4,256]{2,1,0:T(4,128)S(1)}, u32[]{:S(2)}) copy-start(f32[10,4,256]{2,1,0:T(4,128)S(1)} %reshape.232) | copy-start | bytes 122884
  11.7 6.9 %copy-start.7 = (f32[10,4,2,128]{3,2,1,0:T(2,128)}, f32[10,4,2,128]{3,2,1,0:T(2,128)S(1)}, u32[]{:S(2)}) copy-start(f32[10,4,2,128]{3,2,1,0:T(2,128)S(1)} %copy.55) | copy-start | bytes 122884
  11.7 6.8 %copy-start.11 = (f32[10,4,256]{2,1,0:T(4,128)}, f32[10,4,256]{2,1,0:T(4,128)S(1)}, u32[]{:S(2)}) copy-start(f32[10,4,256]{2,1,0:T(4,128)S(1)} %reduce_window_sum.47) | copy-start | bytes 122884
  17.5 1.1 copy-start.17
  18.6 3.7 %copy-start.4 = (f32[4,256,256]{2,1,0:T(8,128)S(1)}, f32[4,256,256]{2,1,0:T(8,128)}, u32[]{:S(2)}) copy-start(f32[4,256,256]{2,1,0:T(8,128)} %fusion.31) | copy-start | bytes 3145732
  18.6 3.7 %copy-start.16 = (pred[256,256]{1,0:T(8,128)(4,1)S(1)}, pred[256,256]{1,0:T(8,128)(4,1)}, u32[]{:S(2)}) copy-start(pred[256,256]{1,0:T(8,128)(4,1)} %iota_compare_fusion) | copy-start | bytes 196612
  18.6 3.7 %copy-start.12 = (f32[10,4,256]{2,1,0:T(4,128)S(1)}, f32[10,4,256]{2,1,0:T(4,128)}, u32[]{:S(2)}) copy-start(f32[10,4,256]{2,1,0:T(4,128)} %copy-done.11) | copy-start | bytes 122884
  18.6 3.7 %copy-start.15 = (f32[10,4,256]{2,1,0:T(4,128)S(1)}, f32[10,4,256]{2,1,0:T(4,128)}, u32[]{:S(2)}) copy-start(f32[10,4,256]{2,1,0:T(4,128)} %copy-done.14) | copy-start | bytes 122884
  22.4 3.0 %copy-start.21 = (f32[10]{0:T(128)S(1)}, f32[10]{0:T(128)}, u32[]{:S(2)}) copy-start(f32[10]{0:T(128)} %get-tuple-element.9) | copy-start | bytes 124
  22.4 3.0 %copy-start.22 = (f32[10]{0:T(128)S(1)}, f32[10]{0:T(128)}, u32[]{:S(2)}) copy-start(f32[10]{0:T(128)} %get-tuple-element.10) | copy-start | bytes 124
  22.4 3.0 %copy-start.23 = (f32[10]{0:T(128)S(1)}, f32[10]{0:T(128)}, u32[]{:S(2)}) copy-start(f32[10]{0:T(128)} %get-tuple-element.11) | copy-start | bytes 124
  22.4 3.0 %copy-start.24 = (f32[10]{0:T(128)S(1)}, f32[10]{0:T(128)}, u32[]{:S(2)}) copy-start(f32[10]{0:T(128)} %get-tuple-element.12) | copy-start | bytes 124
  22.4 3.0 %copy-start.25 = (f32[10]{0:T(128)S(1)}, f32[10]{0:T(128)}, u32[]{:S(2)}) copy-start(f32[10]{0:T(128)} %get-tuple-element.13) | copy-start | bytes 124
  22.4 3.0 %copy-start.26 = (f32[10]{0:T(128)S(1)}, f32[10]{0:T(128)}, u32[]{:S(2)}) copy-start(f32[10]{0:T(128)} %get-tuple-element.14) | copy-start | bytes 124
  26.4 1.3 copy-start.13
  26.4 1.3 copy-start.27
  32.2 3.3 %copy-start = (bf16[10,64,4,256]{3,2,1,0:T(4,128)(2,1)}, bf16[10,64,4,256]{3,2,1,0:T(4,128)(2,1)S(1)}, u32[]{:S(2)}) copy-start(bf16[10,64,4,256]{3,2,1,0:T(4,128)(2,1)S(1)} %fusion.10.after_ref) | copy-start | bytes 3932164
  32.2 1.6 copy-start.8
  32.2 3.1 %copy-start.3 = (f32[1,10,128,64]{2,3,1,0:T(8,128)S(1)}, f32[1,10,128,64]{2,3,1,0:T(8,128)}, u32[]{:S(2)}) copy-start(f32[1,10,128,64]{2,3,1,0:T(8,128)} %get-tuple-element.24) | copy-start | bytes 983044
  32.3 3.5 %copy-start.2 = (f32[1,10,128,64]{2,3,1,0:T(8,128)S(1)}, f32[1,10,128,64]{2,3,1,0:T(8,128)}, u32[]{:S(2)}) copy-start(f32[1,10,128,64]{2,3,1,0:T(8,128)} %get-tuple-element.25) | copy-start | bytes 983044
  33.6 115.4 %all-gather.6.cloned.1.call-start = ((), (), s32[]{:S(2)}) async-start(), calls=%async_computation.1 | async-start | bytes 2949120 | tf_op jit(solution)/shard_map/all_gather | solution.py:151
  36.0 1.0 copy-start.18
  36.0 1.0 copy-start.19
  36.1 1.0 copy-start.20
  37.0 72.3 %copy-start.9 = (f32[2,8,4,256]{3,1,2,0:T(8,128)S(1)}, f32[2,8,4,256]{3,1,2,0:T(8,128)}, u32[]{:S(2)}) copy-start(f32[2,8,4,256]{3,1,2,0:T(8,128)} %copy.71) | copy-start | bytes 196612
  37.0 72.3 %copy-start.10 = (f32[10,1024]{1,0:T(8,128)S(1)}, f32[10,1024]{1,0:T(8,128)}, u32[]{:S(2)}) copy-start(f32[10,1024]{1,0:T(8,128)} %reduce_window_sum.48) | copy-start | bytes 122884
Sparse Core Ops, SparseCore 0:
  33.8 65.2 all-gather.3
  110.2 38.7 all-gather.5

commit v5 on v4

--- a/solution.py
+++ b/solution.py
@@ -12,22 +12,29 @@
 GROUP = 256
 
 
-def scan_kernel(peers, names, msg_ref, after_ref, out_ref, inc_ref, recv_ref, send_sem, recv_sem):
+def scan_kernel(peers, names, msg_ref, after_ref, out_ref, spread_ref, inc_ref, recv_ref, send_ref,
+                send_sem, recv_sem, spread_send, spread_recv):
     here = lax.axis_index("seq")
     grp_here = lax.axis_index("grp")
+    groups = spread_ref.shape[0]
     rows = msg_ref.shape[1] - 8
 
-    def device(target):
-        return tuple(target if name == "seq" else grp_here for name in names)
+    def device(seq_at, grp_at):
+        return tuple(seq_at if name == "seq" else grp_at for name in names)
 
     offsets = sorted({d % peers for d in _hops(peers)} | {(-d) % peers for d in _hops(peers)})
     barrier = pltpu.get_barrier_semaphore()
     for offset in offsets:
         pl.semaphore_signal(
-            barrier, inc=1, device_id=device(lax.rem(here + offset, peers)),
-            device_id_type=pl.DeviceIdType.MESH,
-        )
-    pl.semaphore_wait(barrier, len(offsets))
+            barrier, inc=1, device_id=device(lax.rem(here + offset, peers), grp_here),
+            device_id_type=pl.DeviceIdType.MESH,
+        )
+    for offset in range(1, groups):
+        pl.semaphore_signal(
+            barrier, inc=1, device_id=device(here, lax.rem(grp_here + offset, groups)),
+            device_id_type=pl.DeviceIdType.MESH,
+        )
+    pl.semaphore_wait(barrier, len(offsets) + groups - 1)
 
     inc_ref[...] = msg_ref[...]
     out_ref[:, :rows] = jnp.zeros((out_ref.shape[0], rows, out_ref.shape[2]), jnp.float32)
@@ -38,7 +45,7 @@
             dst_ref=recv_ref.at[r],
             send_sem=send_sem.at[r],
             recv_sem=recv_sem.at[r],
-            device_id=device(lax.rem(here + d, peers)),
+            device_id=device(lax.rem(here + d, peers), grp_here),
             device_id_type=pl.DeviceIdType.MESH,
         )
         copy.start()
@@ -51,6 +58,33 @@
             ref[:, :rows] = jnp.where(reached, decay * got_state + ref[:, :rows], ref[:, :rows])
             ref[:, rows:] = jnp.where(reached, decay * got_decay, ref[:, rows:])
 
+    send_ref[...] = out_ref[:, :rows].astype(send_ref.dtype)
+    spread_ref[grp_here] = out_ref[:, :rows].astype(spread_ref.dtype)
+    copies = []
+    for offset in range(1, groups):
+        copy = pltpu.make_async_remote_copy(
+            src_ref=send_ref,
+            dst_ref=spread_ref.at[grp_here],
+            send_sem=spread_send.at[offset],
+            recv_sem=spread_recv.at[grp_here],
+            device_id=device(here, lax.rem(grp_here + offset, groups)),
+            device_id_type=pl.DeviceIdType.MESH,
+        )
+        copy.start()
+        copies.append(copy)
+    for copy in copies:
+        copy.wait_send()
+    for offset in range(1, groups):
+        source = lax.rem(grp_here + groups - offset, groups)
+        pltpu.make_async_remote_copy(
+            src_ref=send_ref,
+            dst_ref=spread_ref.at[source],
+            send_sem=spread_send.at[offset],
+            recv_sem=spread_recv.at[source],
+            device_id=device(here, source),
+            device_id_type=pl.DeviceIdType.MESH,
+        ).wait_recv()
+
 
 def _hops(peers):
     d, hops = 1, []
@@ -60,29 +94,35 @@
     return hops
 
 
-def carry_in(total_log, final_state, names, after):
+def carry_in(total_log, state_t, names, after):
     peers = lax.axis_size("seq")
-    heads = final_state.shape[0]
-    rows = N * HP // 128
-    state = final_state.reshape(heads, rows, 128)
-    decay = jnp.broadcast_to(jnp.exp(total_log)[:, None, None], (heads, 8, 128))
-    msg = jnp.concatenate([state, decay], axis=1)
+    groups = lax.axis_size("grp")
+    heads, rows, lanes = state_t.shape
+    decay = jnp.broadcast_to(jnp.exp(total_log)[:, None, None], (heads, 8, lanes))
+    msg = jnp.concatenate([state_t, decay], axis=1)
     shape = msg.shape
-    out = pl.pallas_call(
+    hops = len(_hops(peers))
+    _, spread = pl.pallas_call(
         functools.partial(scan_kernel, peers, names),
-        out_shape=jax.ShapeDtypeStruct(shape, jnp.float32),
+        out_shape=(
+            jax.ShapeDtypeStruct(shape, jnp.float32),
+            jax.ShapeDtypeStruct((groups, heads, rows, lanes), jnp.bfloat16),
+        ),
         in_specs=[pl.BlockSpec(memory_space=pltpu.VMEM), pl.BlockSpec(memory_space=pl.ANY)],
-        out_specs=pl.BlockSpec(memory_space=pltpu.VMEM),
+        out_specs=(pl.BlockSpec(memory_space=pltpu.VMEM), pl.BlockSpec(memory_space=pltpu.VMEM)),
         scratch_shapes=[
             pltpu.VMEM(shape, jnp.float32),
-            pltpu.VMEM((len(_hops(peers)),) + shape, jnp.float32),
-            pltpu.SemaphoreType.DMA((len(_hops(peers)),)),
-            pltpu.SemaphoreType.DMA((len(_hops(peers)),)),
+            pltpu.VMEM((hops,) + shape, jnp.float32),
+            pltpu.VMEM((heads, rows, lanes), jnp.bfloat16),
+            pltpu.SemaphoreType.DMA((hops,)),
+            pltpu.SemaphoreType.DMA((hops,)),
+            pltpu.SemaphoreType.DMA((groups,)),
+            pltpu.SemaphoreType.DMA((groups,)),
         ],
         compiler_params=pltpu.CompilerParams(collective_id=0, has_side_effects=True),
         cost_estimate=pl.CostEstimate(flops=0, transcendentals=0, bytes_accessed=512 * msg.size * 4),
     )(msg, after)
-    return out[:, :rows].reshape(heads, N, HP)
+    return spread.reshape(groups * heads, rows, lanes)
 
 
 def on_device(
@@ -139,26 +179,26 @@
         "cin,chnp->hpci", basis_out_wide, entering, precision=lax.Precision.HIGHEST
     )
     local = (inner + from_local * within + direct).astype(jnp.bfloat16)
-    local_all = lax.all_gather(local.reshape(heads_here * HP, tokens_here), "grp", axis=0, tiled=True)
-    carried = carry_in(total_log, final_state, names, local)
     scale = jnp.exp(running + log_prefix[:, :, None]).reshape(heads_here, tokens_here)
     scale_hi = scale.astype(jnp.bfloat16)
     scale_lo = (scale - scale_hi.astype(jnp.float32)).astype(jnp.bfloat16)
-    message = jnp.concatenate(
-        [carried.reshape(heads_here, N * HP).astype(jnp.bfloat16), scale_hi, scale_lo], axis=1
-    )
-    message, local_all = lax.optimization_barrier((message, local_all))
-    message_all = lax.all_gather(message, "grp", axis=0, tiled=True)
-    carried_all = message_all[:, : N * HP].reshape(-1, N, HP)
-    scale_all = message_all[:, N * HP : N * HP + tokens_here].astype(jnp.float32) + message_all[
-        :, N * HP + tokens_here :
-    ].astype(jnp.float32)
-    carried_t = jnp.swapaxes(carried_all, 1, 2)
-    result_t = tail(local_all, output_basis, carried_t, scale_all, out_weight.T)
+    extra = 32 - 2 * heads_here
+    local_ext = jnp.concatenate(
+        [
+            local.reshape(heads_here * HP, tokens_here),
+            scale_hi,
+            scale_lo,
+            jnp.zeros((extra, tokens_here), jnp.bfloat16),
+        ],
+        axis=0,
+    )
+    local_all = lax.all_gather(local_ext, "grp", axis=0, tiled=True)
+    carried_t = carry_in(total_log, jnp.swapaxes(final_state, 1, 2), names, local_ext)
+    result_t = tail(local_all, output_basis, carried_t, out_weight.T)
     return result_t.T
 
 
-def tail_kernel(local_ref, basis_ref, carried_ref, scale_ref, weight_ref, out_ref, acc_ref, mixed_ref):
+def tail_kernel(local_ref, basis_ref, carried_ref, weight_ref, out_ref, acc_ref, mixed_ref):
     g = pl.program_id(0)
 
     @pl.when(g == 0)
@@ -166,13 +206,20 @@
         acc_ref[...] = jnp.zeros_like(acc_ref)
 
     basis = basis_ref[...]
-    for h in range(carried_ref.shape[0]):
+    per = carried_ref.shape[0]
+    base = per * HP
+    for h in range(per):
         rows = pl.ds(h * HP, HP)
         carry = lax.dot_general(
             carried_ref[h], basis, (((1,), (1,)), ((), ())), preferred_element_type=jnp.float32
         )
         mixed_ref[rows, :] = (
-            local_ref[rows, :].astype(jnp.float32) + carry * scale_ref[pl.ds(h, 1), :]
+            local_ref[rows, :].astype(jnp.float32)
+            + carry
+            * (
+                local_ref[pl.ds(base + h, 1), :].astype(jnp.float32)
+                + local_ref[pl.ds(base + per + h, 1), :].astype(jnp.float32)
+            )
         ).astype(jnp.bfloat16)
     acc_ref[...] += jnp.dot(weight_ref[...], mixed_ref[...], preferred_element_type=jnp.float32)
 
@@ -181,7 +228,7 @@
         out_ref[...] = acc_ref[...].astype(out_ref.dtype)
 
 
-def tail(local_all, basis, carried_t, scale_all, weight_t):
+def tail(local_all, basis, carried_t, weight_t):
     channels, tokens = local_all.shape
     features = weight_t.shape[0]
     heads = carried_t.shape[0]
@@ -192,10 +239,9 @@
         out_shape=jax.ShapeDtypeStruct((features, tokens), jnp.bfloat16),
         grid=(groups,),
         in_specs=[
-            pl.BlockSpec((per * HP, tokens), lambda g: (g, 0)),
+            pl.BlockSpec((channels // groups, tokens), lambda g: (g, 0)),
             pl.BlockSpec(basis.shape, lambda g: (0, 0)),
             pl.BlockSpec((per, HP, N), lambda g: (g, 0, 0)),
-            pl.BlockSpec((None, per, tokens), lambda g: (g, 0, 0)),
             pl.BlockSpec((features, per * HP), lambda g: (0, g)),
         ],
         out_specs=pl.BlockSpec((features, tokens), lambda g: (0, 0)),
@@ -204,11 +250,11 @@
             pltpu.VMEM((per * HP, tokens), jnp.bfloat16),
         ],
         cost_estimate=pl.CostEstimate(
-            flops=2 * tokens * channels * (N + features),
+            flops=2 * tokens * per * HP * groups * (N + features),
             transcendentals=0,
             bytes_accessed=2 * (local_all.size + weight_t.size) + 2 * features * tokens,
         ),
-    )(local_all, basis, carried_t, scale_all.reshape(groups, per, tokens), weight_t)
+    )(local_all, basis, carried_t, weight_t)
 
 
 def solution(mesh):

time: 183 us -> 150 us (0.82)
  the two profiles are of different devices: /device:TPU:1 before, /device:TPU:209 now
where the time goes in v5:
time: 150 us; the launch traced here: 149 us
  Pallas kernels  112 us (75%)
  between operations  13.7 us (9%)
  matrix products  8.76 us (6%)
  other arithmetic  8.28 us (6%)
  local copies, waits for them, and re-layouts  6.67 us (4%)
    pallas_call x1, Pallas kernels, carry_in(): pl.pallas_call(functools.partial(scan_kernel, peers, names), out_shape=(j...  96.1 us
    pallas_call x1, Pallas kernels, tail(): pl.pallas_call(tail_kernel, out_shape=jax.ShapeDtypeStruct((features, tok...  15.7 us
    dot_general x1, matrix products, on_device(): jnp.einsum('hcij,hpcj->hpci', mixing, channels, preferred_element_type=jn...  4 us
    dot_general x1, matrix products, on_device(): jnp.einsum('hcjn,hpcj->chnp', weighted_terms, channels, preferred_element...  3.2 us
  transfers between devices with their start and end apart: 1, of which 0 were waited for; matrix products, arithmetic and copies ran while one was open for 1% of the time, Pallas kernels for 64%

profile of v5, /device:TPU:209, one launch (start us, length us, event | category | flops | bytes accessed | tf_op | source)
XLA Modules:
  0.0 149.3 jit_solution(1624231782264689012)
XLA Ops:
  6.5 0.6 iota_compare_fusion
  7.2 0.9 mul.152
  8.1 0.9 fusion.26
  9.1 2.3 %reduce-window.6 = f32[10,4,2,128]{3,0,1,2:T(8,128)S(1)} reduce-window(f32[10,4,2,128]{3,0,1,2:T(8,128)S(1)} %copy.42, f32[]{:T(128)} %constant.5.clone.1), window={size=1x1x1x128 pad=0_0x0_0x0_0x127_0}, to_apply=%region_0.0 | reduce-window | flops 1300480 | bytes 81924 | tf_op jit(solution)/shard_map/reduce-window
  11.4 0.2 slice_reduce_fusion
  11.6 0.1 broadcast_add_fusion
  11.8 0.1 slice.73
  11.9 0.1 copy.45
  12.0 0.1 copy.46
  12.1 0.6 fusion.27
  12.7 0.6 copy.47
  13.4 2.9 %reshape.221 = bf16[10,64,4,256]{3,2,1,0:T(4,128)(2,1)S(1)} reshape(bf16[640,1024]{1,0:T(8,128)(2,1)} %param.7) | data formatting | bytes 2621440 | tf_op jit(solution)/shard_map/reshape | solution.py:135
  16.3 0.1 reduce_sum.9
  16.4 0.2 reduce_window_sum.47
  16.6 0.9 exponential_reduce_fusion.4
  17.5 0.3 fusion.29
  17.8 3.2 %fusion.7 = f32[4,10,128,64]{2,3,1,0:T(8,128)S(1)} fusion(f32[10,4,256]{2,0,1:T(8,128)} %copy.47, f32[4,256,128]{2,1,0:T(8,128)S(1)} %convert_element_type.30, bf16[10,64,4,256]{3,2,1,0:T(4,128)(2,1)S(1)} %reshape.221), kind=kOutput, calls=%fused_computation.9 | convolution fusion | flops 170393600 | bytes 3186688 | tf_op jit(solution)/shard_map/hcjn,hpcj->chnp/dot_general | solution.py:158
  21.0 0.2 slice_multiply_fusion
  21.2 1.3 fusion.13
  22.5 4.0 %fusion.10 = bf16[10,64,4,256]{3,1,2,0:T(8,128)(2,1)S(1)} fusion(f32[4,10,64,256]{3,2,0,1:T(8,128)S(1)} %fusion.13, f32[10,4,256]{2,1,0:T(4,128)S(1)} %mul.152, f32[10,4,256]{2,1,0:T(4,128)S(1)} %reduce_window_sum.46, f32[4,256,256]{2,1,0:T(8,128)S(1)} %fusion.29, pred[256,256]{1,0:T(8,128)(4,1)S(1)} %copy-done.2, ...), kind=kOutput, calls=%fused_computation.13 | convolution fusion | flops 355205120 | bytes 6479912 | tf_op jit(solution)/shard_map/hcij,hpcj->hpci/dot_general | solution.py:153
  26.6 1.0 copy.51
  27.6 0.3 copy.53
  27.9 0.1 add.43
  28.1 0.1 pad.5.clone
  28.1 1.4 maximum_maximum_fusion.after_ref
  29.5 0.0 all-gather.2.cloned.1.call-update
  29.6 0.2 fusion.19
  29.8 0.1 broadcast_in_dim.19
  29.8 0.8 pad_maximum_fusion.1.msg_ref
  30.6 96.1 %shard_map.73 = (f32[10,72,128]{2,1,0:T(8,128)}, bf16[8,10,64,128]{3,2,1,0:T(8,128)(2,1)}) custom-call(f32[10,72,128]{2,1,0:T(8,128)} %pad_maximum_fusion.1.msg_ref, bf16[672,1024]{1,0:T(8,128)(2,1)} %maximum_maximum_fusion.after_ref), custom_call_target="tpu_custom_call" | custom-call | bytes 188743680 | tf_op jit(solution)/shard_map/pallas_call | solution.py:105
  126.7 0.0 all-gather.2.cloned.1.call-done.local_ref
  126.8 15.7 %shard_map.74 = bf16[320,1024]{1,0:T(8,128)(2,1)} custom-call(bf16[5376,1024]{1,0:T(8,128)(2,1)} %all-gather.2.cloned.1.call-done.local_ref, bf16[1024,128]{1,0:T(8,128)(2,1)} %basis_ref.1, bf16[80,64,128]{2,1,0:T(8,128)(2,1)} %bitcast.65, bf16[320,5120]{1,0:T(8,128)(2,1)} %bitcast.64), custom_call_target="tpu_custom_call" | custom-call | flops 4697620480 | bytes 14942208 | tf_op jit(solution)/shard_map/pallas_call | solution.py:237
  (37 shorter events, 0.3 us)
Async XLA Ops:
  6.5 9.7 %copy-start = (bf16[1024,128]{1,0:T(8,128)(2,1)S(1)}, bf16[1024,128]{1,0:T(8,128)(2,1)}, u32[]{:S(2)}) copy-start(bf16[1024,128]{1,0:T(8,128)(2,1)} %param.11) | copy-start | bytes 786436
  6.5 120.2 %all-gather.2.cloned.1.call-start = ((), (), s32[]{:S(2)}) async-start(), calls=%async_computation | async-start | bytes 12386304 | tf_op jit(solution)/shard_map/all_gather | solution.py:195
  7.2 10.3 %copy-start.1 = (bf16[1024,128]{1,0:T(8,128)(2,1)S(1)}, bf16[1024,128]{1,0:T(8,128)(2,1)}, u32[]{:S(2)}) copy-start(bf16[1024,128]{1,0:T(8,128)(2,1)} %basis_ref.1) | copy-start | bytes 786436
  21.0 1.5 %copy-start.2 = (pred[256,256]{1,0:T(8,128)(4,1)S(1)}, pred[256,256]{1,0:T(8,128)(4,1)}, u32[]{:S(2)}) copy-start(pred[256,256]{1,0:T(8,128)(4,1)} %iota_compare_fusion) | copy-start | bytes 196612
  21.0 1.5 %copy-start.3 = (f32[10,4,256]{2,1,0:T(4,128)S(1)}, f32[10,4,256]{2,1,0:T(4,128)}, u32[]{:S(2)}) copy-start(f32[10,4,256]{2,1,0:T(4,128)} %get-tuple-element.25) | copy-start | bytes 122884
  21.0 1.5 %copy-start.9 = (f32[10]{0:T(128)S(1)}, f32[10]{0:T(128)}, u32[]{:S(2)}) copy-start(f32[10]{0:T(128)} %param.10) | copy-start | bytes 124
  27.9 1.7 %copy-start.4 = (f32[10]{0:T(128)S(1)}, f32[10]{0:T(128)}, u32[]{:S(2)}) copy-start(f32[10]{0:T(128)} %get-tuple-element.13) | copy-start | bytes 124
  27.9 1.7 %copy-start.5 = (f32[10]{0:T(128)S(1)}, f32[10]{0:T(128)}, u32[]{:S(2)}) copy-start(f32[10]{0:T(128)} %get-tuple-element.15) | copy-start | bytes 124
  27.9 1.7 %copy-start.6 = (f32[10]{0:T(128)S(1)}, f32[10]{0:T(128)}, u32[]{:S(2)}) copy-start(f32[10]{0:T(128)} %get-tuple-element.16) | copy-start | bytes 124
  27.9 1.7 %copy-start.7 = (f32[10]{0:T(128)S(1)}, f32[10]{0:T(128)}, u32[]{:S(2)}) copy-start(f32[10]{0:T(128)} %get-tuple-element.17) | copy-start | bytes 124
  28.1 1.6 %copy-start.8 = (f32[10]{0:T(128)S(1)}, f32[10]{0:T(128)}, u32[]{:S(2)}) copy-start(f32[10]{0:T(128)} %get-tuple-element.14) | copy-start | bytes 124
Sparse Core Ops, SparseCore 0:
  29.6 64.2 all-gather.1

commit v6 on v5

--- a/solution.py
+++ b/solution.py
@@ -17,7 +17,7 @@
     here = lax.axis_index("seq")
     grp_here = lax.axis_index("grp")
     groups = spread_ref.shape[0]
-    rows = msg_ref.shape[1] - 8
+    rows = msg_ref.shape[0] - 8
 
     def device(seq_at, grp_at):
         return tuple(seq_at if name == "seq" else grp_at for name in names)
@@ -36,9 +36,10 @@
         )
     pl.semaphore_wait(barrier, len(offsets) + groups - 1)
 
+    heads = rows // HP
     inc_ref[...] = msg_ref[...]
-    out_ref[:, :rows] = jnp.zeros((out_ref.shape[0], rows, out_ref.shape[2]), jnp.float32)
-    out_ref[:, rows:] = jnp.ones((out_ref.shape[0], 8, out_ref.shape[2]), jnp.float32)
+    out_ref[:rows] = jnp.zeros((rows, out_ref.shape[1]), jnp.float32)
+    out_ref[rows:] = jnp.ones((8, out_ref.shape[1]), jnp.float32)
     for r, d in enumerate(_hops(peers)):
         copy = pltpu.make_async_remote_copy(
             src_ref=inc_ref,
@@ -51,15 +52,16 @@
         copy.start()
         copy.wait()
         reached = here >= d
-        got_state = recv_ref[r, :, :rows, :]
-        got_decay = recv_ref[r, :, rows:, :]
         for ref in ((out_ref, inc_ref) if 2 * d < peers else (out_ref,)):
-            decay = ref[:, rows:rows + 1, :]
-            ref[:, :rows] = jnp.where(reached, decay * got_state + ref[:, :rows], ref[:, :rows])
-            ref[:, rows:] = jnp.where(reached, decay * got_decay, ref[:, rows:])
-
-    send_ref[...] = out_ref[:, :rows].astype(send_ref.dtype)
-    spread_ref[grp_here] = out_ref[:, :rows].astype(spread_ref.dtype)
+            decay = ref[rows:rows + 1, :]
+            for h in range(heads):
+                part = pl.ds(h * HP, HP)
+                own = ref[part, :]
+                ref[part, :] = jnp.where(reached, decay[:, h:h + 1] * recv_ref[r, part, :] + own, own)
+            ref[rows:] = jnp.where(reached, ref[rows:] * recv_ref[r, rows:, :], ref[rows:])
+
+    send_ref[...] = out_ref[:rows].astype(send_ref.dtype)
+    spread_ref[grp_here] = out_ref[:rows].astype(spread_ref.dtype)
     copies = []
     for offset in range(1, groups):
         copy = pltpu.make_async_remote_copy(
@@ -97,23 +99,24 @@
 def carry_in(total_log, state_t, names, after):
     peers = lax.axis_size("seq")
     groups = lax.axis_size("grp")
-    heads, rows, lanes = state_t.shape
-    decay = jnp.broadcast_to(jnp.exp(total_log)[:, None, None], (heads, 8, lanes))
-    msg = jnp.concatenate([state_t, decay], axis=1)
+    heads, width, lanes = state_t.shape
+    rows = heads * width
+    decay = jnp.ones((8, lanes), jnp.float32).at[0, :heads].set(jnp.exp(total_log))
+    msg = jnp.concatenate([state_t.reshape(rows, lanes), decay], axis=0)
     shape = msg.shape
     hops = len(_hops(peers))
     _, spread = pl.pallas_call(
         functools.partial(scan_kernel, peers, names),
         out_shape=(
             jax.ShapeDtypeStruct(shape, jnp.float32),
-            jax.ShapeDtypeStruct((groups, heads, rows, lanes), jnp.bfloat16),
+            jax.ShapeDtypeStruct((groups, rows, lanes), jnp.bfloat16),
         ),
         in_specs=[pl.BlockSpec(memory_space=pltpu.VMEM), pl.BlockSpec(memory_space=pl.ANY)],
         out_specs=(pl.BlockSpec(memory_space=pltpu.VMEM), pl.BlockSpec(memory_space=pltpu.VMEM)),
         scratch_shapes=[
             pltpu.VMEM(shape, jnp.float32),
             pltpu.VMEM((hops,) + shape, jnp.float32),
-            pltpu.VMEM((heads, rows, lanes), jnp.bfloat16),
+            pltpu.VMEM((rows, lanes), jnp.bfloat16),
             pltpu.SemaphoreType.DMA((hops,)),
             pltpu.SemaphoreType.DMA((hops,)),
             pltpu.SemaphoreType.DMA((groups,)),
@@ -122,7 +125,7 @@
         compiler_params=pltpu.CompilerParams(collective_id=0, has_side_effects=True),
         cost_estimate=pl.CostEstimate(flops=0, transcendentals=0, bytes_accessed=512 * msg.size * 4),
     )(msg, after)
-    return spread.reshape(groups * heads, rows, lanes)
+    return spread.reshape(groups * rows, lanes)
 
 
 def on_device(
@@ -205,22 +208,16 @@
     def _():
         acc_ref[...] = jnp.zeros_like(acc_ref)
 
-    basis = basis_ref[...]
-    per = carried_ref.shape[0]
-    base = per * HP
-    for h in range(per):
-        rows = pl.ds(h * HP, HP)
-        carry = lax.dot_general(
-            carried_ref[h], basis, (((1,), (1,)), ((), ())), preferred_element_type=jnp.float32
-        )
-        mixed_ref[rows, :] = (
-            local_ref[rows, :].astype(jnp.float32)
-            + carry
-            * (
-                local_ref[pl.ds(base + h, 1), :].astype(jnp.float32)
-                + local_ref[pl.ds(base + per + h, 1), :].astype(jnp.float32)
-            )
-        ).astype(jnp.bfloat16)
+    base, tokens = mixed_ref.shape
+    per = base // HP
+    carry = lax.dot_general(
+        carried_ref[...], basis_ref[...], (((1,), (1,)), ((), ())), preferred_element_type=jnp.float32
+    )
+    scale = local_ref[pl.ds(base, per), :].astype(jnp.float32) + local_ref[
+        pl.ds(base + per, per), :
+    ].astype(jnp.float32)
+    carry = (carry.reshape(per, HP, tokens) * scale[:, None, :]).reshape(base, tokens)
+    mixed_ref[...] = (local_ref[pl.ds(0, base), :].astype(jnp.float32) + carry).astype(jnp.bfloat16)
     acc_ref[...] += jnp.dot(weight_ref[...], mixed_ref[...], preferred_element_type=jnp.float32)
 
     @pl.when(g == pl.num_programs(0) - 1)
@@ -231,9 +228,8 @@
 def tail(local_all, basis, carried_t, weight_t):
     channels, tokens = local_all.shape
     features = weight_t.shape[0]
-    heads = carried_t.shape[0]
     groups = lax.axis_size("grp")
-    per = heads // groups
+    per = carried_t.shape[0] // groups // HP
     return pl.pallas_call(
         tail_kernel,
         out_shape=jax.ShapeDtypeStruct((features, tokens), jnp.bfloat16),
@@ -241,7 +237,7 @@
         in_specs=[
             pl.BlockSpec((channels // groups, tokens), lambda g: (g, 0)),
             pl.BlockSpec(basis.shape, lambda g: (0, 0)),
-            pl.BlockSpec((per, HP, N), lambda g: (g, 0, 0)),
+            pl.BlockSpec((per * HP, N), lambda g: (g, 0)),
             pl.BlockSpec((features, per * HP), lambda g: (0, g)),
         ],
         out_specs=pl.BlockSpec((features, tokens), lambda g: (0, 0)),

time: 150 us -> 139 us (0.927)
  the two profiles are of different devices: /device:TPU:209 before, /device:TPU:1 now
where the time goes in v6:
time: 139 us
  Pallas kernels  101 us (73%)
  between operations  13.7 us (10%)
  matrix products  8.76 us (6%)
  other arithmetic  8.26 us (6%)
  local copies, waits for them, and re-layouts  6.6 us (5%)
    pallas_call x1, Pallas kernels, carry_in(): pl.pallas_call(functools.partial(scan_kernel, peers, names), out_shape=(j...  88.9 us
    pallas_call x1, Pallas kernels, tail(): pl.pallas_call(tail_kernel, out_shape=jax.ShapeDtypeStruct((features, tok...  12.5 us
    dot_general x1, matrix products, on_device(): jnp.einsum('hcij,hpcj->hpci', mixing, channels, preferred_element_type=jn...  4 us
    dot_general x1, matrix products, on_device(): jnp.einsum('hcjn,hpcj->chnp', weighted_terms, channels, preferred_element...  3.2 us
    reshape x1, local copies, waits for them, and re-layouts, on_device(): channels = mixer_input.reshape(heads_here, HP, count, GROUP)  2.88 us
  transfers between devices with their start and end apart: 1, of which 0 were waited for; matrix products, arithmetic and copies ran while one was open for 1% of the time, Pallas kernels for 64%

profile of v6, /device:TPU:1, one launch (start us, length us, event | category | flops | bytes accessed | tf_op | source)
XLA Modules:
  0.0 138.8 jit_solution(1634973699036776876)
XLA Ops:
  6.5 0.6 iota_compare_fusion.1
  7.2 0.9 mul.152
  8.1 0.9 fusion.25
  9.1 2.3 %reduce-window.6 = f32[10,4,2,128]{3,0,1,2:T(8,128)S(1)} reduce-window(f32[10,4,2,128]{3,0,1,2:T(8,128)S(1)} %copy.42, f32[]{:T(128)} %constant.35.clone.1), window={size=1x1x1x128 pad=0_0x0_0x0_0x127_0}, to_apply=%region_0.0 | reduce-window | flops 1300480 | bytes 81924 | tf_op jit(solution)/shard_map/reduce-window
  11.4 0.2 slice_reduce_fusion
  11.6 0.1 broadcast_add_fusion
  11.8 0.1 slice.89
  11.9 0.1 copy.45
  12.0 0.1 copy.46
  12.1 0.6 fusion.26
  12.7 0.6 copy.47
  13.4 2.9 %reshape.254 = bf16[10,64,4,256]{3,2,1,0:T(4,128)(2,1)S(1)} reshape(bf16[640,1024]{1,0:T(8,128)(2,1)} %param.9) | data formatting | bytes 2621440 | tf_op jit(solution)/shard_map/reshape | solution.py:138
  16.3 0.1 reduce_sum.9
  16.4 0.2 reduce_window_sum.47
  16.6 0.9 exponential_reduce_fusion.4
  17.5 0.3 fusion.28
  17.8 3.2 %fusion.7 = f32[4,10,128,64]{2,3,1,0:T(8,128)S(1)} fusion(f32[10,4,256]{2,0,1:T(8,128)} %copy.47, f32[4,256,128]{2,1,0:T(8,128)S(1)} %convert_element_type.30, bf16[10,64,4,256]{3,2,1,0:T(4,128)(2,1)S(1)} %reshape.254), kind=kOutput, calls=%fused_computation.9 | convolution fusion | flops 170393600 | bytes 3186688 | tf_op jit(solution)/shard_map/hcjn,hpcj->chnp/dot_general | solution.py:161
  21.0 0.0 copy-start.9
  21.0 0.2 slice_multiply_fusion
  21.2 1.3 fusion.13
  22.5 4.0 %fusion.10 = bf16[10,64,4,256]{3,1,2,0:T(8,128)(2,1)S(1)} fusion(f32[4,10,64,256]{3,2,0,1:T(8,128)S(1)} %fusion.13, f32[10,4,256]{2,1,0:T(4,128)S(1)} %mul.152, f32[10,4,256]{2,1,0:T(4,128)S(1)} %reduce_window_sum.46, f32[4,256,256]{2,1,0:T(8,128)S(1)} %fusion.28, pred[256,256]{1,0:T(8,128)(4,1)S(1)} %copy-done.2, ...), kind=kOutput, calls=%fused_computation.13 | convolution fusion | flops 355205120 | bytes 6479912 | tf_op jit(solution)/shard_map/hcij,hpcj->hpci/dot_general | solution.py:156
  26.5 1.0 copy.51
  27.6 0.3 copy.53
  27.9 0.1 add.47
  28.1 0.1 pad.10.clone
  28.1 1.4 maximum_maximum_fusion.after_ref
  29.5 0.0 all-gather.2.cloned.1.call-update
  29.6 0.2 fusion.18
  29.8 0.7 select_maximum_fusion.msg_ref
  30.5 88.9 %shard_map.73 = (f32[648,128]{1,0:T(8,128)}, bf16[8,640,128]{2,1,0:T(8,128)(2,1)}) custom-call(f32[648,128]{1,0:T(8,128)} %select_maximum_fusion.msg_ref, bf16[672,1024]{1,0:T(8,128)(2,1)} %maximum_maximum_fusion.after_ref), custom_call_target="tpu_custom_call" | custom-call | bytes 169869312 | tf_op jit(solution)/shard_map/pallas_call | solution.py:108
  119.4 0.0 all-gather.2.cloned.1.call-done.local_ref
  119.5 12.5 %shard_map.74 = bf16[320,1024]{1,0:T(8,128)(2,1)} custom-call(bf16[5376,1024]{1,0:T(8,128)(2,1)} %all-gather.2.cloned.1.call-done.local_ref, bf16[1024,128]{1,0:T(8,128)(2,1)} %basis_ref.1, bf16[5120,128]{1,0:T(8,128)(2,1)} %bitcast.67, bf16[320,5120]{1,0:T(8,128)(2,1)} %bitcast.66), custom_call_target="tpu_custom_call" | custom-call | flops 4697620480 | bytes 14942208 | tf_op jit(solution)/shard_map/pallas_call | solution.py:233
  (36 shorter events, 0.3 us)
Async XLA Ops:
  6.5 9.7 %copy-start = (bf16[1024,128]{1,0:T(8,128)(2,1)S(1)}, bf16[1024,128]{1,0:T(8,128)(2,1)}, u32[]{:S(2)}) copy-start(bf16[1024,128]{1,0:T(8,128)(2,1)} %param.13) | copy-start | bytes 786436
  6.5 112.9 %all-gather.2.cloned.1.call-start = ((), (), s32[]{:S(2)}) async-start(), calls=%async_computation | async-start | bytes 12386304 | tf_op jit(solution)/shard_map/all_gather | solution.py:198
  7.2 10.3 %copy-start.1 = (bf16[1024,128]{1,0:T(8,128)(2,1)S(1)}, bf16[1024,128]{1,0:T(8,128)(2,1)}, u32[]{:S(2)}) copy-start(bf16[1024,128]{1,0:T(8,128)(2,1)} %basis_ref.1) | copy-start | bytes 786436
  21.0 1.5 %copy-start.2 = (pred[256,256]{1,0:T(8,128)(4,1)S(1)}, pred[256,256]{1,0:T(8,128)(4,1)}, u32[]{:S(2)}) copy-start(pred[256,256]{1,0:T(8,128)(4,1)} %iota_compare_fusion.1) | copy-start | bytes 196612
  21.0 1.5 %copy-start.3 = (f32[10,4,256]{2,1,0:T(4,128)S(1)}, f32[10,4,256]{2,1,0:T(4,128)}, u32[]{:S(2)}) copy-start(f32[10,4,256]{2,1,0:T(4,128)} %get-tuple-element.37) | copy-start | bytes 122884
  21.0 1.5 %copy-start.9 = (f32[10]{0:T(128)S(1)}, f32[10]{0:T(128)}, u32[]{:S(2)}) copy-start(f32[10]{0:T(128)} %param.12) | copy-start | bytes 124
  27.9 1.7 %copy-start.4 = (f32[10]{0:T(128)S(1)}, f32[10]{0:T(128)}, u32[]{:S(2)}) copy-start(f32[10]{0:T(128)} %get-tuple-element.25) | copy-start | bytes 124
  27.9 1.7 %copy-start.5 = (f32[10]{0:T(128)S(1)}, f32[10]{0:T(128)}, u32[]{:S(2)}) copy-start(f32[10]{0:T(128)} %get-tuple-element.27) | copy-start | bytes 124
  27.9 1.7 %copy-start.6 = (f32[10]{0:T(128)S(1)}, f32[10]{0:T(128)}, u32[]{:S(2)}) copy-start(f32[10]{0:T(128)} %get-tuple-element.28) | copy-start | bytes 124
  27.9 1.7 %copy-start.7 = (f32[10]{0:T(128)S(1)}, f32[10]{0:T(128)}, u32[]{:S(2)}) copy-start(f32[10]{0:T(128)} %get-tuple-element.29) | copy-start | bytes 124
  28.1 1.6 %copy-start.8 = (f32[10]{0:T(128)S(1)}, f32[10]{0:T(128)}, u32[]{:S(2)}) copy-start(f32[10]{0:T(128)} %get-tuple-element.26) | copy-start | bytes 124
Sparse Core Ops, SparseCore 0:
  29.6 67.4 all-gather.1

commit v7 on v6

--- a/solution.py
+++ b/solution.py
@@ -12,12 +12,13 @@
 GROUP = 256
 
 
-def scan_kernel(peers, names, msg_ref, after_ref, out_ref, spread_ref, inc_ref, recv_ref, send_ref,
-                send_sem, recv_sem, spread_send, spread_recv):
+def scan_kernel(peers, names, msg_ref, after_ref, out_ref, spread_ref, inc_ref, out_state, recv_state,
+                recv_decay, send_ref, send_sem, recv_sem, decay_send, decay_recv, spread_send, spread_recv):
     here = lax.axis_index("seq")
     grp_here = lax.axis_index("grp")
     groups = spread_ref.shape[0]
     rows = msg_ref.shape[0] - 8
+    heads = rows // HP
 
     def device(seq_at, grp_at):
         return tuple(seq_at if name == "seq" else grp_at for name in names)
@@ -36,29 +37,41 @@
         )
     pl.semaphore_wait(barrier, len(offsets) + groups - 1)
 
-    heads = rows // HP
     inc_ref[...] = msg_ref[...]
     out_ref[:rows] = jnp.zeros((rows, out_ref.shape[1]), jnp.float32)
     out_ref[rows:] = jnp.ones((8, out_ref.shape[1]), jnp.float32)
     for r, d in enumerate(_hops(peers)):
-        copy = pltpu.make_async_remote_copy(
-            src_ref=inc_ref,
-            dst_ref=recv_ref.at[r],
+        target = device(lax.rem(here + d, peers), grp_here)
+        out_state[r] = inc_ref[:rows].astype(out_state.dtype)
+        state_copy = pltpu.make_async_remote_copy(
+            src_ref=out_state.at[r],
+            dst_ref=recv_state.at[r],
             send_sem=send_sem.at[r],
             recv_sem=recv_sem.at[r],
-            device_id=device(lax.rem(here + d, peers), grp_here),
-            device_id_type=pl.DeviceIdType.MESH,
-        )
-        copy.start()
-        copy.wait()
+            device_id=target,
+            device_id_type=pl.DeviceIdType.MESH,
+        )
+        decay_copy = pltpu.make_async_remote_copy(
+            src_ref=inc_ref.at[pl.ds(rows, 8)],
+            dst_ref=recv_decay.at[r],
+            send_sem=decay_send.at[r],
+            recv_sem=decay_recv.at[r],
+            device_id=target,
+            device_id_type=pl.DeviceIdType.MESH,
+        )
+        state_copy.start()
+        decay_copy.start()
+        state_copy.wait()
+        decay_copy.wait()
         reached = here >= d
         for ref in ((out_ref, inc_ref) if 2 * d < peers else (out_ref,)):
             decay = ref[rows:rows + 1, :]
             for h in range(heads):
                 part = pl.ds(h * HP, HP)
                 own = ref[part, :]
-                ref[part, :] = jnp.where(reached, decay[:, h:h + 1] * recv_ref[r, part, :] + own, own)
-            ref[rows:] = jnp.where(reached, ref[rows:] * recv_ref[r, rows:, :], ref[rows:])
+                got = recv_state[r, part, :].astype(jnp.float32)
+                ref[part, :] = jnp.where(reached, decay[:, h:h + 1] * got + own, own)
+            ref[rows:] = jnp.where(reached, ref[rows:] * recv_decay[r], ref[rows:])
 
     send_ref[...] = out_ref[:rows].astype(send_ref.dtype)
     spread_ref[grp_here] = out_ref[:rows].astype(spread_ref.dtype)
@@ -115,8 +128,12 @@
         out_specs=(pl.BlockSpec(memory_space=pltpu.VMEM), pl.BlockSpec(memory_space=pltpu.VMEM)),
         scratch_shapes=[
             pltpu.VMEM(shape, jnp.float32),
-            pltpu.VMEM((hops,) + shape, jnp.float32),
+            pltpu.VMEM((hops, rows, lanes), jnp.bfloat16),
+            pltpu.VMEM((hops, rows, lanes), jnp.bfloat16),
+            pltpu.VMEM((hops, 8, lanes), jnp.float32),
             pltpu.VMEM((rows, lanes), jnp.bfloat16),
+            pltpu.SemaphoreType.DMA((hops,)),
+            pltpu.SemaphoreType.DMA((hops,)),
             pltpu.SemaphoreType.DMA((hops,)),
             pltpu.SemaphoreType.DMA((hops,)),
             pltpu.SemaphoreType.DMA((groups,)),

time: 139 us -> 131 us (0.942)
  Pallas kernels: 101 us -> 92.3 us
    pallas_call x1, Pallas kernels: 88.9 us -> 79.8 us  [carry_in(): pl.pallas_call(functools.partial(scan_kernel, peers, names), out_shape=(j...]
  transfers between devices with their start and end apart: 1 -> 1, of which waited for: 0 -> 1; matrix products, arithmetic and copies ran while one was open for 1% -> 1% of each run, Pallas kernels for 64% -> 61%
where the time goes in v7:
time: 131 us
  Pallas kernels  92.3 us (70%)
  between operations  13.7 us (10%)
  matrix products  8.76 us (7%)
  other arithmetic  8.26 us (6%)
  local copies, waits for them, and re-layouts  6.6 us (5%)
    pallas_call x1, Pallas kernels, carry_in(): pl.pallas_call(functools.partial(scan_kernel, peers, names), out_shape=(j...  79.8 us
    pallas_call x1, Pallas kernels, tail(): pl.pallas_call(tail_kernel, out_shape=jax.ShapeDtypeStruct((features, tok...  12.5 us
    dot_general x1, matrix products, on_device(): jnp.einsum('hcij,hpcj->hpci', mixing, channels, preferred_element_type=jn...  4 us
    dot_general x1, matrix products, on_device(): jnp.einsum('hcjn,hpcj->chnp', weighted_terms, channels, preferred_element...  3.2 us
    reshape x1, local copies, waits for them, and re-layouts, on_device(): channels = mixer_input.reshape(heads_here, HP, count, GROUP)  2.88 us
  transfers between devices with their start and end apart: 1, of which 1 were waited for; matrix products, arithmetic and copies ran while one was open for 1% of the time, Pallas kernels for 61%

profile of v7, /device:TPU:1, one launch (start us, length us, event | category | flops | bytes accessed | tf_op | source)
XLA Modules:
  0.0 130.5 jit_solution(1124117824354570617)
XLA Ops:
  6.5 0.6 iota_compare_fusion.1
  7.2 0.9 mul.152
  8.1 0.9 fusion.25
  9.1 2.3 %reduce-window.6 = f32[10,4,2,128]{3,0,1,2:T(8,128)S(1)} reduce-window(f32[10,4,2,128]{3,0,1,2:T(8,128)S(1)} %copy.42, f32[]{:T(128)} %constant.35.clone.1), window={size=1x1x1x128 pad=0_0x0_0x0_0x127_0}, to_apply=%region_0.0 | reduce-window | flops 1300480 | bytes 81924 | tf_op jit(solution)/shard_map/reduce-window
  11.4 0.2 slice_reduce_fusion
  11.6 0.1 broadcast_add_fusion
  11.8 0.1 slice.89
  11.9 0.1 copy.45
  12.0 0.1 copy.46
  12.1 0.6 fusion.26
  12.7 0.6 copy.47
  13.4 2.9 %reshape.254 = bf16[10,64,4,256]{3,2,1,0:T(4,128)(2,1)S(1)} reshape(bf16[640,1024]{1,0:T(8,128)(2,1)} %param.9) | data formatting | bytes 2621440 | tf_op jit(solution)/shard_map/reshape | solution.py:155
  16.3 0.1 reduce_sum.9
  16.4 0.2 reduce_window_sum.47
  16.6 0.9 exponential_reduce_fusion.4
  17.5 0.3 fusion.28
  17.8 3.2 %fusion.7 = f32[4,10,128,64]{2,3,1,0:T(8,128)S(1)} fusion(f32[10,4,256]{2,0,1:T(8,128)} %copy.47, f32[4,256,128]{2,1,0:T(8,128)S(1)} %convert_element_type.30, bf16[10,64,4,256]{3,2,1,0:T(4,128)(2,1)S(1)} %reshape.254), kind=kOutput, calls=%fused_computation.9 | convolution fusion | flops 170393600 | bytes 3186688 | tf_op jit(solution)/shard_map/hcjn,hpcj->chnp/dot_general | solution.py:178
  21.0 0.0 copy-start.9
  21.0 0.2 slice_multiply_fusion
  21.2 1.3 fusion.13
  22.5 4.0 %fusion.10 = bf16[10,64,4,256]{3,1,2,0:T(8,128)(2,1)S(1)} fusion(f32[4,10,64,256]{3,2,0,1:T(8,128)S(1)} %fusion.13, f32[10,4,256]{2,1,0:T(4,128)S(1)} %mul.152, f32[10,4,256]{2,1,0:T(4,128)S(1)} %reduce_window_sum.46, f32[4,256,256]{2,1,0:T(8,128)S(1)} %fusion.28, pred[256,256]{1,0:T(8,128)(4,1)S(1)} %copy-done.2, ...), kind=kOutput, calls=%fused_computation.13 | convolution fusion | flops 355205120 | bytes 6479912 | tf_op jit(solution)/shard_map/hcij,hpcj->hpci/dot_general | solution.py:173
  26.5 1.0 copy.51
  27.6 0.3 copy.53
  27.9 0.1 add.47
  28.1 0.1 pad.10.clone
  28.1 1.4 %maximum_maximum_fusion.after_ref = bf16[672,1024]{1,0:T(8,128)(2,1)} fusion(bf16[10,1024]{1,0:T(8,128)(2,1)S(1)} %get-tuple-element.36, bf16[10,1024]{1,0:T(8,128)(2,1)S(1)} %get-tuple-element.35, bf16[640,1024]{1,0:T(8,128)(2,1)S(1)} %bitcast.55, bf16[672]{0:T(1024)(128)(2,1)S(1)} %pad.10.clone), kind=kLoop, calls=%fused_computation.16 | loop fusion | flops 5505024 | bytes 2729280 | tf_op jit(solution)/shard_map/concatenate | solution.py:206
  29.5 0.0 all-gather.2.cloned.1.call-update
  29.6 0.2 fusion.18
  29.8 0.7 select_maximum_fusion.msg_ref
  30.5 79.8 %shard_map.73 = (f32[648,128]{1,0:T(8,128)}, bf16[8,640,128]{2,1,0:T(8,128)(2,1)}) custom-call(f32[648,128]{1,0:T(8,128)} %select_maximum_fusion.msg_ref, bf16[672,1024]{1,0:T(8,128)(2,1)} %maximum_maximum_fusion.after_ref), custom_call_target="tpu_custom_call" | custom-call | bytes 169869312 | tf_op jit(solution)/shard_map/pallas_call | solution.py:121
  110.3 0.9 all-gather.2.cloned.1.call-done.local_ref
  111.2 12.5 %shard_map.74 = bf16[320,1024]{1,0:T(8,128)(2,1)} custom-call(bf16[5376,1024]{1,0:T(8,128)(2,1)} %all-gather.2.cloned.1.call-done.local_ref, bf16[1024,128]{1,0:T(8,128)(2,1)} %basis_ref.1, bf16[5120,128]{1,0:T(8,128)(2,1)} %bitcast.67, bf16[320,5120]{1,0:T(8,128)(2,1)} %bitcast.66), custom_call_target="tpu_custom_call" | custom-call | flops 4697620480 | bytes 14942208 | tf_op jit(solution)/shard_map/pallas_call | solution.py:250
  (36 shorter events, 0.3 us)
Async XLA Ops:
  6.5 9.7 %copy-start = (bf16[1024,128]{1,0:T(8,128)(2,1)S(1)}, bf16[1024,128]{1,0:T(8,128)(2,1)}, u32[]{:S(2)}) copy-start(bf16[1024,128]{1,0:T(8,128)(2,1)} %param.13) | copy-start | bytes 786436
  6.5 104.6 %all-gather.2.cloned.1.call-start = ((), (), s32[]{:S(2)}) async-start(), calls=%async_computation | async-start | bytes 12386304 | tf_op jit(solution)/shard_map/all_gather | solution.py:215
  7.2 10.3 %copy-start.1 = (bf16[1024,128]{1,0:T(8,128)(2,1)S(1)}, bf16[1024,128]{1,0:T(8,128)(2,1)}, u32[]{:S(2)}) copy-start(bf16[1024,128]{1,0:T(8,128)(2,1)} %basis_ref.1) | copy-start | bytes 786436
  21.0 1.5 %copy-start.2 = (pred[256,256]{1,0:T(8,128)(4,1)S(1)}, pred[256,256]{1,0:T(8,128)(4,1)}, u32[]{:S(2)}) copy-start(pred[256,256]{1,0:T(8,128)(4,1)} %iota_compare_fusion.1) | copy-start | bytes 196612
  21.0 1.5 %copy-start.3 = (f32[10,4,256]{2,1,0:T(4,128)S(1)}, f32[10,4,256]{2,1,0:T(4,128)}, u32[]{:S(2)}) copy-start(f32[10,4,256]{2,1,0:T(4,128)} %get-tuple-element.37) | copy-start | bytes 122884
  21.0 1.5 %copy-start.9 = (f32[10]{0:T(128)S(1)}, f32[10]{0:T(128)}, u32[]{:S(2)}) copy-start(f32[10]{0:T(128)} %param.12) | copy-start | bytes 124
  27.9 1.7 %copy-start.4 = (f32[10]{0:T(128)S(1)}, f32[10]{0:T(128)}, u32[]{:S(2)}) copy-start(f32[10]{0:T(128)} %get-tuple-element.25) | copy-start | bytes 124
  27.9 1.7 %copy-start.5 = (f32[10]{0:T(128)S(1)}, f32[10]{0:T(128)}, u32[]{:S(2)}) copy-start(f32[10]{0:T(128)} %get-tuple-element.27) | copy-start | bytes 124
  27.9 1.7 %copy-start.6 = (f32[10]{0:T(128)S(1)}, f32[10]{0:T(128)}, u32[]{:S(2)}) copy-start(f32[10]{0:T(128)} %get-tuple-element.28) | copy-start | bytes 124
  27.9 1.7 %copy-start.7 = (f32[10]{0:T(128)S(1)}, f32[10]{0:T(128)}, u32[]{:S(2)}) copy-start(f32[10]{0:T(128)} %get-tuple-element.29) | copy-start | bytes 124
  28.1 1.6 %copy-start.8 = (f32[10]{0:T(128)S(1)}, f32[10]{0:T(128)}, u32[]{:S(2)}) copy-start(f32[10]{0:T(128)} %get-tuple-element.26) | copy-start | bytes 124
Sparse Core Ops, SparseCore 0:
  29.6 81.4 all-gather.1

commit v8 on v6

--- a/solution.py
+++ b/solution.py
@@ -12,12 +12,14 @@
 GROUP = 256
 
 
-def scan_kernel(peers, names, msg_ref, after_ref, out_ref, spread_ref, inc_ref, recv_ref, send_ref,
-                send_sem, recv_sem, spread_send, spread_recv):
+def scan_kernel(peers, names, msg_ref, local_ref, out_ref, spread_ref, gathered_ref, inc_ref, out_state,
+                recv_state, recv_decay, send_ref, send_sem, recv_sem, decay_send, decay_recv, spread_send,
+                spread_recv, ring_send, ring_recv, own_sem):
     here = lax.axis_index("seq")
     grp_here = lax.axis_index("grp")
     groups = spread_ref.shape[0]
     rows = msg_ref.shape[0] - 8
+    heads = rows // HP
 
     def device(seq_at, grp_at):
         return tuple(seq_at if name == "seq" else grp_at for name in names)
@@ -36,29 +38,98 @@
         )
     pl.semaphore_wait(barrier, len(offsets) + groups - 1)
 
-    heads = rows // HP
     inc_ref[...] = msg_ref[...]
     out_ref[:rows] = jnp.zeros((rows, out_ref.shape[1]), jnp.float32)
     out_ref[rows:] = jnp.ones((8, out_ref.shape[1]), jnp.float32)
-    for r, d in enumerate(_hops(peers)):
-        copy = pltpu.make_async_remote_copy(
-            src_ref=inc_ref,
-            dst_ref=recv_ref.at[r],
-            send_sem=send_sem.at[r],
-            recv_sem=recv_sem.at[r],
-            device_id=device(lax.rem(here + d, peers), grp_here),
-            device_id_type=pl.DeviceIdType.MESH,
-        )
-        copy.start()
-        copy.wait()
-        reached = here >= d
-        for ref in ((out_ref, inc_ref) if 2 * d < peers else (out_ref,)):
-            decay = ref[rows:rows + 1, :]
-            for h in range(heads):
-                part = pl.ds(h * HP, HP)
-                own = ref[part, :]
-                ref[part, :] = jnp.where(reached, decay[:, h:h + 1] * recv_ref[r, part, :] + own, own)
-            ref[rows:] = jnp.where(reached, ref[rows:] * recv_ref[r, rows:, :], ref[rows:])
+    half = local_ref.shape[0] // 2
+    right = device(here, lax.rem(grp_here + 1, groups))
+    left = device(here, lax.rem(grp_here + groups - 1, groups))
+    own_copy = pltpu.make_async_copy(local_ref, gathered_ref.at[grp_here], own_sem.at[0])
+    own_copy.start()
+
+    def ring(k, direction):
+        first = pl.ds(0, half) if direction == 0 else pl.ds(half, half)
+        if direction == 0:
+            slot = lax.rem(grp_here + groups - k, groups)
+        else:
+            slot = lax.rem(grp_here + k, groups)
+        source = local_ref.at[first] if k == 0 else gathered_ref.at[slot, first]
+        return pltpu.make_async_remote_copy(
+            src_ref=source,
+            dst_ref=gathered_ref.at[slot, first],
+            send_sem=ring_send.at[direction, k],
+            recv_sem=ring_recv.at[direction, k],
+            device_id=right if direction == 0 else left,
+            device_id_type=pl.DeviceIdType.MESH,
+        )
+
+    def incoming(k, direction):
+        first = pl.ds(0, half) if direction == 0 else pl.ds(half, half)
+        if direction == 0:
+            slot = lax.rem(grp_here + groups - 1 - k, groups)
+        else:
+            slot = lax.rem(grp_here + 1 + k, groups)
+        return pltpu.make_async_remote_copy(
+            src_ref=local_ref.at[first],
+            dst_ref=gathered_ref.at[slot, first],
+            send_sem=ring_send.at[direction, k],
+            recv_sem=ring_recv.at[direction, k],
+            device_id=left if direction == 0 else right,
+            device_id_type=pl.DeviceIdType.MESH,
+        )
+
+    sent = []
+    hops = _hops(peers)
+    for k in range(max(groups - 1, len(hops))):
+        if k < groups - 1:
+            if k >= 1:
+                incoming(k - 1, 0).wait_recv()
+                incoming(k - 1, 1).wait_recv()
+            for direction in (0, 1):
+                copy = ring(k, direction)
+                copy.start()
+                sent.append(copy)
+        if k < len(hops):
+            r, d = k, hops[k]
+            target = device(lax.rem(here + d, peers), grp_here)
+            out_state[r] = inc_ref[:rows].astype(out_state.dtype)
+            state_copy = pltpu.make_async_remote_copy(
+                src_ref=out_state.at[r],
+                dst_ref=recv_state.at[r],
+                send_sem=send_sem.at[r],
+                recv_sem=recv_sem.at[r],
+                device_id=target,
+                device_id_type=pl.DeviceIdType.MESH,
+            )
+            decay_copy = pltpu.make_async_remote_copy(
+                src_ref=inc_ref.at[pl.ds(rows, 8)],
+                dst_ref=recv_decay.at[r],
+                send_sem=decay_send.at[r],
+                recv_sem=decay_recv.at[r],
+                device_id=target,
+                device_id_type=pl.DeviceIdType.MESH,
+            )
+            state_copy.start()
+            decay_copy.start()
+            state_copy.wait()
+            decay_copy.wait()
+            reached = here >= d
+            for ref in ((out_ref, inc_ref) if 2 * d < peers else (out_ref,)):
+                decay = ref[rows:rows + 1, :]
+                for h in range(heads):
+                    part = pl.ds(h * HP, HP)
+                    own = ref[part, :]
+                    got = recv_state[r, part, :].astype(jnp.float32)
+                    ref[part, :] = jnp.where(reached, decay[:, h:h + 1] * got + own, own)
+                ref[rows:] = jnp.where(reached, ref[rows:] * recv_decay[r], ref[rows:])
+
+
+    if groups > 1:
+        incoming(groups - 2, 0).wait_recv()
+        incoming(groups - 2, 1).wait_recv()
+    for copy in sent:
+        copy.wait_send()
+    own_copy.wait()
 
     send_ref[...] = out_ref[:rows].astype(send_ref.dtype)
     spread_ref[grp_here] = out_ref[:rows].astype(spread_ref.dtype)
@@ -96,7 +167,7 @@
     return hops
 
 
-def carry_in(total_log, state_t, names, after):
+def carry_in(total_log, state_t, names, local_ext):
     peers = lax.axis_size("seq")
     groups = lax.axis_size("grp")
     heads, width, lanes = state_t.shape
@@ -105,27 +176,39 @@
     msg = jnp.concatenate([state_t.reshape(rows, lanes), decay], axis=0)
     shape = msg.shape
     hops = len(_hops(peers))
-    _, spread = pl.pallas_call(
+    _, spread, gathered = pl.pallas_call(
         functools.partial(scan_kernel, peers, names),
         out_shape=(
             jax.ShapeDtypeStruct(shape, jnp.float32),
             jax.ShapeDtypeStruct((groups, rows, lanes), jnp.bfloat16),
+            jax.ShapeDtypeStruct((groups,) + local_ext.shape, jnp.bfloat16),
         ),
-        in_specs=[pl.BlockSpec(memory_space=pltpu.VMEM), pl.BlockSpec(memory_space=pl.ANY)],
-        out_specs=(pl.BlockSpec(memory_space=pltpu.VMEM), pl.BlockSpec(memory_space=pltpu.VMEM)),
+        in_specs=[pl.BlockSpec(memory_space=pltpu.VMEM), pl.BlockSpec(memory_space=pltpu.VMEM)],
+        out_specs=(
+            pl.BlockSpec(memory_space=pltpu.VMEM),
+            pl.BlockSpec(memory_space=pltpu.VMEM),
+            pl.BlockSpec(memory_space=pl.ANY),
+        ),
         scratch_shapes=[
             pltpu.VMEM(shape, jnp.float32),
-            pltpu.VMEM((hops,) + shape, jnp.float32),
+            pltpu.VMEM((hops, rows, lanes), jnp.bfloat16),
+            pltpu.VMEM((hops, rows, lanes), jnp.bfloat16),
+            pltpu.VMEM((hops, 8, lanes), jnp.float32),
             pltpu.VMEM((rows, lanes), jnp.bfloat16),
+            pltpu.SemaphoreType.DMA((hops,)),
+            pltpu.SemaphoreType.DMA((hops,)),
             pltpu.SemaphoreType.DMA((hops,)),
             pltpu.SemaphoreType.DMA((hops,)),
             pltpu.SemaphoreType.DMA((groups,)),
             pltpu.SemaphoreType.DMA((groups,)),
+            pltpu.SemaphoreType.DMA((2, max(groups - 1, 1))),
+            pltpu.SemaphoreType.DMA((2, max(groups - 1, 1))),
+            pltpu.SemaphoreType.DMA((1,)),
         ],
         compiler_params=pltpu.CompilerParams(collective_id=0, has_side_effects=True),
         cost_estimate=pl.CostEstimate(flops=0, transcendentals=0, bytes_accessed=512 * msg.size * 4),
-    )(msg, after)
-    return spread.reshape(groups * rows, lanes)
+    )(msg, local_ext)
+    return spread.reshape(groups * rows, lanes), gathered.reshape(groups * local_ext.shape[0], -1)
 
 
 def on_device(
@@ -195,8 +278,7 @@
         ],
         axis=0,
     )
-    local_all = lax.all_gather(local_ext, "grp", axis=0, tiled=True)
-    carried_t = carry_in(total_log, jnp.swapaxes(final_state, 1, 2), names, local_ext)
+    carried_t, local_all = carry_in(total_log, jnp.swapaxes(final_state, 1, 2), names, local_ext)
     result_t = tail(local_all, output_basis, carried_t, out_weight.T)
     return result_t.T
 

time: 139 us -> 143 us (1.029)
  Pallas kernels: 101 us -> 117 us
  between operations: 13.7 us -> 0.45 us
    pallas_call x1, Pallas kernels: 88.9 us -> 104 us  [carry_in(): pl.pallas_call(functools.partial(scan_kernel, peers, names), out_shape=(j...]
    reshape x1, local copies, waits for them, and re-layouts: 2.88 us -> 1.01 us  [on_device(): channels = mixer_input.reshape(heads_here, HP, count, GROUP)]
  transfers between devices with their start and end apart: 1 -> 0, of which waited for: 0 -> 0; matrix products, arithmetic and copies ran while one was open for 1% -> 0% of each run, Pallas kernels for 64% -> 0%
where the time goes in v8:
time: 143 us; the launch traced here: 142 us
  Pallas kernels  117 us (82%)
  matrix products  9.75 us (7%)
  other arithmetic  9.24 us (6%)
  local copies, waits for them, and re-layouts  6.06 us (4%)
    pallas_call x1, Pallas kernels, carry_in(): pl.pallas_call(functools.partial(scan_kernel, peers, names), out_shape=(j...  104 us
    pallas_call x1, Pallas kernels, tail(): pl.pallas_call(tail_kernel, out_shape=jax.ShapeDtypeStruct((features, tok...  12.5 us
    dot_general x1, matrix products, on_device(): jnp.einsum('hcij,hpcj->hpci', mixing, channels, preferred_element_type=jn...  4 us
    dot_general x1, matrix products, on_device(): jnp.einsum('hcjn,hpcj->chnp', weighted_terms, channels, preferred_element...  3.19 us

profile of v8, /device:TPU:1, one launch (start us, length us, event | category | flops | bytes accessed | tf_op | source)
XLA Modules:
  0.0 142.1 jit_solution(10973205884536311611)
XLA Ops:
  0.0 0.6 pad.9.clone
  0.6 0.7 pad.8.clone
  1.2 0.9 reshape.259
  2.1 0.6 iota_compare_fusion.1
  2.8 0.9 fusion.25
  3.7 2.3 %reduce-window.6 = f32[10,4,2,128]{3,0,1,2:T(8,128)S(1)} reduce-window(f32[10,4,2,128]{3,0,1,2:T(8,128)S(1)} %copy.42, f32[]{:T(128)} %constant.35.clone.1), window={size=1x1x1x128 pad=0_0x0_0x0_0x127_0}, to_apply=%region_2.3 | reduce-window | flops 1300480 | bytes 81924 | tf_op jit(solution)/shard_map/reduce-window
  6.0 0.2 slice_reduce_fusion
  6.2 0.1 broadcast_add_fusion
  6.4 0.1 slice.89
  6.5 0.1 copy.44
  6.6 0.1 copy.45
  6.8 0.1 reduce_sum.9
  6.9 0.2 reduce_window_sum.45
  7.0 0.9 fusion.23
  8.0 0.1 add.50
  8.1 0.6 fusion.26
  8.7 0.6 copy.46
  9.4 1.0 convert_element_type.29
  10.4 1.3 fusion.28
  11.7 1.0 reshape.260
  12.8 3.2 %fusion.7 = f32[4,10,128,64]{2,3,1,0:T(8,128)S(1)} fusion(f32[10,4,256]{2,0,1:T(8,128)} %copy.46, f32[4,256,128]{2,1,0:T(8,128)S(1)} %convert_element_type.29, bf16[10,64,4,256]{3,2,1,0:T(4,128)(2,1)S(1)} %reshape.260), kind=kOutput, calls=%fused_computation.9 | convolution fusion | flops 170393600 | bytes 3186688 | tf_op jit(solution)/shard_map/hcjn,hpcj->chnp/dot_general | solution.py:244
  16.1 0.2 fusion.18
  16.3 0.2 slice_multiply_fusion
  16.5 0.2 copy-done.11
  16.7 0.7 select_maximum_fusion.msg_ref
  17.5 1.3 fusion.13
  18.8 4.0 %fusion.10 = bf16[10,64,4,256]{3,1,2,0:T(8,128)(2,1)S(1)} fusion(f32[4,10,64,256]{3,2,0,1:T(8,128)S(1)} %fusion.13, f32[10,4,256]{2,1,0:T(4,128)S(1)} %reshape.259, f32[10,4,256]{2,1,0:T(4,128)S(1)} %reduce_window_sum.47, f32[4,256,256]{2,1,0:T(8,128)S(1)} %copy-done.1, pred[256,256]{1,0:T(8,128)(4,1)S(1)} %copy-done.4, ...), kind=kOutput, calls=%fused_computation.13 | convolution fusion | flops 355205120 | bytes 6479912 | tf_op jit(solution)/shard_map/hcij,hpcj->hpci/dot_general | solution.py:239
  22.8 1.0 copy.51
  23.8 0.3 copy.53
  24.1 1.4 maximum_maximum_fusion.local_ref
  25.5 104.1 %shard_map.73 = (f32[648,128]{1,0:T(8,128)}, bf16[8,640,128]{2,1,0:T(8,128)(2,1)}, bf16[8,672,1024]{2,1,0:T(8,128)(2,1)}) custom-call(f32[648,128]{1,0:T(8,128)} %select_maximum_fusion.msg_ref, bf16[672,1024]{1,0:T(8,128)(2,1)} %maximum_maximum_fusion.local_ref), custom_call_target="tpu_custom_call" | custom-call | bytes 169869312 | tf_op jit(solution)/shard_map/pallas_call | solution.py:179
  129.6 12.5 %shard_map.74 = bf16[320,1024]{1,0:T(8,128)(2,1)} custom-call(bf16[5376,1024]{1,0:T(8,128)(2,1)} %bitcast.67, bf16[1024,128]{1,0:T(8,128)(2,1)} %basis_ref.1, bf16[5120,128]{1,0:T(8,128)(2,1)} %bitcast.69, bf16[320,5120]{1,0:T(8,128)(2,1)} %bitcast.68), custom_call_target="tpu_custom_call" | custom-call | flops 4697620480 | bytes 14942208 | tf_op jit(solution)/shard_map/pallas_call | solution.py:315
  (53 shorter events, 0.3 us)
Async XLA Ops:
  0.0 10.4 %copy-start.3 = (bf16[1024,128]{1,0:T(8,128)(2,1)S(1)}, bf16[1024,128]{1,0:T(8,128)(2,1)}, u32[]{:S(2)}) copy-start(bf16[1024,128]{1,0:T(8,128)(2,1)} %basis_ref.1) | copy-start | bytes 786436
  0.0 10.4 %copy-start.2 = (bf16[1024,128]{1,0:T(8,128)(2,1)S(1)}, bf16[1024,128]{1,0:T(8,128)(2,1)}, u32[]{:S(2)}) copy-start(bf16[1024,128]{1,0:T(8,128)(2,1)} %param.13) | copy-start | bytes 786436
  0.0 11.7 %copy-start = (bf16[640,1024]{1,0:T(8,128)(2,1)S(1)}, bf16[640,1024]{1,0:T(8,128)(2,1)}, u32[]{:S(2)}) copy-start(bf16[640,1024]{1,0:T(8,128)(2,1)} %param.9) | copy-start | bytes 3932164
  12.7 3.3 %copy-start.7 = (f32[10]{0:T(128)S(1)}, f32[10]{0:T(128)}, u32[]{:S(2)}) copy-start(f32[10]{0:T(128)} %get-tuple-element.28) | copy-start | bytes 124
  12.7 3.3 %copy-start.8 = (f32[10]{0:T(128)S(1)}, f32[10]{0:T(128)}, u32[]{:S(2)}) copy-start(f32[10]{0:T(128)} %get-tuple-element.29) | copy-start | bytes 124
  12.7 3.3 %copy-start.9 = (f32[10]{0:T(128)S(1)}, f32[10]{0:T(128)}, u32[]{:S(2)}) copy-start(f32[10]{0:T(128)} %get-tuple-element.30) | copy-start | bytes 124
  12.7 3.3 %copy-start.10 = (f32[10]{0:T(128)S(1)}, f32[10]{0:T(128)}, u32[]{:S(2)}) copy-start(f32[10]{0:T(128)} %get-tuple-element.40) | copy-start | bytes 124
  12.7 3.5 %copy-start.12 = (f32[10]{0:T(128)S(1)}, f32[10]{0:T(128)}, u32[]{:S(2)}) copy-start(f32[10]{0:T(128)} %get-tuple-element.21) | copy-start | bytes 124
  12.7 3.5 %copy-start.13 = (f32[10]{0:T(128)S(1)}, f32[10]{0:T(128)}, u32[]{:S(2)}) copy-start(f32[10]{0:T(128)} %get-tuple-element.22) | copy-start | bytes 124
  12.8 3.5 %copy-start.14 = (f32[10]{0:T(128)S(1)}, f32[10]{0:T(128)}, u32[]{:S(2)}) copy-start(f32[10]{0:T(128)} %get-tuple-element.23) | copy-start | bytes 124
  12.8 3.5 %copy-start.15 = (f32[10]{0:T(128)S(1)}, f32[10]{0:T(128)}, u32[]{:S(2)}) copy-start(f32[10]{0:T(128)} %get-tuple-element.24) | copy-start | bytes 124
  12.8 3.5 %copy-start.16 = (f32[10]{0:T(128)S(1)}, f32[10]{0:T(128)}, u32[]{:S(2)}) copy-start(f32[10]{0:T(128)} %get-tuple-element.25) | copy-start | bytes 124
  12.8 3.5 %copy-start.17 = (f32[10]{0:T(128)S(1)}, f32[10]{0:T(128)}, u32[]{:S(2)}) copy-start(f32[10]{0:T(128)} %get-tuple-element.26) | copy-start | bytes 124
  16.0 0.7 copy-start.11
  16.0 1.4 %copy-start.18 = (f32[4]{0:T(128)S(1)}, f32[4]{0:T(128)}, u32[]{:S(2)}) copy-start(f32[4]{0:T(128)} %pad.9.clone) | copy-start | bytes 52
  16.5 2.2 %copy-start.1 = (f32[4,256,256]{2,1,0:T(8,128)S(1)}, f32[4,256,256]{2,1,0:T(8,128)}, u32[]{:S(2)}) copy-start(f32[4,256,256]{2,1,0:T(8,128)} %fusion.28) | copy-start | bytes 3145732
  16.5 2.2 %copy-start.4 = (pred[256,256]{1,0:T(8,128)(4,1)S(1)}, pred[256,256]{1,0:T(8,128)(4,1)}, u32[]{:S(2)}) copy-start(pred[256,256]{1,0:T(8,128)(4,1)} %iota_compare_fusion.1) | copy-start | bytes 196612
  16.5 2.2 %copy-start.5 = (f32[10,4,256]{2,1,0:T(4,128)S(1)}, f32[10,4,256]{2,1,0:T(4,128)}, u32[]{:S(2)}) copy-start(f32[10,4,256]{2,1,0:T(4,128)} %get-tuple-element.38) | copy-start | bytes 122884
  16.5 2.2 %copy-start.19 = (f32[10]{0:T(128)S(1)}, f32[10]{0:T(128)}, u32[]{:S(2)}) copy-start(f32[10]{0:T(128)} %param.12) | copy-start | bytes 124
  22.8 1.3 copy-start.6

commit v9 on v7

--- a/solution.py
+++ b/solution.py
@@ -152,7 +152,8 @@
     heads_here = step_sizes.shape[0]
     tokens_here = step_sizes.shape[1]
     count = tokens_here // GROUP
-    channels = mixer_input.reshape(heads_here, HP, count, GROUP)
+    channels = mixer_input.reshape(heads_here, HP, tokens_here)
+    blocks = [channels[:, :, c * GROUP : (c + 1) * GROUP] for c in range(count)]
     log_decay = -(decay_rates[:, None] * step_sizes).reshape(heads_here, count, GROUP)
     steps_blocked = step_sizes.reshape(heads_here, count, GROUP)
     running = jnp.cumsum(log_decay, axis=2)
@@ -170,14 +171,16 @@
         gram[None] * jnp.exp(jnp.where(causal, gaps, 0.0)) * steps_blocked[:, :, None, :],
         0.0,
     ).astype(jnp.bfloat16)
-    inner = jnp.einsum("hcij,hpcj->hpci", mixing, channels, preferred_element_type=jnp.float32)
     tail_decay = jnp.exp(running[:, :, -1:] - running) * steps_blocked
     weighted_terms = (basis_in_blocked.astype(jnp.float32)[None] * tail_decay[:, :, :, None]).astype(
         jnp.bfloat16
     )
-    summaries = jnp.einsum(
-        "hcjn,hpcj->chnp", weighted_terms, channels, preferred_element_type=jnp.float32
-    )
+    summaries = [
+        jnp.einsum(
+            "hjn,hpj->hnp", weighted_terms[:, c], blocks[c], preferred_element_type=jnp.float32
+        )
+        for c in range(count)
+    ]
     block_sums = jnp.sum(log_decay, axis=2)
     block_cum = jnp.cumsum(block_sums, axis=1)
     log_prefix = block_cum - block_sums
@@ -191,14 +194,21 @@
             term = term + weight[:, None, None] * summaries[earlier]
         entering.append(term)
     final_state = entering[count]
-    entering = jnp.stack(entering[:count])
-    basis_out_wide = basis_out_blocked.astype(jnp.float32)
-    within = jnp.exp(running)[:, None]
-    direct = skip_gain[:, None, None, None] * channels.astype(jnp.float32)
-    from_local = jnp.einsum(
-        "cin,chnp->hpci", basis_out_wide, entering, precision=lax.Precision.HIGHEST
-    )
-    local = (inner + from_local * within + direct).astype(jnp.bfloat16)
+    within = jnp.exp(running)
+    pieces = []
+    for c in range(count):
+        inner = jnp.einsum(
+            "hij,hpj->hpi", mixing[:, c], blocks[c], preferred_element_type=jnp.float32
+        )
+        from_local = jnp.einsum(
+            "in,hnp->hpi",
+            basis_out_blocked[c].astype(jnp.float32),
+            entering[c],
+            precision=lax.Precision.HIGHEST,
+        )
+        direct = skip_gain[:, None, None] * blocks[c].astype(jnp.float32)
+        pieces.append(inner + from_local * within[:, c][:, None, :] + direct)
+    local = jnp.concatenate(pieces, axis=2).astype(jnp.bfloat16)
     scale = jnp.exp(running + log_prefix[:, :, None]).reshape(heads_here, tokens_here)
     scale_hi = scale.astype(jnp.bfloat16)
     scale_lo = (scale - scale_hi.astype(jnp.float32)).astype(jnp.bfloat16)

time: 131 us -> 142 us (1.084)
  other arithmetic: 8.26 us -> 19.8 us
    convert_element_type x0 -> x2, other arithmetic: none -> 5.77 us  [the longest x1 4.12 us: on_device(): mixing = jnp.where(causal, gram[None] * jnp.exp(jnp.where(causal, gaps, 0...]
    reshape x1 -> x0, local copies, waits for them, and re-layouts: 2.88 us -> none  [on_device(): channels = mixer_input.reshape(heads_here, HP, count, GROUP)]
    concatenate x1, other arithmetic: 1.37 us -> 3.77 us  [on_device(): jnp.concatenate([local.reshape(heads_here * HP, tokens_here), scale_hi, s...]
    another operation x6, local copies, waits for them, and re-layouts: 0.3 us -> 2.31 us
    reshape x1, local copies, waits for them, and re-layouts: 0.02 us -> 1.46 us  [on_device(): (decay_rates[:, None] * step_sizes).reshape(heads_here, count, GROUP)]
    dot_general x3 -> x12, matrix products: 8.47 us -> 7.73 us  [the longest x4 3.79 us: on_device(): jnp.einsum('hjn,hpj->hnp', weighted_terms[:, c], blocks[c], preferred_ele...]
  transfers between devices with their start and end apart: 1 -> 1, of which waited for: 1 -> 1; matrix products, arithmetic and copies ran while one was open for 1% -> 1% of each run, Pallas kernels for 61% -> 55%
where the time goes in v9:
time: 142 us
  Pallas kernels  91 us (64%)
  other arithmetic  19.8 us (14%)
  between operations  13.8 us (10%)
  matrix products  8.97 us (6%)
  local copies, waits for them, and re-layouts  6.86 us (5%)
    pallas_call x1, Pallas kernels, carry_in(): pl.pallas_call(functools.partial(scan_kernel, peers, names), out_shape=(j...  78.5 us
    pallas_call x1, Pallas kernels, tail(): pl.pallas_call(tail_kernel, out_shape=jax.ShapeDtypeStruct((features, tok...  12.5 us
    convert_element_type x1, other arithmetic, on_device(): mixing = jnp.where(causal, gram[None] * jnp.exp(jnp.where(causal, gaps, 0...  4.12 us
    dot_general x4, matrix products, on_device(): jnp.einsum('hjn,hpj->hnp', weighted_terms[:, c], blocks[c], preferred_ele...  3.79 us
    concatenate x1, other arithmetic, on_device(): jnp.concatenate([local.reshape(heads_here * HP, tokens_here), scale_hi, s...  3.77 us
  transfers between devices with their start and end apart: 1, of which 1 were waited for; matrix products, arithmetic and copies ran while one was open for 1% of the time, Pallas kernels for 55%

profile of v9, /device:TPU:1, one launch (start us, length us, event | category | flops | bytes accessed | tf_op | source)
XLA Modules:
  0.0 141.5 jit_solution(1433811074608559237)
XLA Ops:
  6.5 0.9 mul.204
  7.4 1.6 %fusion.60 = (f32[10,1024]{1,0:T(8,128)S(1)}, f32[10,1024]{1,0:T(8,128)}) fusion(f32[10,1024]{1,0:T(8,128)} %param.10, f32[10]{0:T(128)} %param.11), kind=kLoop, calls=%fused_computation.101 | loop fusion | flops 20480 | bytes 122920 | tf_op jit(solution)/shard_map/neg | solution.py:157
  9.0 2.3 %reduce-window.6 = f32[10,4,2,128]{3,0,1,2:T(8,128)S(1)} reduce-window(f32[10,4,2,128]{3,0,1,2:T(8,128)S(1)} %copy.39, f32[]{:T(128)} %constant.35.clone.1), window={size=1x1x1x128 pad=0_0x0_0x0_0x127_0}, to_apply=%region_0.0 | reduce-window | flops 1300480 | bytes 81924 | tf_op jit(solution)/shard_map/reduce-window
  12.0 0.6 exponential_multiply_fusion
  12.7 1.1 convert_element_type.42
  13.8 1.7 %multiply_convert_fusion = bf16[10,4,256,128]{3,2,0,1:T(8,128)(2,1)S(1)} fusion(f32[10,4,256]{2,0,1:T(8,128)S(1)} %copy.46, f32[4,256,128]{2,1,0:T(8,128)S(1)} %convert_element_type.42), kind=kLoop, calls=%fused_computation.1 | loop fusion | flops 2621440 | bytes 3186688 | tf_op jit(solution)/shard_map/convert_element_type | solution.py:175
  15.5 1.3 fusion.23
  17.0 1.0 fusion.21
  18.0 0.6 copy.41
  18.6 0.6 copy.43
  19.2 0.6 iota_compare_fusion.1
  19.9 1.4 %reduce_window_sum.44 = f32[10,1024]{1,0:T(8,128)} reshape(f32[10,4,2,128]{3,2,1,0:T(2,128)} %copy-done.7) | data formatting | bytes 81920 | tf_op jit(solution)/shard_map/reduce_window_sum
  21.3 1.5 %reshape.259 = f32[10,4,256]{2,1,0:T(4,128)} reshape(f32[10,1024]{1,0:T(8,128)} %get-tuple-element.31) | data formatting | bytes 81920 | tf_op jit(solution)/shard_map/reshape | solution.py:157
  22.8 0.9 reduce_sum.9
  23.6 0.6 neg.11
  24.2 0.8 reduce_window_sum.43
  25.1 0.9 exponential_reduce_fusion.4
  26.0 1.0 fusion.61
  27.0 1.2 fusion.63
  28.3 4.1 %select_convert_fusion = bf16[10,4,256,256]{3,2,0,1:T(8,128)(2,1)S(1)} fusion(f32[10,4,256]{2,0,1:T(8,128)} %copy.43, f32[10,4,256]{2,0,1:T(8,128)} %copy.41, f32[4,256,256]{2,1,0:T(8,128)S(1)} %fusion.63, pred[256,256]{1,0:T(8,128)(4,1)} %iota_compare_fusion.1), kind=kLoop, calls=%fused_computation | loop fusion | flops 15728640 | bytes 6438912 | tf_op jit(solution)/shard_map/convert_element_type | solution.py:173
  32.9 0.5 fusion.18
  33.4 0.5 convolution_multiply_fusion
  33.9 0.5 fusion.19
  34.5 0.5 convolution_multiply_fusion.2
  34.9 0.5 fusion.17
  35.9 0.5 fusion.16
  36.7 3.8 %maximum_maximum_fusion.after_ref = bf16[672,1024]{1,0:T(8,128)(2,1)} fusion(bf16[10,1024]{1,0:T(8,128)(2,1)S(1)} %get-tuple-element.33, bf16[10,1024]{1,0:T(8,128)(2,1)S(1)} %get-tuple-element.32, bf16[640,256]{1,0:T(8,128)(2,1)S(1)} %bitcast.142, bf16[640,256]{1,0:T(8,128)(2,1)S(1)} %bitcast.141, bf16[640,256]{1,0:T(8,128)(2,1)S(1)} %bitcast.143, ...), kind=kLoop, calls=%fused_computation.2 | loop fusion | flops 9633792 | bytes 2729280 | tf_op jit(solution)/shard_map/concatenate | solution.py:216
  40.5 1.3 fusion.20
  41.9 0.7 select_maximum_fusion.msg_ref
  42.6 78.5 %shard_map.73 = (f32[648,128]{1,0:T(8,128)}, bf16[8,640,128]{2,1,0:T(8,128)(2,1)}) custom-call(f32[648,128]{1,0:T(8,128)} %select_maximum_fusion.msg_ref, bf16[672,1024]{1,0:T(8,128)(2,1)} %maximum_maximum_fusion.after_ref), custom_call_target="tpu_custom_call" | custom-call | bytes 169869312 | tf_op jit(solution)/shard_map/pallas_call | solution.py:121
  121.1 1.1 all-gather.2.cloned.1.call-done.local_ref
  122.2 12.5 %shard_map.74 = bf16[320,1024]{1,0:T(8,128)(2,1)} custom-call(bf16[5376,1024]{1,0:T(8,128)(2,1)} %all-gather.2.cloned.1.call-done.local_ref, bf16[1024,128]{1,0:T(8,128)(2,1)} %basis_ref.1, bf16[5120,128]{1,0:T(8,128)(2,1)} %bitcast.150, bf16[320,5120]{1,0:T(8,128)(2,1)} %bitcast.149), custom_call_target="tpu_custom_call" | custom-call | flops 4697620480 | bytes 14942208 | tf_op jit(solution)/shard_map/pallas_call | solution.py:260
  (56 shorter events, 2.1 us)
Async XLA Ops:
  6.5 115.6 %all-gather.2.cloned.1.call-start = ((), (), s32[]{:S(2)}) async-start(), calls=%async_computation | async-start | bytes 12386304 | tf_op jit(solution)/shard_map/all_gather | solution.py:225
  7.4 5.3 %copy-start.8 = (f32[10,4,256]{2,1,0:T(4,128)}, f32[10,4,256]{2,1,0:T(4,128)S(1)}, u32[]{:S(2)}) copy-start(f32[10,4,256]{2,1,0:T(4,128)S(1)} %mul.204) | copy-start | bytes 122884
  11.6 1.0 copy-start.7
  11.7 1.0 copy-start.5
  12.7 4.1 %copy-start.1 = (bf16[640,1024]{1,0:T(8,128)(2,1)S(1)}, bf16[640,1024]{1,0:T(8,128)(2,1)}, u32[]{:S(2)}) copy-start(bf16[640,1024]{1,0:T(8,128)(2,1)} %param.9) | copy-start | bytes 3932164
  15.4 2.5 %copy-start.6 = (f32[10,4,256]{2,1,0:T(4,128)S(1)}, f32[10,4,256]{2,1,0:T(4,128)}, u32[]{:S(2)}) copy-start(f32[10,4,256]{2,1,0:T(4,128)} %copy-done.5) | copy-start | bytes 122884
  15.5 3.1 %copy-start.9 = (f32[10,4,256]{2,1,0:T(4,128)S(1)}, f32[10,4,256]{2,1,0:T(4,128)}, u32[]{:S(2)}) copy-start(f32[10,4,256]{2,1,0:T(4,128)} %copy-done.8) | copy-start | bytes 122884
  15.5 11.5 %copy-start.3 = (bf16[1024,128]{1,0:T(8,128)(2,1)S(1)}, bf16[1024,128]{1,0:T(8,128)(2,1)}, u32[]{:S(2)}) copy-start(bf16[1024,128]{1,0:T(8,128)(2,1)} %param.13) | copy-start | bytes 786436
  28.2 4.2 %copy-start.4 = (bf16[1024,128]{1,0:T(8,128)(2,1)S(1)}, bf16[1024,128]{1,0:T(8,128)(2,1)}, u32[]{:S(2)}) copy-start(bf16[1024,128]{1,0:T(8,128)(2,1)} %basis_ref.1) | copy-start | bytes 786436
  28.2 4.7 %copy-start.2 = (bf16[640,1024]{1,0:T(8,128)(2,1)S(1)}, bf16[640,1024]{1,0:T(8,128)(2,1)}, u32[]{:S(2)}) copy-start(bf16[640,1024]{1,0:T(8,128)(2,1)} %param.9) | copy-start | bytes 3932164
  28.3 4.7 %copy-start.14 = (f32[10]{0:T(128)S(1)}, f32[10]{0:T(128)}, u32[]{:S(2)}) copy-start(f32[10]{0:T(128)} %param.12) | copy-start | bytes 124
  32.4 1.0 copy-start
  35.5 1.1 copy-start.10
  36.4 4.1 %copy-start.11 = (f32[10]{0:T(128)S(1)}, f32[10]{0:T(128)}, u32[]{:S(2)}) copy-start(f32[10]{0:T(128)} %get-tuple-element.27) | copy-start | bytes 124
  36.4 4.1 %copy-start.12 = (f32[10]{0:T(128)S(1)}, f32[10]{0:T(128)}, u32[]{:S(2)}) copy-start(f32[10]{0:T(128)} %get-tuple-element.28) | copy-start | bytes 124
  36.4 4.1 %copy-start.13 = (f32[10]{0:T(128)S(1)}, f32[10]{0:T(128)}, u32[]{:S(2)}) copy-start(f32[10]{0:T(128)} %get-tuple-element.29) | copy-start | bytes 124
Sparse Core Ops, SparseCore 0:
  40.6 81.5 all-gather.1

commit v10 on v7

--- a/solution.py
+++ b/solution.py
@@ -12,7 +12,7 @@
 GROUP = 256
 
 
-def scan_kernel(peers, names, msg_ref, after_ref, out_ref, spread_ref, inc_ref, out_state, recv_state,
+def scan_kernel(peers, names, msg_ref, after_ref, scale_ref, out_ref, spread_ref, inc_ref, out_state, recv_state,
                 recv_decay, send_ref, send_sem, recv_sem, decay_send, decay_recv, spread_send, spread_recv):
     here = lax.axis_index("seq")
     grp_here = lax.axis_index("grp")
@@ -73,8 +73,9 @@
                 ref[part, :] = jnp.where(reached, decay[:, h:h + 1] * got + own, own)
             ref[rows:] = jnp.where(reached, ref[rows:] * recv_decay[r], ref[rows:])
 
-    send_ref[...] = out_ref[:rows].astype(send_ref.dtype)
-    spread_ref[grp_here] = out_ref[:rows].astype(spread_ref.dtype)
+    send_ref[:rows] = out_ref[:rows].astype(send_ref.dtype)
+    send_ref[rows:] = scale_ref[...]
+    spread_ref[grp_here] = send_ref[...]
     copies = []
     for offset in range(1, groups):
         copy = pltpu.make_async_remote_copy(
@@ -109,7 +110,7 @@
     return hops
 
 
-def carry_in(total_log, state_t, names, after):
+def carry_in(total_log, state_t, names, after, scale_packed):
     peers = lax.axis_size("seq")
     groups = lax.axis_size("grp")
     heads, width, lanes = state_t.shape
@@ -122,16 +123,20 @@
         functools.partial(scan_kernel, peers, names),
         out_shape=(
             jax.ShapeDtypeStruct(shape, jnp.float32),
-            jax.ShapeDtypeStruct((groups, rows, lanes), jnp.bfloat16),
+            jax.ShapeDtypeStruct((groups, rows + scale_packed.shape[0], lanes), jnp.bfloat16),
         ),
-        in_specs=[pl.BlockSpec(memory_space=pltpu.VMEM), pl.BlockSpec(memory_space=pl.ANY)],
+        in_specs=[
+            pl.BlockSpec(memory_space=pltpu.VMEM),
+            pl.BlockSpec(memory_space=pl.ANY),
+            pl.BlockSpec(memory_space=pltpu.VMEM),
+        ],
         out_specs=(pl.BlockSpec(memory_space=pltpu.VMEM), pl.BlockSpec(memory_space=pltpu.VMEM)),
         scratch_shapes=[
             pltpu.VMEM(shape, jnp.float32),
             pltpu.VMEM((hops, rows, lanes), jnp.bfloat16),
             pltpu.VMEM((hops, rows, lanes), jnp.bfloat16),
             pltpu.VMEM((hops, 8, lanes), jnp.float32),
-            pltpu.VMEM((rows, lanes), jnp.bfloat16),
+            pltpu.VMEM((rows + scale_packed.shape[0], lanes), jnp.bfloat16),
             pltpu.SemaphoreType.DMA((hops,)),
             pltpu.SemaphoreType.DMA((hops,)),
             pltpu.SemaphoreType.DMA((hops,)),
@@ -141,8 +146,8 @@
         ],
         compiler_params=pltpu.CompilerParams(collective_id=0, has_side_effects=True),
         cost_estimate=pl.CostEstimate(flops=0, transcendentals=0, bytes_accessed=512 * msg.size * 4),
-    )(msg, after)
-    return spread.reshape(groups * rows, lanes)
+    )(msg, after, scale_packed)
+    return spread
 
 
 def on_device(
@@ -202,23 +207,19 @@
     scale = jnp.exp(running + log_prefix[:, :, None]).reshape(heads_here, tokens_here)
     scale_hi = scale.astype(jnp.bfloat16)
     scale_lo = (scale - scale_hi.astype(jnp.float32)).astype(jnp.bfloat16)
-    extra = 32 - 2 * heads_here
-    local_ext = jnp.concatenate(
-        [
-            local.reshape(heads_here * HP, tokens_here),
-            scale_hi,
-            scale_lo,
-            jnp.zeros((extra, tokens_here), jnp.bfloat16),
-        ],
-        axis=0,
-    )
-    local_all = lax.all_gather(local_ext, "grp", axis=0, tiled=True)
-    carried_t = carry_in(total_log, jnp.swapaxes(final_state, 1, 2), names, local_ext)
-    result_t = tail(local_all, output_basis, carried_t, out_weight.T)
+    scale_rows = jnp.concatenate([scale_hi, scale_lo], axis=0)
+    scale_packed = scale_rows.reshape(-1, 128)
+    local_flat = local.reshape(heads_here * HP, tokens_here)
+    local_all = lax.all_gather(local_flat, "grp", axis=0, tiled=True)
+    spread = carry_in(total_log, jnp.swapaxes(final_state, 1, 2), names, local_flat, scale_packed)
+    groups = spread.shape[0]
+    carried_t = spread[:, : heads_here * HP].reshape(groups * heads_here * HP, N)
+    scale_all = spread[:, heads_here * HP :].reshape(groups, 2 * heads_here, tokens_here)
+    result_t = tail(local_all, output_basis, carried_t, scale_all, out_weight.T)
     return result_t.T
 
 
-def tail_kernel(local_ref, basis_ref, carried_ref, weight_ref, out_ref, acc_ref, mixed_ref):
+def tail_kernel(local_ref, basis_ref, carried_ref, scale_ref, weight_ref, out_ref, acc_ref, mixed_ref):
     g = pl.program_id(0)
 
     @pl.when(g == 0)
@@ -230,8 +231,8 @@
     carry = lax.dot_general(
         carried_ref[...], basis_ref[...], (((1,), (1,)), ((), ())), preferred_element_type=jnp.float32
     )
-    scale = local_ref[pl.ds(base, per), :].astype(jnp.float32) + local_ref[
-        pl.ds(base + per, per), :
+    scale = scale_ref[pl.ds(0, per), :].astype(jnp.float32) + scale_ref[
+        pl.ds(per, per), :
     ].astype(jnp.float32)
     carry = (carry.reshape(per, HP, tokens) * scale[:, None, :]).reshape(base, tokens)
     mixed_ref[...] = (local_ref[pl.ds(0, base), :].astype(jnp.float32) + carry).astype(jnp.bfloat16)
@@ -242,7 +243,7 @@
         out_ref[...] = acc_ref[...].astype(out_ref.dtype)
 
 
-def tail(local_all, basis, carried_t, weight_t):
+def tail(local_all, basis, carried_t, scale_all, weight_t):
     channels, tokens = local_all.shape
     features = weight_t.shape[0]
     groups = lax.axis_size("grp")
@@ -255,6 +256,7 @@
             pl.BlockSpec((channels // groups, tokens), lambda g: (g, 0)),
             pl.BlockSpec(basis.shape, lambda g: (0, 0)),
             pl.BlockSpec((per * HP, N), lambda g: (g, 0)),
+            pl.BlockSpec((None, 2 * per, tokens), lambda g: (g, 0, 0)),
             pl.BlockSpec((features, per * HP), lambda g: (0, g)),
         ],
         out_specs=pl.BlockSpec((features, tokens), lambda g: (0, 0)),
@@ -267,7 +269,7 @@
             transcendentals=0,
             bytes_accessed=2 * (local_all.size + weight_t.size) + 2 * features * tokens,
         ),
-    )(local_all, basis, carried_t, weight_t)
+    )(local_all, basis, carried_t, scale_all, weight_t)
 
 
 def solution(mesh):

time: 131 us -> 136 us (1.038)
  local copies, waits for them, and re-layouts: 6.6 us -> 12.7 us
  other arithmetic: 8.26 us -> 6.86 us
    slice x0 -> x2, local copies, waits for them, and re-layouts: none -> 3.47 us  [the longest x1 2.48 us: on_device(): carried_t = spread[:, :heads_here * HP].reshape(groups * heads_here * HP, N)]
    reshape x0 -> x2, local copies, waits for them, and re-layouts: none -> 1.62 us  [the longest x1 0.97 us: on_device(): spread[:, heads_here * HP:].reshape(groups, 2 * heads_here, tokens_here)]
  transfers between devices with their start and end apart: 1 -> 1, of which waited for: 1 -> 0; matrix products, arithmetic and copies ran while one was open for 1% -> 5% of each run, Pallas kernels for 61% -> 60%
where the time goes in v10:
time: 136 us
  Pallas kernels  93.6 us (69%)
  between operations  13.7 us (10%)
  local copies, waits for them, and re-layouts  12.7 us (9%)
  matrix products  8.77 us (6%)
  other arithmetic  6.86 us (5%)
    pallas_call x1, Pallas kernels, carry_in(): pl.pallas_call(functools.partial(scan_kernel, peers, names), out_shape=(j...  80.7 us
    pallas_call x1, Pallas kernels, tail(): pl.pallas_call(tail_kernel, out_shape=jax.ShapeDtypeStruct((features, tok...  12.9 us
    dot_general x1, matrix products, on_device(): jnp.einsum('hcij,hpcj->hpci', mixing, channels, preferred_element_type=jn...  4.01 us
    dot_general x1, matrix products, on_device(): jnp.einsum('hcjn,hpcj->chnp', weighted_terms, channels, preferred_element...  3.2 us
    reshape x1, local copies, waits for them, and re-layouts, on_device(): channels = mixer_input.reshape(heads_here, HP, count, GROUP)  2.88 us
  transfers between devices with their start and end apart: 1, of which 0 were waited for; matrix products, arithmetic and copies ran while one was open for 5% of the time, Pallas kernels for 60%

profile of v10, /device:TPU:1, one launch (start us, length us, event | category | flops | bytes accessed | tf_op | source)
XLA Modules:
  0.0 135.6 jit_solution(14832572444437309018)
XLA Ops:
  6.5 0.6 iota_compare_fusion.1
  7.2 0.9 mul.152
  8.0 0.9 fusion.25
  9.0 2.3 %reduce-window.6 = f32[10,4,2,128]{3,0,1,2:T(8,128)S(1)} reduce-window(f32[10,4,2,128]{3,0,1,2:T(8,128)S(1)} %copy.41, f32[]{:T(128)} %constant.34.clone.1), window={size=1x1x1x128 pad=0_0x0_0x0_0x127_0}, to_apply=%region_0.0 | reduce-window | flops 1300480 | bytes 81924 | tf_op jit(solution)/shard_map/reduce-window
  11.3 0.2 slice_reduce_fusion
  11.5 0.1 broadcast_add_fusion
  11.7 0.1 slice.97
  11.8 0.1 copy.44
  11.9 0.1 copy.45
  12.0 0.6 fusion.26
  12.6 0.6 copy.46
  13.3 2.9 %reshape.260 = bf16[10,64,4,256]{3,2,1,0:T(4,128)(2,1)S(1)} reshape(bf16[640,1024]{1,0:T(8,128)(2,1)} %param.9) | data formatting | bytes 2621440 | tf_op jit(solution)/shard_map/reshape | solution.py:160
  16.2 0.1 reduce_sum.9
  16.3 0.2 reduce_window_sum.47
  16.5 0.9 exponential_reduce_fusion.4
  17.4 0.3 fusion.28
  17.7 3.2 %fusion.7 = f32[4,10,128,64]{2,3,1,0:T(8,128)S(1)} fusion(f32[10,4,256]{2,0,1:T(8,128)} %copy.46, f32[4,256,128]{2,1,0:T(8,128)S(1)} %convert_element_type.30, bf16[10,64,4,256]{3,2,1,0:T(4,128)(2,1)S(1)} %reshape.260), kind=kOutput, calls=%fused_computation.9 | convolution fusion | flops 170393600 | bytes 3186688 | tf_op jit(solution)/shard_map/hcjn,hpcj->chnp/dot_general | solution.py:183
  20.9 0.2 slice_multiply_fusion
  21.1 1.3 fusion.13
  22.4 4.0 %fusion.10 = bf16[10,64,4,256]{3,1,2,0:T(8,128)(2,1)S(1)} fusion(f32[4,10,64,256]{3,2,0,1:T(8,128)S(1)} %fusion.13, f32[10,4,256]{2,1,0:T(4,128)S(1)} %mul.152, f32[10,4,256]{2,1,0:T(4,128)S(1)} %reduce_window_sum.46, f32[4,256,256]{2,1,0:T(8,128)S(1)} %fusion.28, pred[256,256]{1,0:T(8,128)(4,1)S(1)} %copy-done.2, ...), kind=kOutput, calls=%fused_computation.13 | convolution fusion | flops 355205120 | bytes 6479912 | tf_op jit(solution)/shard_map/hcij,hpcj->hpci/dot_general | solution.py:178
  26.4 1.0 copy.50
  27.5 1.4 %copy.52 = bf16[80,8,4,256]{3,1,2,0:T(8,128)(2,1)} copy(bf16[80,8,4,256]{3,2,1,0:T(4,128)(2,1)S(1)} %bitcast.57) | data formatting | bytes 2621440
  28.9 0.0 all-gather.2.cloned.1.call-update
  29.0 0.1 add.50
  29.1 0.7 reshape.264.scale_ref
  29.8 0.2 fusion.18
  30.0 0.7 select_maximum_fusion.msg_ref
  30.7 80.7 %shard_map.73 = (f32[648,128]{1,0:T(8,128)}, bf16[8,800,128]{2,1,0:T(8,128)(2,1)}) custom-call(f32[648,128]{1,0:T(8,128)} %select_maximum_fusion.msg_ref, bf16[640,1024]{1,0:T(8,128)(2,1)} %bitcast.56, bf16[160,128]{1,0:T(8,128)(2,1)} %reshape.264.scale_ref), custom_call_target="tpu_custom_call" | custom-call | bytes 169869312 | tf_op jit(solution)/shard_map/pallas_call | solution.py:122
  111.4 2.5 %slice.91 = bf16[8,640,128]{2,1,0:T(8,128)(2,1)} slice(bf16[8,800,128]{2,1,0:T(8,128)(2,1)} %get-tuple-element.18), slice={[0:8], [0:640], [0:128]} | slice | bytes 2621440 | tf_op jit(solution)/shard_map/slice | solution.py:216
  113.9 1.0 slice.92
  114.9 1.0 reshape.266.scale_ref
  115.9 12.9 %shard_map.74 = bf16[320,1024]{1,0:T(8,128)(2,1)} custom-call(bf16[5120,1024]{1,0:T(8,128)(2,1)} %all-gather.2.cloned.1.call-done.local_ref, bf16[1024,128]{1,0:T(8,128)(2,1)} %basis_ref.1, bf16[5120,128]{1,0:T(8,128)(2,1)} %bitcast.58, bf16[8,20,1024]{2,1,0:T(8,128)(2,1)} %reshape.266.scale_ref, bf16[320,5120]{1,0:T(8,128)(2,1)} %bitcast.68), custom_call_target="tpu_custom_call" | custom-call | flops 4697620480 | bytes 14417920 | tf_op jit(solution)/shard_map/pallas_call | solution.py:251
  (30 shorter events, 0.3 us)
Async XLA Ops:
  6.5 9.6 %copy-start = (bf16[1024,128]{1,0:T(8,128)(2,1)S(1)}, bf16[1024,128]{1,0:T(8,128)(2,1)}, u32[]{:S(2)}) copy-start(bf16[1024,128]{1,0:T(8,128)(2,1)} %param.13) | copy-start | bytes 786436
  6.5 10.8 %copy-start.1 = (bf16[1024,128]{1,0:T(8,128)(2,1)S(1)}, bf16[1024,128]{1,0:T(8,128)(2,1)}, u32[]{:S(2)}) copy-start(bf16[1024,128]{1,0:T(8,128)(2,1)} %basis_ref.1) | copy-start | bytes 786436
  6.5 109.3 %all-gather.2.cloned.1.call-start = ((), (), s32[]{:S(2)}) async-start(), calls=%async_computation | async-start | bytes 11796480 | tf_op jit(solution)/shard_map/all_gather | solution.py:213
  20.9 1.5 %copy-start.2 = (pred[256,256]{1,0:T(8,128)(4,1)S(1)}, pred[256,256]{1,0:T(8,128)(4,1)}, u32[]{:S(2)}) copy-start(pred[256,256]{1,0:T(8,128)(4,1)} %iota_compare_fusion.1) | copy-start | bytes 196612
  20.9 1.5 %copy-start.3 = (f32[10,4,256]{2,1,0:T(4,128)S(1)}, f32[10,4,256]{2,1,0:T(4,128)}, u32[]{:S(2)}) copy-start(f32[10,4,256]{2,1,0:T(4,128)} %get-tuple-element.37) | copy-start | bytes 122884
  20.9 1.5 %copy-start.5 = (f32[10]{0:T(128)S(1)}, f32[10]{0:T(128)}, u32[]{:S(2)}) copy-start(f32[10]{0:T(128)} %param.12) | copy-start | bytes 124
  27.5 2.5 %copy-start.4 = (f32[10]{0:T(128)S(1)}, f32[10]{0:T(128)}, u32[]{:S(2)}) copy-start(f32[10]{0:T(128)} %get-tuple-element.26) | copy-start | bytes 124
Sparse Core Ops, SparseCore 0:
  29.0 78.9 all-gather.1

commit v11 on v10

--- a/solution.py
+++ b/solution.py
@@ -212,10 +212,7 @@
     local_flat = local.reshape(heads_here * HP, tokens_here)
     local_all = lax.all_gather(local_flat, "grp", axis=0, tiled=True)
     spread = carry_in(total_log, jnp.swapaxes(final_state, 1, 2), names, local_flat, scale_packed)
-    groups = spread.shape[0]
-    carried_t = spread[:, : heads_here * HP].reshape(groups * heads_here * HP, N)
-    scale_all = spread[:, heads_here * HP :].reshape(groups, 2 * heads_here, tokens_here)
-    result_t = tail(local_all, output_basis, carried_t, scale_all, out_weight.T)
+    result_t = tail(local_all, output_basis, spread, out_weight.T)
     return result_t.T
 
 
@@ -228,14 +225,19 @@
 
     base, tokens = mixed_ref.shape
     per = base // HP
+    tiles = tokens // 128
     carry = lax.dot_general(
         carried_ref[...], basis_ref[...], (((1,), (1,)), ((), ())), preferred_element_type=jnp.float32
     )
-    scale = scale_ref[pl.ds(0, per), :].astype(jnp.float32) + scale_ref[
-        pl.ds(per, per), :
-    ].astype(jnp.float32)
-    carry = (carry.reshape(per, HP, tokens) * scale[:, None, :]).reshape(base, tokens)
-    mixed_ref[...] = (local_ref[pl.ds(0, base), :].astype(jnp.float32) + carry).astype(jnp.bfloat16)
+    for h in range(per):
+        for k in range(tiles):
+            rows, lanes = slice(h * HP, (h + 1) * HP), slice(k * 128, (k + 1) * 128)
+            scale = scale_ref[pl.ds(h * tiles + k, 1), :].astype(jnp.float32) + scale_ref[
+                pl.ds((per + h) * tiles + k, 1), :
+            ].astype(jnp.float32)
+            mixed_ref[rows, lanes] = (
+                local_ref[rows, lanes].astype(jnp.float32) + carry[rows, lanes] * scale
+            ).astype(jnp.bfloat16)
     acc_ref[...] += jnp.dot(weight_ref[...], mixed_ref[...], preferred_element_type=jnp.float32)
 
     @pl.when(g == pl.num_programs(0) - 1)
@@ -243,11 +245,12 @@
         out_ref[...] = acc_ref[...].astype(out_ref.dtype)
 
 
-def tail(local_all, basis, carried_t, scale_all, weight_t):
+def tail(local_all, basis, spread, weight_t):
     channels, tokens = local_all.shape
     features = weight_t.shape[0]
     groups = lax.axis_size("grp")
-    per = carried_t.shape[0] // groups // HP
+    per = channels // groups // HP
+    packed = 2 * per * tokens // 128
     return pl.pallas_call(
         tail_kernel,
         out_shape=jax.ShapeDtypeStruct((features, tokens), jnp.bfloat16),
@@ -255,8 +258,8 @@
         in_specs=[
             pl.BlockSpec((channels // groups, tokens), lambda g: (g, 0)),
             pl.BlockSpec(basis.shape, lambda g: (0, 0)),
-            pl.BlockSpec((per * HP, N), lambda g: (g, 0)),
-            pl.BlockSpec((None, 2 * per, tokens), lambda g: (g, 0, 0)),
+            pl.BlockSpec((None, per * HP, N), lambda g: (g, 0, 0)),
+            pl.BlockSpec((None, packed, N), lambda g: (g, per * HP // packed, 0)),
             pl.BlockSpec((features, per * HP), lambda g: (0, g)),
         ],
         out_specs=pl.BlockSpec((features, tokens), lambda g: (0, 0)),
@@ -269,7 +272,7 @@
             transcendentals=0,
             bytes_accessed=2 * (local_all.size + weight_t.size) + 2 * features * tokens,
         ),
-    )(local_all, basis, carried_t, scale_all, weight_t)
+    )(local_all, basis, spread, spread, weight_t)
 
 
 def solution(mesh):

time: 136 us -> 132 us (0.971)
  local copies, waits for them, and re-layouts: 12.7 us -> 8.2 us
    slice x2 -> x0, local copies, waits for them, and re-layouts: 3.47 us -> none  [the longest x1 2.48 us: on_device(): carried_t = spread[:, :heads_here * HP].reshape(groups * heads_here * HP, N)]
  transfers between devices with their start and end apart: 1 -> 1, of which waited for: 0 -> 0; matrix products, arithmetic and copies ran while one was open for 5% -> 1% of each run, Pallas kernels for 60% -> 62%
where the time goes in v11:
time: 132 us; the launch traced here: 131 us
  Pallas kernels  93.6 us (71%)
  between operations  13.7 us (10%)
  matrix products  8.75 us (7%)
  local copies, waits for them, and re-layouts  8.2 us (6%)
  other arithmetic  6.89 us (5%)
    pallas_call x1, Pallas kernels, carry_in(): pl.pallas_call(functools.partial(scan_kernel, peers, names), out_shape=(j...  80.8 us
    pallas_call x1, Pallas kernels, tail(): pl.pallas_call(tail_kernel, out_shape=jax.ShapeDtypeStruct((features, tok...  12.7 us
    dot_general x1, matrix products, on_device(): jnp.einsum('hcij,hpcj->hpci', mixing, channels, preferred_element_type=jn...  3.99 us
    dot_general x1, matrix products, on_device(): jnp.einsum('hcjn,hpcj->chnp', weighted_terms, channels, preferred_element...  3.19 us
    reshape x1, local copies, waits for them, and re-layouts, on_device(): channels = mixer_input.reshape(heads_here, HP, count, GROUP)  2.88 us
  transfers between devices with their start and end apart: 1, of which 0 were waited for; matrix products, arithmetic and copies ran while one was open for 1% of the time, Pallas kernels for 62%

profile of v11, /device:TPU:1, one launch (start us, length us, event | category | flops | bytes accessed | tf_op | source)
XLA Modules:
  0.0 131.1 jit_solution(1033375971636624915)
XLA Ops:
  6.5 0.6 iota_compare_fusion.1
  7.2 0.9 mul.152
  8.0 0.9 fusion.25
  9.0 2.3 %reduce-window.6 = f32[10,4,2,128]{3,0,1,2:T(8,128)S(1)} reduce-window(f32[10,4,2,128]{3,0,1,2:T(8,128)S(1)} %copy.41, f32[]{:T(128)} %constant.34.clone.1), window={size=1x1x1x128 pad=0_0x0_0x0_0x127_0}, to_apply=%region_0.0 | reduce-window | flops 1300480 | bytes 81924 | tf_op jit(solution)/shard_map/reduce-window
  11.3 0.2 slice_reduce_fusion
  11.5 0.1 broadcast_add_fusion
  11.7 0.1 slice.89
  11.8 0.1 copy.44
  11.9 0.1 copy.45
  12.0 0.6 fusion.26
  12.6 0.6 copy.46
  13.3 2.9 %reshape.254 = bf16[10,64,4,256]{3,2,1,0:T(4,128)(2,1)S(1)} reshape(bf16[640,1024]{1,0:T(8,128)(2,1)} %param.9) | data formatting | bytes 2621440 | tf_op jit(solution)/shard_map/reshape | solution.py:160
  16.2 0.0 copy-done.1
  16.2 0.1 reduce_sum.9
  16.3 0.2 reduce_window_sum.47
  16.5 0.9 exponential_reduce_fusion.4
  17.4 0.3 fusion.28
  17.7 3.2 %fusion.7 = f32[4,10,128,64]{2,3,1,0:T(8,128)S(1)} fusion(f32[10,4,256]{2,0,1:T(8,128)} %copy.46, f32[4,256,128]{2,1,0:T(8,128)S(1)} %convert_element_type.30, bf16[10,64,4,256]{3,2,1,0:T(4,128)(2,1)S(1)} %reshape.254), kind=kOutput, calls=%fused_computation.9 | convolution fusion | flops 170393600 | bytes 3186688 | tf_op jit(solution)/shard_map/hcjn,hpcj->chnp/dot_general | solution.py:183
  20.9 0.0 copy-start.5
  20.9 0.2 slice_multiply_fusion
  21.1 1.3 fusion.13
  22.5 4.0 %fusion.10 = bf16[10,64,4,256]{3,1,2,0:T(8,128)(2,1)S(1)} fusion(f32[4,10,64,256]{3,2,0,1:T(8,128)S(1)} %fusion.13, f32[10,4,256]{2,1,0:T(4,128)S(1)} %mul.152, f32[10,4,256]{2,1,0:T(4,128)S(1)} %reduce_window_sum.46, f32[4,256,256]{2,1,0:T(8,128)S(1)} %fusion.28, pred[256,256]{1,0:T(8,128)(4,1)S(1)} %copy-done.2, ...), kind=kOutput, calls=%fused_computation.13 | convolution fusion | flops 355205120 | bytes 6479912 | tf_op jit(solution)/shard_map/hcij,hpcj->hpci/dot_general | solution.py:178
  26.5 1.0 copy.50
  27.5 1.4 %copy.52 = bf16[80,8,4,256]{3,1,2,0:T(8,128)(2,1)} copy(bf16[80,8,4,256]{3,2,1,0:T(4,128)(2,1)S(1)} %bitcast.56) | data formatting | bytes 2621440
  28.9 0.0 all-gather.2.cloned.1.call-update
  28.9 0.1 add.50
  29.1 0.7 reshape.258.scale_ref
  29.7 0.2 fusion.18
  29.9 0.7 select_maximum_fusion.msg_ref
  30.7 80.8 %shard_map.73 = (f32[648,128]{1,0:T(8,128)}, bf16[8,800,128]{2,1,0:T(8,128)(2,1)}) custom-call(f32[648,128]{1,0:T(8,128)} %select_maximum_fusion.msg_ref, bf16[640,1024]{1,0:T(8,128)(2,1)} %bitcast.55, bf16[160,128]{1,0:T(8,128)(2,1)} %reshape.258.scale_ref), custom_call_target="tpu_custom_call" | custom-call | bytes 169869312 | tf_op jit(solution)/shard_map/pallas_call | solution.py:122
  111.5 0.0 all-gather.2.cloned.1.call-done.local_ref
  111.5 12.7 %shard_map.74 = bf16[320,1024]{1,0:T(8,128)(2,1)} custom-call(bf16[5120,1024]{1,0:T(8,128)(2,1)} %all-gather.2.cloned.1.call-done.local_ref, bf16[1024,128]{1,0:T(8,128)(2,1)} %basis_ref.1, bf16[8,800,128]{2,1,0:T(8,128)(2,1)} %get-tuple-element.18.carried_ref.scale_ref, bf16[8,800,128]{2,1,0:T(8,128)(2,1)} %get-tuple-element.18.carried_ref.scale_ref, ...), custom_call_target="tpu_custom_call" | custom-call | flops 4697620480 | bytes 14417920 | tf_op jit(solution)/shard_map/pallas_call | solution.py:254
  (27 shorter events, 0.3 us)
Async XLA Ops:
  6.5 9.6 %copy-start.1 = (bf16[1024,128]{1,0:T(8,128)(2,1)S(1)}, bf16[1024,128]{1,0:T(8,128)(2,1)}, u32[]{:S(2)}) copy-start(bf16[1024,128]{1,0:T(8,128)(2,1)} %param.13) | copy-start | bytes 786436
  6.5 10.9 %copy-start = (bf16[1024,128]{1,0:T(8,128)(2,1)S(1)}, bf16[1024,128]{1,0:T(8,128)(2,1)}, u32[]{:S(2)}) copy-start(bf16[1024,128]{1,0:T(8,128)(2,1)} %basis_ref.1) | copy-start | bytes 786436
  6.5 105.0 %all-gather.2.cloned.1.call-start = ((), (), s32[]{:S(2)}) async-start(), calls=%async_computation | async-start | bytes 11796480 | tf_op jit(solution)/shard_map/all_gather | solution.py:213
  20.9 1.5 %copy-start.2 = (pred[256,256]{1,0:T(8,128)(4,1)S(1)}, pred[256,256]{1,0:T(8,128)(4,1)}, u32[]{:S(2)}) copy-start(pred[256,256]{1,0:T(8,128)(4,1)} %iota_compare_fusion.1) | copy-start | bytes 196612
  20.9 1.5 %copy-start.3 = (f32[10,4,256]{2,1,0:T(4,128)S(1)}, f32[10,4,256]{2,1,0:T(4,128)}, u32[]{:S(2)}) copy-start(f32[10,4,256]{2,1,0:T(4,128)} %get-tuple-element.37) | copy-start | bytes 122884
  20.9 1.5 %copy-start.5 = (f32[10]{0:T(128)S(1)}, f32[10]{0:T(128)}, u32[]{:S(2)}) copy-start(f32[10]{0:T(128)} %param.12) | copy-start | bytes 124
  27.5 2.4 %copy-start.4 = (f32[10]{0:T(128)S(1)}, f32[10]{0:T(128)}, u32[]{:S(2)}) copy-start(f32[10]{0:T(128)} %get-tuple-element.26) | copy-start | bytes 124
Sparse Core Ops, SparseCore 0:
  29.0 78.9 all-gather.1

commit v12 on v7

--- a/solution.py
+++ b/solution.py
@@ -75,30 +75,47 @@
 
     send_ref[...] = out_ref[:rows].astype(send_ref.dtype)
     spread_ref[grp_here] = out_ref[:rows].astype(spread_ref.dtype)
-    copies = []
-    for offset in range(1, groups):
-        copy = pltpu.make_async_remote_copy(
+    partner = grp_here + 1 - 2 * lax.rem(grp_here, 2)
+
+    def spread_copy(slot, target, sem):
+        return pltpu.make_async_remote_copy(
+            src_ref=send_ref if slot is None else spread_ref.at[slot],
+            dst_ref=spread_ref.at[grp_here if slot is None else slot],
+            send_sem=sem,
+            recv_sem=spread_recv.at[grp_here if slot is None else slot],
+            device_id=device(here, target),
+            device_id_type=pl.DeviceIdType.MESH,
+        )
+
+    def arriving(slot, source):
+        return pltpu.make_async_remote_copy(
             src_ref=send_ref,
-            dst_ref=spread_ref.at[grp_here],
-            send_sem=spread_send.at[offset],
-            recv_sem=spread_recv.at[grp_here],
-            device_id=device(here, lax.rem(grp_here + offset, groups)),
-            device_id_type=pl.DeviceIdType.MESH,
-        )
+            dst_ref=spread_ref.at[slot],
+            send_sem=spread_send.at[0],
+            recv_sem=spread_recv.at[slot],
+            device_id=device(here, source),
+            device_id_type=pl.DeviceIdType.MESH,
+        )
+
+    chips = groups // 2
+    copies = [spread_copy(None, partner, spread_send.at[0])]
+    for k in range(1, chips):
+        copies.append(spread_copy(None, lax.rem(grp_here + 2 * k, groups), spread_send.at[k]))
+    for copy in copies:
         copy.start()
-        copies.append(copy)
-    for copy in copies:
+    arriving(partner, partner).wait_recv()
+    forwards = []
+    for k in range(1, chips):
+        source = lax.rem(grp_here + groups - 2 * k, groups)
+        arriving(source, source).wait_recv()
+        forward = spread_copy(source, partner, spread_send.at[chips - 1 + k])
+        forward.start()
+        forwards.append(forward)
+    for k in range(1, chips):
+        slot = lax.rem(partner + groups - 2 * k, groups)
+        arriving(slot, partner).wait_recv()
+    for copy in copies + forwards:
         copy.wait_send()
-    for offset in range(1, groups):
-        source = lax.rem(grp_here + groups - offset, groups)
-        pltpu.make_async_remote_copy(
-            src_ref=send_ref,
-            dst_ref=spread_ref.at[source],
-            send_sem=spread_send.at[offset],
-            recv_sem=spread_recv.at[source],
-            device_id=device(here, source),
-            device_id_type=pl.DeviceIdType.MESH,
-        ).wait_recv()
 
 
 def _hops(peers):

time: 131 us -> 124 us (0.947)
  Pallas kernels: 92.3 us -> 79.5 us
  waiting for transfers between devices: 0.91 us -> 6.65 us
    pallas_call x1, Pallas kernels: 79.8 us -> 67 us  [carry_in(): pl.pallas_call(functools.partial(scan_kernel, peers, names), out_shape=(j...]
    all_gather x1, waiting for transfers between devices: 0.9 us -> 6.63 us  [on_device(): local_all = lax.all_gather(local_ext, 'grp', axis=0, tiled=True)]
  transfers between devices with their start and end apart: 1 -> 1, of which waited for: 1 -> 1; matrix products, arithmetic and copies ran while one was open for 1% -> 1% of each run, Pallas kernels for 61% -> 54%
where the time goes in v12:
time: 124 us
  Pallas kernels  79.5 us (64%)
  between operations  13.7 us (11%)
  matrix products  8.76 us (7%)
  other arithmetic  8.26 us (7%)
  waiting for transfers between devices  6.65 us (5%)
  local copies, waits for them, and re-layouts  6.6 us (5%)
    pallas_call x1, Pallas kernels, carry_in(): pl.pallas_call(functools.partial(scan_kernel, peers, names), out_shape=(j...  67 us
    pallas_call x1, Pallas kernels, tail(): pl.pallas_call(tail_kernel, out_shape=jax.ShapeDtypeStruct((features, tok...  12.5 us
    all_gather x1, waiting for transfers between devices, on_device(): local_all = lax.all_gather(local_ext, 'grp', axis=0, tiled=True)  6.63 us
    dot_general x1, matrix products, on_device(): jnp.einsum('hcij,hpcj->hpci', mixing, channels, preferred_element_type=jn...  4 us
    dot_general x1, matrix products, on_device(): jnp.einsum('hcjn,hpcj->chnp', weighted_terms, channels, preferred_element...  3.2 us
    reshape x1, local copies, waits for them, and re-layouts, on_device(): channels = mixer_input.reshape(heads_here, HP, count, GROUP)  2.88 us
  transfers between devices with their start and end apart: 1, of which 1 were waited for; matrix products, arithmetic and copies ran while one was open for 1% of the time, Pallas kernels for 54%

profile of v12, /device:TPU:1, one launch (start us, length us, event | category | flops | bytes accessed | tf_op | source)
XLA Modules:
  0.0 123.5 jit_solution(11959889288850949971)
XLA Ops:
  6.5 0.6 iota_compare_fusion.1
  7.2 0.9 mul.152
  8.1 0.9 fusion.25
  9.1 2.3 %reduce-window.6 = f32[10,4,2,128]{3,0,1,2:T(8,128)S(1)} reduce-window(f32[10,4,2,128]{3,0,1,2:T(8,128)S(1)} %copy.42, f32[]{:T(128)} %constant.35.clone.1), window={size=1x1x1x128 pad=0_0x0_0x0_0x127_0}, to_apply=%region_0.0 | reduce-window | flops 1300480 | bytes 81924 | tf_op jit(solution)/shard_map/reduce-window
  11.4 0.2 slice_reduce_fusion
  11.6 0.1 broadcast_add_fusion
  11.8 0.1 slice.89
  11.9 0.1 copy.45
  12.0 0.1 copy.46
  12.1 0.6 fusion.26
  12.7 0.6 copy.47
  13.4 2.9 %reshape.254 = bf16[10,64,4,256]{3,2,1,0:T(4,128)(2,1)S(1)} reshape(bf16[640,1024]{1,0:T(8,128)(2,1)} %param.9) | data formatting | bytes 2621440 | tf_op jit(solution)/shard_map/reshape | solution.py:172
  16.3 0.1 reduce_sum.9
  16.4 0.2 reduce_window_sum.47
  16.6 0.9 exponential_reduce_fusion.4
  17.5 0.3 fusion.28
  17.8 3.2 %fusion.7 = f32[4,10,128,64]{2,3,1,0:T(8,128)S(1)} fusion(f32[10,4,256]{2,0,1:T(8,128)} %copy.47, f32[4,256,128]{2,1,0:T(8,128)S(1)} %convert_element_type.30, bf16[10,64,4,256]{3,2,1,0:T(4,128)(2,1)S(1)} %reshape.254), kind=kOutput, calls=%fused_computation.9 | convolution fusion | flops 170393600 | bytes 3186688 | tf_op jit(solution)/shard_map/hcjn,hpcj->chnp/dot_general | solution.py:195
  21.0 0.0 copy-start.9
  21.0 0.2 slice_multiply_fusion
  21.2 1.3 %fusion.13 = f32[4,10,64,256]{3,2,0,1:T(8,128)S(1)} fusion(bf16[4,256,128,1]{2,1,0,3:T(8,128)(2,1)S(1)} %bitcast.61, f32[1,10,128,64]{2,3,1,0:T(8,128)S(1)} %get-tuple-element.33, f32[1,10,128,64]{2,3,1,0:T(8,128)S(1)} %get-tuple-element.34, f32[1,10,128,64]{2,3,1,0:T(8,128)S(1)} %get-tuple-element.32, f32[4]{0:T(128)S(1)} %pad.11.clone), kind=kOutput, calls=%fused_computation.18 | convolution fusion | flops 1007616000 | bytes 3866640 | tf_op jit(solution)/shard_map/cin,chnp->hpci/dot_general | solution.py:215
  22.5 4.0 %fusion.10 = bf16[10,64,4,256]{3,1,2,0:T(8,128)(2,1)S(1)} fusion(f32[4,10,64,256]{3,2,0,1:T(8,128)S(1)} %fusion.13, f32[10,4,256]{2,1,0:T(4,128)S(1)} %mul.152, f32[10,4,256]{2,1,0:T(4,128)S(1)} %reduce_window_sum.46, f32[4,256,256]{2,1,0:T(8,128)S(1)} %fusion.28, pred[256,256]{1,0:T(8,128)(4,1)S(1)} %copy-done.2, ...), kind=kOutput, calls=%fused_computation.13 | convolution fusion | flops 355205120 | bytes 6479912 | tf_op jit(solution)/shard_map/hcij,hpcj->hpci/dot_general | solution.py:190
  26.5 1.0 copy.51
  27.6 0.3 copy.53
  27.9 0.1 add.47
  28.1 0.1 pad.10.clone
  28.1 1.4 %maximum_maximum_fusion.after_ref = bf16[672,1024]{1,0:T(8,128)(2,1)} fusion(bf16[10,1024]{1,0:T(8,128)(2,1)S(1)} %get-tuple-element.36, bf16[10,1024]{1,0:T(8,128)(2,1)S(1)} %get-tuple-element.35, bf16[640,1024]{1,0:T(8,128)(2,1)S(1)} %bitcast.55, bf16[672]{0:T(1024)(128)(2,1)S(1)} %pad.10.clone), kind=kLoop, calls=%fused_computation.16 | loop fusion | flops 5505024 | bytes 2729280 | tf_op jit(solution)/shard_map/concatenate | solution.py:223
  29.5 0.0 all-gather.2.cloned.1.call-update
  29.6 0.2 fusion.18
  29.8 0.7 select_maximum_fusion.msg_ref
  30.5 67.0 %shard_map.73 = (f32[648,128]{1,0:T(8,128)}, bf16[8,640,128]{2,1,0:T(8,128)(2,1)}) custom-call(f32[648,128]{1,0:T(8,128)} %select_maximum_fusion.msg_ref, bf16[672,1024]{1,0:T(8,128)(2,1)} %maximum_maximum_fusion.after_ref), custom_call_target="tpu_custom_call" | custom-call | bytes 169869312 | tf_op jit(solution)/shard_map/pallas_call | solution.py:138
  97.5 6.6 %all-gather.2.cloned.1.call-done.local_ref = bf16[5376,1024]{1,0:T(8,128)(2,1)} async-done(((bf16[672,1024]{1,0:T(8,128)(2,1)}), bf16[5376,1024]{1,0:T(8,128)(2,1)}) %all-gather.2.cloned.1.call-update) | async-done | bytes 11010064 | tf_op jit(solution)/shard_map/all_gather | solution.py:232
  104.1 12.5 %shard_map.74 = bf16[320,1024]{1,0:T(8,128)(2,1)} custom-call(bf16[5376,1024]{1,0:T(8,128)(2,1)} %all-gather.2.cloned.1.call-done.local_ref, bf16[1024,128]{1,0:T(8,128)(2,1)} %basis_ref.1, bf16[5120,128]{1,0:T(8,128)(2,1)} %bitcast.67, bf16[320,5120]{1,0:T(8,128)(2,1)} %bitcast.66), custom_call_target="tpu_custom_call" | custom-call | flops 4697620480 | bytes 14942208 | tf_op jit(solution)/shard_map/pallas_call | solution.py:267
  (36 shorter events, 0.3 us)
Async XLA Ops:
  6.5 9.7 %copy-start = (bf16[1024,128]{1,0:T(8,128)(2,1)S(1)}, bf16[1024,128]{1,0:T(8,128)(2,1)}, u32[]{:S(2)}) copy-start(bf16[1024,128]{1,0:T(8,128)(2,1)} %param.13) | copy-start | bytes 786436
  6.5 97.6 %all-gather.2.cloned.1.call-start = ((), (), s32[]{:S(2)}) async-start(), calls=%async_computation | async-start | bytes 12386304 | tf_op jit(solution)/shard_map/all_gather | solution.py:232
  7.2 10.3 %copy-start.1 = (bf16[1024,128]{1,0:T(8,128)(2,1)S(1)}, bf16[1024,128]{1,0:T(8,128)(2,1)}, u32[]{:S(2)}) copy-start(bf16[1024,128]{1,0:T(8,128)(2,1)} %basis_ref.1) | copy-start | bytes 786436
  21.0 1.5 %copy-start.2 = (pred[256,256]{1,0:T(8,128)(4,1)S(1)}, pred[256,256]{1,0:T(8,128)(4,1)}, u32[]{:S(2)}) copy-start(pred[256,256]{1,0:T(8,128)(4,1)} %iota_compare_fusion.1) | copy-start | bytes 196612
  21.0 1.5 %copy-start.3 = (f32[10,4,256]{2,1,0:T(4,128)S(1)}, f32[10,4,256]{2,1,0:T(4,128)}, u32[]{:S(2)}) copy-start(f32[10,4,256]{2,1,0:T(4,128)} %get-tuple-element.37) | copy-start | bytes 122884
  21.0 1.5 %copy-start.9 = (f32[10]{0:T(128)S(1)}, f32[10]{0:T(128)}, u32[]{:S(2)}) copy-start(f32[10]{0:T(128)} %param.12) | copy-start | bytes 124
  27.9 1.7 %copy-start.4 = (f32[10]{0:T(128)S(1)}, f32[10]{0:T(128)}, u32[]{:S(2)}) copy-start(f32[10]{0:T(128)} %get-tuple-element.25) | copy-start | bytes 124
  27.9 1.7 %copy-start.5 = (f32[10]{0:T(128)S(1)}, f32[10]{0:T(128)}, u32[]{:S(2)}) copy-start(f32[10]{0:T(128)} %get-tuple-element.27) | copy-start | bytes 124
  27.9 1.7 %copy-start.6 = (f32[10]{0:T(128)S(1)}, f32[10]{0:T(128)}, u32[]{:S(2)}) copy-start(f32[10]{0:T(128)} %get-tuple-element.28) | copy-start | bytes 124
  27.9 1.7 %copy-start.7 = (f32[10]{0:T(128)S(1)}, f32[10]{0:T(128)}, u32[]{:S(2)}) copy-start(f32[10]{0:T(128)} %get-tuple-element.29) | copy-start | bytes 124
  28.1 1.6 %copy-start.8 = (f32[10]{0:T(128)S(1)}, f32[10]{0:T(128)}, u32[]{:S(2)}) copy-start(f32[10]{0:T(128)} %get-tuple-element.26) | copy-start | bytes 124
Sparse Core Ops, SparseCore 0:
  29.6 74.4 all-gather.1

commit v13 on v11

--- a/solution.py
+++ b/solution.py
@@ -76,30 +76,47 @@
     send_ref[:rows] = out_ref[:rows].astype(send_ref.dtype)
     send_ref[rows:] = scale_ref[...]
     spread_ref[grp_here] = send_ref[...]
-    copies = []
-    for offset in range(1, groups):
-        copy = pltpu.make_async_remote_copy(
+    partner = grp_here + 1 - 2 * lax.rem(grp_here, 2)
+
+    def spread_copy(slot, target, sem):
+        return pltpu.make_async_remote_copy(
+            src_ref=send_ref if slot is None else spread_ref.at[slot],
+            dst_ref=spread_ref.at[grp_here if slot is None else slot],
+            send_sem=sem,
+            recv_sem=spread_recv.at[grp_here if slot is None else slot],
+            device_id=device(here, target),
+            device_id_type=pl.DeviceIdType.MESH,
+        )
+
+    def arriving(slot, source):
+        return pltpu.make_async_remote_copy(
             src_ref=send_ref,
-            dst_ref=spread_ref.at[grp_here],
-            send_sem=spread_send.at[offset],
-            recv_sem=spread_recv.at[grp_here],
-            device_id=device(here, lax.rem(grp_here + offset, groups)),
-            device_id_type=pl.DeviceIdType.MESH,
-        )
+            dst_ref=spread_ref.at[slot],
+            send_sem=spread_send.at[0],
+            recv_sem=spread_recv.at[slot],
+            device_id=device(here, source),
+            device_id_type=pl.DeviceIdType.MESH,
+        )
+
+    chips = groups // 2
+    copies = [spread_copy(None, partner, spread_send.at[0])]
+    for k in range(1, chips):
+        copies.append(spread_copy(None, lax.rem(grp_here + 2 * k, groups), spread_send.at[k]))
+    for copy in copies:
         copy.start()
-        copies.append(copy)
-    for copy in copies:
+    arriving(partner, partner).wait_recv()
+    forwards = []
+    for k in range(1, chips):
+        source = lax.rem(grp_here + groups - 2 * k, groups)
+        arriving(source, source).wait_recv()
+        forward = spread_copy(source, partner, spread_send.at[chips - 1 + k])
+        forward.start()
+        forwards.append(forward)
+    for k in range(1, chips):
+        slot = lax.rem(partner + groups - 2 * k, groups)
+        arriving(slot, partner).wait_recv()
+    for copy in copies + forwards:
         copy.wait_send()
-    for offset in range(1, groups):
-        source = lax.rem(grp_here + groups - offset, groups)
-        pltpu.make_async_remote_copy(
-            src_ref=send_ref,
-            dst_ref=spread_ref.at[source],
-            send_sem=spread_send.at[offset],
-            recv_sem=spread_recv.at[source],
-            device_id=device(here, source),
-            device_id_type=pl.DeviceIdType.MESH,
-        ).wait_recv()
 
 
 def _hops(peers):

time: 132 us -> 123 us (0.932)
  Pallas kernels: 93.6 us -> 82.7 us
  waiting for transfers between devices: 0.04 us -> 2.42 us
    pallas_call x1, Pallas kernels: 80.8 us -> 70 us  [carry_in(): pl.pallas_call(functools.partial(scan_kernel, peers, names), out_shape=(j...]
    all_gather x1, waiting for transfers between devices: 0.02 us -> 2.41 us  [on_device(): local_all = lax.all_gather(local_flat, 'grp', axis=0, tiled=True)]
  transfers between devices with their start and end apart: 1 -> 1, of which waited for: 0 -> 1; matrix products, arithmetic and copies ran while one was open for 1% -> 1% of each run, Pallas kernels for 62% -> 57%
where the time goes in v13:
time: 123 us
  Pallas kernels  82.7 us (67%)
  between operations  13.7 us (11%)
  matrix products  8.75 us (7%)
  local copies, waits for them, and re-layouts  8.2 us (7%)
  other arithmetic  6.89 us (6%)
  waiting for transfers between devices  2.42 us (2%)
    pallas_call x1, Pallas kernels, carry_in(): pl.pallas_call(functools.partial(scan_kernel, peers, names), out_shape=(j...  70 us
    pallas_call x1, Pallas kernels, tail(): pl.pallas_call(tail_kernel, out_shape=jax.ShapeDtypeStruct((features, tok...  12.7 us
    dot_general x1, matrix products, on_device(): jnp.einsum('hcij,hpcj->hpci', mixing, channels, preferred_element_type=jn...  3.99 us
    dot_general x1, matrix products, on_device(): jnp.einsum('hcjn,hpcj->chnp', weighted_terms, channels, preferred_element...  3.19 us
    reshape x1, local copies, waits for them, and re-layouts, on_device(): channels = mixer_input.reshape(heads_here, HP, count, GROUP)  2.88 us
  transfers between devices with their start and end apart: 1, of which 1 were waited for; matrix products, arithmetic and copies ran while one was open for 1% of the time, Pallas kernels for 57%

profile of v13, /device:TPU:1, one launch (start us, length us, event | category | flops | bytes accessed | tf_op | source)
XLA Modules:
  0.0 122.6 jit_solution(14850735264315858955)
XLA Ops:
  6.5 0.6 iota_compare_fusion.1
  7.2 0.9 mul.152
  8.0 0.9 fusion.25
  9.0 2.3 %reduce-window.6 = f32[10,4,2,128]{3,0,1,2:T(8,128)S(1)} reduce-window(f32[10,4,2,128]{3,0,1,2:T(8,128)S(1)} %copy.41, f32[]{:T(128)} %constant.34.clone.1), window={size=1x1x1x128 pad=0_0x0_0x0_0x127_0}, to_apply=%region_0.0 | reduce-window | flops 1300480 | bytes 81924 | tf_op jit(solution)/shard_map/reduce-window
  11.3 0.2 slice_reduce_fusion
  11.5 0.1 broadcast_add_fusion
  11.7 0.1 slice.89
  11.8 0.1 copy.44
  11.9 0.1 copy.45
  12.0 0.6 fusion.26
  12.6 0.6 copy.46
  13.3 2.9 %reshape.254 = bf16[10,64,4,256]{3,2,1,0:T(4,128)(2,1)S(1)} reshape(bf16[640,1024]{1,0:T(8,128)(2,1)} %param.9) | data formatting | bytes 2621440 | tf_op jit(solution)/shard_map/reshape | solution.py:177
  16.2 0.0 copy-done.1
  16.2 0.1 reduce_sum.9
  16.3 0.2 reduce_window_sum.47
  16.5 0.9 exponential_reduce_fusion.4
  17.4 0.3 fusion.28
  17.7 3.2 %fusion.7 = f32[4,10,128,64]{2,3,1,0:T(8,128)S(1)} fusion(f32[10,4,256]{2,0,1:T(8,128)} %copy.46, f32[4,256,128]{2,1,0:T(8,128)S(1)} %convert_element_type.30, bf16[10,64,4,256]{3,2,1,0:T(4,128)(2,1)S(1)} %reshape.254), kind=kOutput, calls=%fused_computation.9 | convolution fusion | flops 170393600 | bytes 3186688 | tf_op jit(solution)/shard_map/hcjn,hpcj->chnp/dot_general | solution.py:200
  20.9 0.0 copy-start.5
  20.9 0.2 slice_multiply_fusion
  21.1 1.3 %fusion.13 = f32[4,10,64,256]{3,2,0,1:T(8,128)S(1)} fusion(bf16[4,256,128,1]{2,1,0,3:T(8,128)(2,1)S(1)} %bitcast.59, f32[1,10,128,64]{2,3,1,0:T(8,128)S(1)} %get-tuple-element.33, f32[1,10,128,64]{2,3,1,0:T(8,128)S(1)} %get-tuple-element.34, f32[1,10,128,64]{2,3,1,0:T(8,128)S(1)} %get-tuple-element.32, f32[4]{0:T(128)S(1)} %pad.9.clone), kind=kOutput, calls=%fused_computation.17 | convolution fusion | flops 1007616000 | bytes 3866640 | tf_op jit(solution)/shard_map/cin,chnp->hpci/dot_general | solution.py:220
  22.5 4.0 %fusion.10 = bf16[10,64,4,256]{3,1,2,0:T(8,128)(2,1)S(1)} fusion(f32[4,10,64,256]{3,2,0,1:T(8,128)S(1)} %fusion.13, f32[10,4,256]{2,1,0:T(4,128)S(1)} %mul.152, f32[10,4,256]{2,1,0:T(4,128)S(1)} %reduce_window_sum.46, f32[4,256,256]{2,1,0:T(8,128)S(1)} %fusion.28, pred[256,256]{1,0:T(8,128)(4,1)S(1)} %copy-done.2, ...), kind=kOutput, calls=%fused_computation.13 | convolution fusion | flops 355205120 | bytes 6479912 | tf_op jit(solution)/shard_map/hcij,hpcj->hpci/dot_general | solution.py:195
  26.5 1.0 copy.50
  27.5 1.4 %copy.52 = bf16[80,8,4,256]{3,1,2,0:T(8,128)(2,1)} copy(bf16[80,8,4,256]{3,2,1,0:T(4,128)(2,1)S(1)} %bitcast.56) | data formatting | bytes 2621440
  28.9 0.0 all-gather.2.cloned.1.call-update
  28.9 0.1 add.50
  29.1 0.7 reshape.258.scale_ref
  29.7 0.2 fusion.18
  29.9 0.7 select_maximum_fusion.msg_ref
  30.7 70.0 %shard_map.73 = (f32[648,128]{1,0:T(8,128)}, bf16[8,800,128]{2,1,0:T(8,128)(2,1)}) custom-call(f32[648,128]{1,0:T(8,128)} %select_maximum_fusion.msg_ref, bf16[640,1024]{1,0:T(8,128)(2,1)} %bitcast.55, bf16[160,128]{1,0:T(8,128)(2,1)} %reshape.258.scale_ref), custom_call_target="tpu_custom_call" | custom-call | bytes 169869312 | tf_op jit(solution)/shard_map/pallas_call | solution.py:139
  100.7 2.4 %all-gather.2.cloned.1.call-done.local_ref = bf16[5120,1024]{1,0:T(8,128)(2,1)} async-done(((bf16[640,1024]{1,0:T(8,128)(2,1)}), bf16[5120,1024]{1,0:T(8,128)(2,1)}) %all-gather.2.cloned.1.call-update) | async-done | bytes 10485776 | tf_op jit(solution)/shard_map/all_gather | solution.py:230
  103.1 12.7 %shard_map.74 = bf16[320,1024]{1,0:T(8,128)(2,1)} custom-call(bf16[5120,1024]{1,0:T(8,128)(2,1)} %all-gather.2.cloned.1.call-done.local_ref, bf16[1024,128]{1,0:T(8,128)(2,1)} %basis_ref.1, bf16[8,800,128]{2,1,0:T(8,128)(2,1)} %get-tuple-element.18.carried_ref.scale_ref, bf16[8,800,128]{2,1,0:T(8,128)(2,1)} %get-tuple-element.18.carried_ref.scale_ref, ...), custom_call_target="tpu_custom_call" | custom-call | flops 4697620480 | bytes 14417920 | tf_op jit(solution)/shard_map/pallas_call | solution.py:271
  (27 shorter events, 0.3 us)
Async XLA Ops:
  6.5 9.6 %copy-start.1 = (bf16[1024,128]{1,0:T(8,128)(2,1)S(1)}, bf16[1024,128]{1,0:T(8,128)(2,1)}, u32[]{:S(2)}) copy-start(bf16[1024,128]{1,0:T(8,128)(2,1)} %param.13) | copy-start | bytes 786436
  6.5 10.9 %copy-start = (bf16[1024,128]{1,0:T(8,128)(2,1)S(1)}, bf16[1024,128]{1,0:T(8,128)(2,1)}, u32[]{:S(2)}) copy-start(bf16[1024,128]{1,0:T(8,128)(2,1)} %basis_ref.1) | copy-start | bytes 786436
  6.5 96.5 %all-gather.2.cloned.1.call-start = ((), (), s32[]{:S(2)}) async-start(), calls=%async_computation | async-start | bytes 11796480 | tf_op jit(solution)/shard_map/all_gather | solution.py:230
  20.9 1.5 %copy-start.2 = (pred[256,256]{1,0:T(8,128)(4,1)S(1)}, pred[256,256]{1,0:T(8,128)(4,1)}, u32[]{:S(2)}) copy-start(pred[256,256]{1,0:T(8,128)(4,1)} %iota_compare_fusion.1) | copy-start | bytes 196612
  20.9 1.5 %copy-start.3 = (f32[10,4,256]{2,1,0:T(4,128)S(1)}, f32[10,4,256]{2,1,0:T(4,128)}, u32[]{:S(2)}) copy-start(f32[10,4,256]{2,1,0:T(4,128)} %get-tuple-element.37) | copy-start | bytes 122884
  20.9 1.5 %copy-start.5 = (f32[10]{0:T(128)S(1)}, f32[10]{0:T(128)}, u32[]{:S(2)}) copy-start(f32[10]{0:T(128)} %param.12) | copy-start | bytes 124
  27.5 2.4 %copy-start.4 = (f32[10]{0:T(128)S(1)}, f32[10]{0:T(128)}, u32[]{:S(2)}) copy-start(f32[10]{0:T(128)} %get-tuple-element.26) | copy-start | bytes 124
Sparse Core Ops, SparseCore 0:
  29.0 74.0 all-gather.1

commit v14 on v13

--- a/solution.py
+++ b/solution.py
@@ -240,21 +240,26 @@
     def _():
         acc_ref[...] = jnp.zeros_like(acc_ref)
 
-    base, tokens = mixed_ref.shape
+    pair, base = carried_ref.shape[0], carried_ref.shape[1]
+    tokens = mixed_ref.shape[1]
     per = base // HP
     tiles = tokens // 128
-    carry = lax.dot_general(
-        carried_ref[...], basis_ref[...], (((1,), (1,)), ((), ())), preferred_element_type=jnp.float32
-    )
-    for h in range(per):
-        for k in range(tiles):
-            rows, lanes = slice(h * HP, (h + 1) * HP), slice(k * 128, (k + 1) * 128)
-            scale = scale_ref[pl.ds(h * tiles + k, 1), :].astype(jnp.float32) + scale_ref[
-                pl.ds((per + h) * tiles + k, 1), :
-            ].astype(jnp.float32)
-            mixed_ref[rows, lanes] = (
-                local_ref[rows, lanes].astype(jnp.float32) + carry[rows, lanes] * scale
-            ).astype(jnp.bfloat16)
+    for sub in range(pair):
+        carry = lax.dot_general(
+            carried_ref[sub], basis_ref[...], (((1,), (1,)), ((), ())),
+            preferred_element_type=jnp.float32,
+        )
+        for h in range(per):
+            for k in range(tiles):
+                rows = slice(sub * base + h * HP, sub * base + (h + 1) * HP)
+                lanes = slice(k * 128, (k + 1) * 128)
+                scale = scale_ref[sub, pl.ds(h * tiles + k, 1), :].astype(jnp.float32) + scale_ref[
+                    sub, pl.ds((per + h) * tiles + k, 1), :
+                ].astype(jnp.float32)
+                mixed_ref[rows, lanes] = (
+                    local_ref[rows, lanes].astype(jnp.float32)
+                    + carry[h * HP : (h + 1) * HP, lanes] * scale
+                ).astype(jnp.bfloat16)
     acc_ref[...] += jnp.dot(weight_ref[...], mixed_ref[...], preferred_element_type=jnp.float32)
 
     @pl.when(g == pl.num_programs(0) - 1)
@@ -268,21 +273,22 @@
     groups = lax.axis_size("grp")
     per = channels // groups // HP
     packed = 2 * per * tokens // 128
+    pair = 2 if groups % 2 == 0 else 1
     return pl.pallas_call(
         tail_kernel,
         out_shape=jax.ShapeDtypeStruct((features, tokens), jnp.bfloat16),
-        grid=(groups,),
+        grid=(groups // pair,),
         in_specs=[
-            pl.BlockSpec((channels // groups, tokens), lambda g: (g, 0)),
+            pl.BlockSpec((pair * channels // groups, tokens), lambda g: (g, 0)),
             pl.BlockSpec(basis.shape, lambda g: (0, 0)),
-            pl.BlockSpec((None, per * HP, N), lambda g: (g, 0, 0)),
-            pl.BlockSpec((None, packed, N), lambda g: (g, per * HP // packed, 0)),
-            pl.BlockSpec((features, per * HP), lambda g: (0, g)),
+            pl.BlockSpec((pair, per * HP, N), lambda g: (g, 0, 0)),
+            pl.BlockSpec((pair, packed, N), lambda g: (g, per * HP // packed, 0)),
+            pl.BlockSpec((features, pair * per * HP), lambda g: (0, g)),
         ],
         out_specs=pl.BlockSpec((features, tokens), lambda g: (0, 0)),
         scratch_shapes=[
             pltpu.VMEM((features, tokens), jnp.float32),
-            pltpu.VMEM((per * HP, tokens), jnp.bfloat16),
+            pltpu.VMEM((pair * per * HP, tokens), jnp.bfloat16),
         ],
         cost_estimate=pl.CostEstimate(
             flops=2 * tokens * per * HP * groups * (N + features),

time: 123 us -> 121 us (0.984)
  Pallas kernels: 82.7 us -> 80.5 us
    pallas_call x1, Pallas kernels: 12.7 us -> 10.5 us  [tail(): pl.pallas_call(tail_kernel, out_shape=jax.ShapeDtypeStruct((features, tok...]
  transfers between devices with their start and end apart: 1 -> 1, of which waited for: 1 -> 1; matrix products, arithmetic and copies ran while one was open for 1% -> 1% of each run, Pallas kernels for 57% -> 58%
where the time goes in v14:
time: 121 us; the launch traced here: 120 us
  Pallas kernels  80.5 us (67%)
  between operations  13.7 us (11%)
  matrix products  8.75 us (7%)
  local copies, waits for them, and re-layouts  8.2 us (7%)
  other arithmetic  6.89 us (6%)
  waiting for transfers between devices  2.42 us (2%)
    pallas_call x1, Pallas kernels, carry_in(): pl.pallas_call(functools.partial(scan_kernel, peers, names), out_shape=(j...  70 us
    pallas_call x1, Pallas kernels, tail(): pl.pallas_call(tail_kernel, out_shape=jax.ShapeDtypeStruct((features, tok...  10.5 us
    dot_general x1, matrix products, on_device(): jnp.einsum('hcij,hpcj->hpci', mixing, channels, preferred_element_type=jn...  3.99 us
    dot_general x1, matrix products, on_device(): jnp.einsum('hcjn,hpcj->chnp', weighted_terms, channels, preferred_element...  3.19 us
    reshape x1, local copies, waits for them, and re-layouts, on_device(): channels = mixer_input.reshape(heads_here, HP, count, GROUP)  2.88 us
  transfers between devices with their start and end apart: 1, of which 1 were waited for; matrix products, arithmetic and copies ran while one was open for 1% of the time, Pallas kernels for 58%

profile of v14, /device:TPU:1, one launch (start us, length us, event | category | flops | bytes accessed | tf_op | source)
XLA Modules:
  0.0 120.4 jit_solution(12158674831098989416)
XLA Ops:
  6.5 0.6 iota_compare_fusion.1
  7.2 0.9 mul.152
  8.0 0.9 fusion.25
  9.0 2.3 %reduce-window.6 = f32[10,4,2,128]{3,0,1,2:T(8,128)S(1)} reduce-window(f32[10,4,2,128]{3,0,1,2:T(8,128)S(1)} %copy.41, f32[]{:T(128)} %constant.34.clone.1), window={size=1x1x1x128 pad=0_0x0_0x0_0x127_0}, to_apply=%region_0.0 | reduce-window | flops 1300480 | bytes 81924 | tf_op jit(solution)/shard_map/reduce-window
  11.3 0.2 slice_reduce_fusion
  11.5 0.1 broadcast_add_fusion
  11.7 0.1 slice.89
  11.8 0.1 copy.44
  11.9 0.1 copy.45
  12.0 0.6 fusion.26
  12.6 0.6 copy.46
  13.3 2.9 %reshape.254 = bf16[10,64,4,256]{3,2,1,0:T(4,128)(2,1)S(1)} reshape(bf16[640,1024]{1,0:T(8,128)(2,1)} %param.9) | data formatting | bytes 2621440 | tf_op jit(solution)/shard_map/reshape | solution.py:177
  16.2 0.1 reduce_sum.9
  16.3 0.2 reduce_window_sum.47
  16.5 0.9 exponential_reduce_fusion.4
  17.4 0.3 fusion.28
  17.7 3.2 %fusion.7 = f32[4,10,128,64]{2,3,1,0:T(8,128)S(1)} fusion(f32[10,4,256]{2,0,1:T(8,128)} %copy.46, f32[4,256,128]{2,1,0:T(8,128)S(1)} %convert_element_type.30, bf16[10,64,4,256]{3,2,1,0:T(4,128)(2,1)S(1)} %reshape.254), kind=kOutput, calls=%fused_computation.9 | convolution fusion | flops 170393600 | bytes 3186688 | tf_op jit(solution)/shard_map/hcjn,hpcj->chnp/dot_general | solution.py:200
  20.9 0.0 copy-start.2
  20.9 0.0 copy-start.5
  20.9 0.2 slice_multiply_fusion
  21.1 1.3 %fusion.13 = f32[4,10,64,256]{3,2,0,1:T(8,128)S(1)} fusion(bf16[4,256,128,1]{2,1,0,3:T(8,128)(2,1)S(1)} %bitcast.59, f32[1,10,128,64]{2,3,1,0:T(8,128)S(1)} %get-tuple-element.33, f32[1,10,128,64]{2,3,1,0:T(8,128)S(1)} %get-tuple-element.34, f32[1,10,128,64]{2,3,1,0:T(8,128)S(1)} %get-tuple-element.32, f32[4]{0:T(128)S(1)} %pad.9.clone), kind=kOutput, calls=%fused_computation.17 | convolution fusion | flops 1007616000 | bytes 3866640 | tf_op jit(solution)/shard_map/cin,chnp->hpci/dot_general | solution.py:220
  22.5 4.0 %fusion.10 = bf16[10,64,4,256]{3,1,2,0:T(8,128)(2,1)S(1)} fusion(f32[4,10,64,256]{3,2,0,1:T(8,128)S(1)} %fusion.13, f32[10,4,256]{2,1,0:T(4,128)S(1)} %mul.152, f32[10,4,256]{2,1,0:T(4,128)S(1)} %reduce_window_sum.46, f32[4,256,256]{2,1,0:T(8,128)S(1)} %fusion.28, pred[256,256]{1,0:T(8,128)(4,1)S(1)} %copy-done.2, ...), kind=kOutput, calls=%fused_computation.13 | convolution fusion | flops 355205120 | bytes 6479912 | tf_op jit(solution)/shard_map/hcij,hpcj->hpci/dot_general | solution.py:195
  26.5 1.0 copy.50
  27.5 1.4 %copy.52 = bf16[80,8,4,256]{3,1,2,0:T(8,128)(2,1)} copy(bf16[80,8,4,256]{3,2,1,0:T(4,128)(2,1)S(1)} %bitcast.56) | data formatting | bytes 2621440
  28.9 0.0 all-gather.2.cloned.1.call-update
  28.9 0.1 add.50
  29.1 0.7 reshape.258.scale_ref
  29.7 0.2 fusion.18
  29.9 0.7 select_maximum_fusion.msg_ref
  30.7 70.0 %shard_map.73 = (f32[648,128]{1,0:T(8,128)}, bf16[8,800,128]{2,1,0:T(8,128)(2,1)}) custom-call(f32[648,128]{1,0:T(8,128)} %select_maximum_fusion.msg_ref, bf16[640,1024]{1,0:T(8,128)(2,1)} %bitcast.55, bf16[160,128]{1,0:T(8,128)(2,1)} %reshape.258.scale_ref), custom_call_target="tpu_custom_call" | custom-call | bytes 169869312 | tf_op jit(solution)/shard_map/pallas_call | solution.py:139
  100.7 2.4 %all-gather.2.cloned.1.call-done.local_ref = bf16[5120,1024]{1,0:T(8,128)(2,1)} async-done(((bf16[640,1024]{1,0:T(8,128)(2,1)}), bf16[5120,1024]{1,0:T(8,128)(2,1)}) %all-gather.2.cloned.1.call-update) | async-done | bytes 10485776 | tf_op jit(solution)/shard_map/all_gather | solution.py:230
  103.1 10.5 %shard_map.74 = bf16[320,1024]{1,0:T(8,128)(2,1)} custom-call(bf16[5120,1024]{1,0:T(8,128)(2,1)} %all-gather.2.cloned.1.call-done.local_ref, bf16[1024,128]{1,0:T(8,128)(2,1)} %basis_ref.1, bf16[8,800,128]{2,1,0:T(8,128)(2,1)} %get-tuple-element.18.carried_ref.scale_ref, bf16[8,800,128]{2,1,0:T(8,128)(2,1)} %get-tuple-element.18.carried_ref.scale_ref, ...), custom_call_target="tpu_custom_call" | custom-call | flops 4697620480 | bytes 14417920 | tf_op jit(solution)/shard_map/pallas_call | solution.py:277
  (27 shorter events, 0.3 us)
Async XLA Ops:
  6.5 9.6 %copy-start.1 = (bf16[1024,128]{1,0:T(8,128)(2,1)S(1)}, bf16[1024,128]{1,0:T(8,128)(2,1)}, u32[]{:S(2)}) copy-start(bf16[1024,128]{1,0:T(8,128)(2,1)} %param.13) | copy-start | bytes 786436
  6.5 10.9 %copy-start = (bf16[1024,128]{1,0:T(8,128)(2,1)S(1)}, bf16[1024,128]{1,0:T(8,128)(2,1)}, u32[]{:S(2)}) copy-start(bf16[1024,128]{1,0:T(8,128)(2,1)} %basis_ref.1) | copy-start | bytes 786436
  6.5 96.5 %all-gather.2.cloned.1.call-start = ((), (), s32[]{:S(2)}) async-start(), calls=%async_computation | async-start | bytes 11796480 | tf_op jit(solution)/shard_map/all_gather | solution.py:230
  20.9 1.5 %copy-start.2 = (pred[256,256]{1,0:T(8,128)(4,1)S(1)}, pred[256,256]{1,0:T(8,128)(4,1)}, u32[]{:S(2)}) copy-start(pred[256,256]{1,0:T(8,128)(4,1)} %iota_compare_fusion.1) | copy-start | bytes 196612
  20.9 1.5 %copy-start.3 = (f32[10,4,256]{2,1,0:T(4,128)S(1)}, f32[10,4,256]{2,1,0:T(4,128)}, u32[]{:S(2)}) copy-start(f32[10,4,256]{2,1,0:T(4,128)} %get-tuple-element.37) | copy-start | bytes 122884
  20.9 1.5 %copy-start.5 = (f32[10]{0:T(128)S(1)}, f32[10]{0:T(128)}, u32[]{:S(2)}) copy-start(f32[10]{0:T(128)} %param.12) | copy-start | bytes 124
  27.5 2.4 %copy-start.4 = (f32[10]{0:T(128)S(1)}, f32[10]{0:T(128)}, u32[]{:S(2)}) copy-start(f32[10]{0:T(128)} %get-tuple-element.26) | copy-start | bytes 124
Sparse Core Ops, SparseCore 0:
  29.0 74.0 all-gather.1

commit v15 on v14

--- a/solution.py
+++ b/solution.py
@@ -273,7 +273,7 @@
     groups = lax.axis_size("grp")
     per = channels // groups // HP
     packed = 2 * per * tokens // 128
-    pair = 2 if groups % 2 == 0 else 1
+    pair = 4 if groups % 4 == 0 else 1
     return pl.pallas_call(
         tail_kernel,
         out_shape=jax.ShapeDtypeStruct((features, tokens), jnp.bfloat16),

time: 121 us -> 121 us (level)
  no operation moved by 1% of the time
where the time goes in v15:
time: 121 us
  Pallas kernels  80.8 us (67%)
  between operations  13.7 us (11%)
  matrix products  8.75 us (7%)
  local copies, waits for them, and re-layouts  8.2 us (7%)
  other arithmetic  6.89 us (6%)
  waiting for transfers between devices  2.42 us (2%)
    pallas_call x1, Pallas kernels, carry_in(): pl.pallas_call(functools.partial(scan_kernel, peers, names), out_shape=(j...  70 us
    pallas_call x1, Pallas kernels, tail(): pl.pallas_call(tail_kernel, out_shape=jax.ShapeDtypeStruct((features, tok...  10.8 us
    dot_general x1, matrix products, on_device(): jnp.einsum('hcij,hpcj->hpci', mixing, channels, preferred_element_type=jn...  3.99 us
    dot_general x1, matrix products, on_device(): jnp.einsum('hcjn,hpcj->chnp', weighted_terms, channels, preferred_element...  3.19 us
    reshape x1, local copies, waits for them, and re-layouts, on_device(): channels = mixer_input.reshape(heads_here, HP, count, GROUP)  2.88 us
  transfers between devices with their start and end apart: 1, of which 1 were waited for; matrix products, arithmetic and copies ran while one was open for 1% of the time, Pallas kernels for 58%

profile of v15, /device:TPU:1, one launch (start us, length us, event | category | flops | bytes accessed | tf_op | source)
XLA Modules:
  0.0 120.8 jit_solution(12692262393217202127)
XLA Ops:
  6.5 0.6 iota_compare_fusion.1
  7.2 0.9 mul.152
  8.0 0.9 fusion.25
  9.0 2.3 %reduce-window.6 = f32[10,4,2,128]{3,0,1,2:T(8,128)S(1)} reduce-window(f32[10,4,2,128]{3,0,1,2:T(8,128)S(1)} %copy.41, f32[]{:T(128)} %constant.34.clone.1), window={size=1x1x1x128 pad=0_0x0_0x0_0x127_0}, to_apply=%region_0.0 | reduce-window | flops 1300480 | bytes 81924 | tf_op jit(solution)/shard_map/reduce-window
  11.3 0.2 slice_reduce_fusion
  11.5 0.1 broadcast_add_fusion
  11.7 0.1 slice.89
  11.8 0.1 copy.44
  11.9 0.1 copy.45
  12.0 0.6 fusion.26
  12.6 0.6 copy.46
  13.3 2.9 %reshape.254 = bf16[10,64,4,256]{3,2,1,0:T(4,128)(2,1)S(1)} reshape(bf16[640,1024]{1,0:T(8,128)(2,1)} %param.9) | data formatting | bytes 2621440 | tf_op jit(solution)/shard_map/reshape | solution.py:177
  16.2 0.0 copy-done.1
  16.2 0.1 reduce_sum.9
  16.3 0.2 reduce_window_sum.47
  16.5 0.9 exponential_reduce_fusion.4
  17.4 0.3 fusion.28
  17.7 3.2 %fusion.7 = f32[4,10,128,64]{2,3,1,0:T(8,128)S(1)} fusion(f32[10,4,256]{2,0,1:T(8,128)} %copy.46, f32[4,256,128]{2,1,0:T(8,128)S(1)} %convert_element_type.30, bf16[10,64,4,256]{3,2,1,0:T(4,128)(2,1)S(1)} %reshape.254), kind=kOutput, calls=%fused_computation.9 | convolution fusion | flops 170393600 | bytes 3186688 | tf_op jit(solution)/shard_map/hcjn,hpcj->chnp/dot_general | solution.py:200
  20.9 0.0 copy-start.5
  20.9 0.2 slice_multiply_fusion
  21.1 1.3 %fusion.13 = f32[4,10,64,256]{3,2,0,1:T(8,128)S(1)} fusion(bf16[4,256,128,1]{2,1,0,3:T(8,128)(2,1)S(1)} %bitcast.59, f32[1,10,128,64]{2,3,1,0:T(8,128)S(1)} %get-tuple-element.33, f32[1,10,128,64]{2,3,1,0:T(8,128)S(1)} %get-tuple-element.34, f32[1,10,128,64]{2,3,1,0:T(8,128)S(1)} %get-tuple-element.32, f32[4]{0:T(128)S(1)} %pad.9.clone), kind=kOutput, calls=%fused_computation.17 | convolution fusion | flops 1007616000 | bytes 3866640 | tf_op jit(solution)/shard_map/cin,chnp->hpci/dot_general | solution.py:220
  22.5 4.0 %fusion.10 = bf16[10,64,4,256]{3,1,2,0:T(8,128)(2,1)S(1)} fusion(f32[4,10,64,256]{3,2,0,1:T(8,128)S(1)} %fusion.13, f32[10,4,256]{2,1,0:T(4,128)S(1)} %mul.152, f32[10,4,256]{2,1,0:T(4,128)S(1)} %reduce_window_sum.46, f32[4,256,256]{2,1,0:T(8,128)S(1)} %fusion.28, pred[256,256]{1,0:T(8,128)(4,1)S(1)} %copy-done.2, ...), kind=kOutput, calls=%fused_computation.13 | convolution fusion | flops 355205120 | bytes 6479912 | tf_op jit(solution)/shard_map/hcij,hpcj->hpci/dot_general | solution.py:195
  26.5 1.0 copy.50
  27.5 1.4 %copy.52 = bf16[80,8,4,256]{3,1,2,0:T(8,128)(2,1)} copy(bf16[80,8,4,256]{3,2,1,0:T(4,128)(2,1)S(1)} %bitcast.56) | data formatting | bytes 2621440
  28.9 0.0 all-gather.2.cloned.1.call-update
  28.9 0.1 add.50
  29.1 0.7 reshape.258.scale_ref
  29.7 0.2 fusion.18
  29.9 0.7 select_maximum_fusion.msg_ref
  30.7 70.0 %shard_map.73 = (f32[648,128]{1,0:T(8,128)}, bf16[8,800,128]{2,1,0:T(8,128)(2,1)}) custom-call(f32[648,128]{1,0:T(8,128)} %select_maximum_fusion.msg_ref, bf16[640,1024]{1,0:T(8,128)(2,1)} %bitcast.55, bf16[160,128]{1,0:T(8,128)(2,1)} %reshape.258.scale_ref), custom_call_target="tpu_custom_call" | custom-call | bytes 169869312 | tf_op jit(solution)/shard_map/pallas_call | solution.py:139
  100.7 2.4 %all-gather.2.cloned.1.call-done.local_ref = bf16[5120,1024]{1,0:T(8,128)(2,1)} async-done(((bf16[640,1024]{1,0:T(8,128)(2,1)}), bf16[5120,1024]{1,0:T(8,128)(2,1)}) %all-gather.2.cloned.1.call-update) | async-done | bytes 10485776 | tf_op jit(solution)/shard_map/all_gather | solution.py:230
  103.1 10.8 %shard_map.74 = bf16[320,1024]{1,0:T(8,128)(2,1)} custom-call(bf16[5120,1024]{1,0:T(8,128)(2,1)} %all-gather.2.cloned.1.call-done.local_ref, bf16[1024,128]{1,0:T(8,128)(2,1)} %basis_ref.1, bf16[8,800,128]{2,1,0:T(8,128)(2,1)} %get-tuple-element.18.carried_ref.scale_ref, bf16[8,800,128]{2,1,0:T(8,128)(2,1)} %get-tuple-element.18.carried_ref.scale_ref, ...), custom_call_target="tpu_custom_call" | custom-call | flops 4697620480 | bytes 14417920 | tf_op jit(solution)/shard_map/pallas_call | solution.py:277
  (27 shorter events, 0.3 us)
Async XLA Ops:
  6.5 9.6 %copy-start.1 = (bf16[1024,128]{1,0:T(8,128)(2,1)S(1)}, bf16[1024,128]{1,0:T(8,128)(2,1)}, u32[]{:S(2)}) copy-start(bf16[1024,128]{1,0:T(8,128)(2,1)} %param.13) | copy-start | bytes 786436
  6.5 10.9 %copy-start = (bf16[1024,128]{1,0:T(8,128)(2,1)S(1)}, bf16[1024,128]{1,0:T(8,128)(2,1)}, u32[]{:S(2)}) copy-start(bf16[1024,128]{1,0:T(8,128)(2,1)} %basis_ref.1) | copy-start | bytes 786436
  6.5 96.5 %all-gather.2.cloned.1.call-start = ((), (), s32[]{:S(2)}) async-start(), calls=%async_computation | async-start | bytes 11796480 | tf_op jit(solution)/shard_map/all_gather | solution.py:230
  20.9 1.5 %copy-start.2 = (pred[256,256]{1,0:T(8,128)(4,1)S(1)}, pred[256,256]{1,0:T(8,128)(4,1)}, u32[]{:S(2)}) copy-start(pred[256,256]{1,0:T(8,128)(4,1)} %iota_compare_fusion.1) | copy-start | bytes 196612
  20.9 1.5 %copy-start.3 = (f32[10,4,256]{2,1,0:T(4,128)S(1)}, f32[10,4,256]{2,1,0:T(4,128)}, u32[]{:S(2)}) copy-start(f32[10,4,256]{2,1,0:T(4,128)} %get-tuple-element.37) | copy-start | bytes 122884
  20.9 1.5 %copy-start.5 = (f32[10]{0:T(128)S(1)}, f32[10]{0:T(128)}, u32[]{:S(2)}) copy-start(f32[10]{0:T(128)} %param.12) | copy-start | bytes 124
  27.5 2.4 %copy-start.4 = (f32[10]{0:T(128)S(1)}, f32[10]{0:T(128)}, u32[]{:S(2)}) copy-start(f32[10]{0:T(128)} %get-tuple-element.26) | copy-start | bytes 124
Sparse Core Ops, SparseCore 0:
  29.0 74.0 all-gather.1
